TPU v7x, 32 devices: a whole 2x2x4 slice. The times are simulated.
32 devices in a mesh: ctx: 8 (over z, x), fsdp: 4 (over y, core).
Axes of the slice: x: 2, y: 2, z: 4, core: 2. Of those that a mesh axis runs over, the one named last changes fastest.
Arguments:
- tokens: bfloat16 [3, 4, 1024, 768], P(None, 'fsdp', 'ctx'), may hold values from -6 to 6
- doc_starts: int32 [3, 4, 8], P(None, 'fsdp'), may hold values from 0 to 1023, as said below
- joint_weight: bfloat16 [768, 2304], P('fsdp'), may hold values from -0.21875 to 0.21875
- mixer_weight: bfloat16 [768, 768], P('fsdp'), may hold values from -2.5 to 2.5
- inner_weight: bfloat16 [768, 3072], P('fsdp'), may hold values from -0.21875 to 0.21875
- outer_weight: bfloat16 [3072, 768], P('fsdp'), may hold values from -0.109375 to 0.109375
- query_bias: bfloat16 [768], P('fsdp'), may hold values from -4 to 4
- value_bias: bfloat16 [768], P('fsdp'), may hold values from -0.4375 to 0.4375
- mixer_bias: bfloat16 [768], P('fsdp'), may hold values from -4 to 4
- first_gain: bfloat16 [768], P('fsdp'), may hold values from 0.5 to 1.5
- first_shift: bfloat16 [768], P('fsdp'), may hold values from -4 to 4
- inner_bias: bfloat16 [3072], P('fsdp'), may hold values from -4 to 4
- outer_bias: bfloat16 [768], P('fsdp'), may hold values from -4 to 4
- second_gain: bfloat16 [768], P('fsdp'), may hold values from 0.5 to 1.5
- second_shift: bfloat16 [768], P('fsdp'), may hold values from -4 to 4
- upstream: bfloat16 [3, 4, 1024, 768], P(None, 'fsdp', 'ctx'), may hold values from -6 to 6
Outputs:
- result: bfloat16 [3, 4, 1024, 768], P(None, 'fsdp', 'ctx')
- tokens_gradient: float32 [3, 4, 1024, 768], P(None, 'fsdp', 'ctx')
- joint_gradient: float32 [768, 2304], P('fsdp', 'ctx')
- mixer_gradient: float32 [768, 768], P('fsdp', 'ctx')
- inner_gradient: float32 [768, 3072], P('fsdp', 'ctx')
- outer_gradient: float32 [3072, 768], P('fsdp', 'ctx')
- query_gradient: float32 [768], P(('ctx', 'fsdp'))
- values_gradient: float32 [768], P(('ctx', 'fsdp'))
- mixing_gradient: float32 [768], P(('ctx', 'fsdp'))
- scale_gradient: float32 [768], P(('ctx', 'fsdp'))
- shift_gradient: float32 [768], P(('ctx', 'fsdp'))
- hidden_gradient: float32 [3072], P(('ctx', 'fsdp'))
- return_gradient: float32 [768], P(('ctx', 'fsdp'))
- rescale_gradient: float32 [768], P(('ctx', 'fsdp'))
- reshift_gradient: float32 [768], P(('ctx', 'fsdp'))
Inputs may be any that keep to these rules, and one draw needn't show every extreme that they name: `doc_starts`: each row of 8 starts begins with 0 and rises strictly; documents may begin anywhere in a sequence.
All inputs are finite; a program needn't handle non-finite values.
Results may differ from a plain program's by a relative error of at most 0.017.
Values may be sent and summed in bfloat16 or wider, within the bound.
A program may use at most 320 MiB of HBM per device.

v0:
```python
import math

import jax
import jax.numpy as jnp
from jax import lax
from jax.sharding import PartitionSpec as P

D = 768
H = 12
HD = 64
FF = 3072
MB = 3


SCALE = 0.125
EPSILON = 1e-12
MASKED = -1000000000.0
ROOT_HALF = 0.7071067811865476
GAUSS_PEAK = 0.3989422804014327


def doc_index(positions, starts_row):
    return jnp.sum((starts_row[None, :] <= positions[:, None]).astype(jnp.int32), axis=1) - 1


def norm_forward(hidden, gain, shift):
    average = jnp.mean(hidden, axis=-1, keepdims=True)
    centred = hidden - average
    reciprocal = lax.rsqrt(jnp.mean(centred * centred, axis=-1, keepdims=True) + EPSILON)
    normed = centred * reciprocal
    return (normed * gain + shift, normed, reciprocal)


def norm_backward(incoming, normed, reciprocal, gain):
    scaled = incoming * gain
    return reciprocal * (
        scaled
        - jnp.mean(scaled, axis=-1, keepdims=True)
        - normed * jnp.mean(scaled * normed, axis=-1, keepdims=True)
    )


def gelu_parts(inner):
    cumulative = 0.5 * (1.0 + lax.erf(inner * ROOT_HALF))
    return (inner * cumulative, cumulative + inner * jnp.exp(-0.5 * inner * inner) * GAUSS_PEAK)


def masked_scores(queries, key_block, query_docs, block_docs):
    raw_scores = jnp.einsum("ihd,jhd->hij", queries, key_block, preferred_element_type=jnp.float32)
    allowed = query_docs[:, None] == block_docs[None, :]
    return jnp.where(allowed[None], raw_scores * SCALE, MASKED)


def over_blocks(key_docs, advance, initial):
    length = key_docs.shape[0]
    width = math.gcd(length, 1024)

    def visit(number, running):
        begin = number * width
        return advance(begin, width, running)

    return lax.fori_loop(0, length // width, visit, initial)


def block_slices(key_rows, value_rows, key_docs, begin, width):
    return (
        lax.dynamic_slice_in_dim(key_rows, begin, width, 0),
        lax.dynamic_slice_in_dim(value_rows, begin, width, 0),
        lax.dynamic_slice_in_dim(key_docs, begin, width, 0),
    )


def attend_forward(queries, key_rows, value_rows, query_docs, key_docs):
    shape_rows = (queries.shape[1], queries.shape[0])

    def first_pass(begin, width, running):
        peak, total = running
        key_block, value_block, block_docs = block_slices(
            key_rows, value_rows, key_docs, begin, width
        )
        scores = masked_scores(queries, key_block, query_docs, block_docs)
        new_peak = jnp.maximum(peak, jnp.max(scores, axis=-1))
        return (
            new_peak,
            total * jnp.exp(peak - new_peak)
            + jnp.sum(jnp.exp(scores - new_peak[:, :, None]), axis=-1),
        )

    start_peak = jnp.full(shape_rows, -jnp.inf, jnp.float32)
    peak, total = over_blocks(
        key_docs, first_pass, (start_peak, jnp.zeros(shape_rows, jnp.float32))
    )
    log_total = peak + jnp.log(total)

    def second_pass(begin, width, running):
        key_block, value_block, block_docs = block_slices(
            key_rows, value_rows, key_docs, begin, width
        )
        scores = masked_scores(queries, key_block, query_docs, block_docs)
        probs_low = jnp.exp(scores - log_total[:, :, None]).astype(jnp.bfloat16)
        return running + jnp.einsum(
            "hij,jhd->ihd", probs_low, value_block, preferred_element_type=jnp.float32
        )

    mixed = over_blocks(key_docs, second_pass, jnp.zeros(queries.shape, jnp.float32))
    return (mixed, log_total)


def probs_pressure(queries, flow, key_block, value_block, query_docs, block_docs, log_total):
    scores = masked_scores(queries, key_block, query_docs, block_docs)
    probs = jnp.exp(scores - log_total[:, :, None])
    pressure = jnp.einsum("ihd,jhd->hij", flow, value_block, preferred_element_type=jnp.float32)
    return (probs, pressure)


def key_value_terms(
    queries, flow, key_block, value_block, query_docs, block_docs, log_total, spread
):
    probs, pressure = probs_pressure(
        queries, flow, key_block, value_block, query_docs, block_docs, log_total
    )
    d_scores = (SCALE * probs * (pressure - spread[:, :, None])).astype(jnp.bfloat16)
    value_term = jnp.einsum(
        "hij,ihd->jhd", probs.astype(jnp.bfloat16), flow, preferred_element_type=jnp.float32
    )
    key_term = jnp.einsum("hij,ihd->jhd", d_scores, queries, preferred_element_type=jnp.float32)
    width = key_block.shape[0]
    return jnp.stack([key_term.reshape(width, D), value_term.reshape(width, D)], axis=1)


def on_device(
    tokens,
    doc_starts,
    joint_weight,
    mixer_weight,
    inner_weight,
    outer_weight,
    query_bias,
    value_bias,
    mixer_bias,
    first_gain,
    first_shift,
    inner_bias,
    outer_bias,
    second_gain,
    second_shift,
    upstream,
):
    rows = tokens.shape[2]
    joint_grad = jnp.zeros((D, 3 * D), jnp.float32)
    mixer_grad = jnp.zeros((D, D), jnp.float32)
    inner_grad = jnp.zeros((D, FF), jnp.float32)
    outer_grad = jnp.zeros((FF, D), jnp.float32)
    query_grad = jnp.zeros((D,), jnp.float32)
    values_grad = jnp.zeros((D,), jnp.float32)
    mixing_grad = jnp.zeros((D,), jnp.float32)
    scale_grad = jnp.zeros((D,), jnp.float32)
    shift_grad = jnp.zeros((D,), jnp.float32)
    hidden_grad = jnp.zeros((FF,), jnp.float32)
    return_grad = jnp.zeros((D,), jnp.float32)
    rescale_grad = jnp.zeros((D,), jnp.float32)
    reshift_grad = jnp.zeros((D,), jnp.float32)
    result_rows = []
    input_rows = []
    for batch in range(MB):
        forward_set = (
            lax.all_gather(joint_weight, "fsdp", axis=0, tiled=True),
            lax.all_gather(mixer_weight, "fsdp", axis=0, tiled=True),
            lax.all_gather(inner_weight, "fsdp", axis=0, tiled=True),
            lax.all_gather(outer_weight, "fsdp", axis=0, tiled=True),
            lax.all_gather(query_bias, "fsdp", axis=0, tiled=True),
            lax.all_gather(value_bias, "fsdp", axis=0, tiled=True),
            lax.all_gather(mixer_bias, "fsdp", axis=0, tiled=True),
            lax.all_gather(first_gain, "fsdp", axis=0, tiled=True),
            lax.all_gather(first_shift, "fsdp", axis=0, tiled=True),
            lax.all_gather(inner_bias, "fsdp", axis=0, tiled=True),
            lax.all_gather(outer_bias, "fsdp", axis=0, tiled=True),
            lax.all_gather(second_gain, "fsdp", axis=0, tiled=True),
            lax.all_gather(second_shift, "fsdp", axis=0, tiled=True),
        )
        (
            joint_full,
            mixer_full,
            inner_full,
            outer_full,
            qbias_full,
            vbias_full,
            mbias_full,
            gain_one,
            shift_one,
            ibias_full,
            obias_full,
            gain_two,
            shift_two,
        ) = forward_set
        source = tokens[batch, 0]
        starts_row = doc_starts[batch, 0]
        projected = jnp.dot(source, joint_full, preferred_element_type=jnp.float32)
        queries = (projected[:, 0:D] + qbias_full.astype(jnp.float32)).astype(jnp.bfloat16)
        key_local = projected[:, D : 2 * D].astype(jnp.bfloat16)
        value_local = (projected[:, 2 * D : 3 * D] + vbias_full.astype(jnp.float32)).astype(
            jnp.bfloat16
        )
        key_all, value_all = (
            lax.all_gather(key_local, "ctx", axis=0, tiled=True),
            lax.all_gather(value_local, "ctx", axis=0, tiled=True),
        )
        length = key_all.shape[0]
        key_docs = doc_index(jnp.arange(length, dtype=jnp.int32), starts_row)
        query_docs = lax.dynamic_slice_in_dim(key_docs, lax.axis_index("ctx") * rows, rows, 0)
        query_heads = queries.reshape(rows, H, HD)
        key_heads = key_all.reshape(length, H, HD)
        value_heads = value_all.reshape(length, H, HD)
        mixed, log_total = attend_forward(query_heads, key_heads, value_heads, query_docs, key_docs)
        attended = mixed.reshape(rows, D).astype(jnp.bfloat16)
        branch = jnp.dot(
            attended, mixer_full, preferred_element_type=jnp.float32
        ) + mbias_full.astype(jnp.float32)
        first, first_normed, first_recip = norm_forward(
            source.astype(jnp.float32) + branch,
            gain_one.astype(jnp.float32),
            shift_one.astype(jnp.float32),
        )
        first_low = first.astype(jnp.bfloat16)
        inner_pre = jnp.dot(
            first_low, inner_full, preferred_element_type=jnp.float32
        ) + ibias_full.astype(jnp.float32)
        activated, gelu_slope = gelu_parts(inner_pre)
        activated_low = activated.astype(jnp.bfloat16)
        outer_out = jnp.dot(
            activated_low, outer_full, preferred_element_type=jnp.float32
        ) + obias_full.astype(jnp.float32)
        final, second_normed, second_recip = norm_forward(
            first + outer_out, gain_two.astype(jnp.float32), shift_two.astype(jnp.float32)
        )
        result_rows.append(final.astype(jnp.bfloat16))
        backward_set = (
            lax.all_gather(joint_weight, "fsdp", axis=0, tiled=True),
            lax.all_gather(mixer_weight, "fsdp", axis=0, tiled=True),
            lax.all_gather(inner_weight, "fsdp", axis=0, tiled=True),
            lax.all_gather(outer_weight, "fsdp", axis=0, tiled=True),
            lax.all_gather(query_bias, "fsdp", axis=0, tiled=True),
            lax.all_gather(value_bias, "fsdp", axis=0, tiled=True),
            lax.all_gather(mixer_bias, "fsdp", axis=0, tiled=True),
            lax.all_gather(first_gain, "fsdp", axis=0, tiled=True),
            lax.all_gather(first_shift, "fsdp", axis=0, tiled=True),
            lax.all_gather(inner_bias, "fsdp", axis=0, tiled=True),
            lax.all_gather(outer_bias, "fsdp", axis=0, tiled=True),
            lax.all_gather(second_gain, "fsdp", axis=0, tiled=True),
            lax.all_gather(second_shift, "fsdp", axis=0, tiled=True),
        )
        (
            joint_back,
            mixer_back,
            inner_back,
            outer_back,
            qbias_back,
            vbias_back,
            mbias_back,
            gain_one_back,
            shift_one_back,
            ibias_back,
            obias_back,
            gain_two_back,
            shift_two_back,
        ) = backward_set
        incoming = upstream[batch, 0].astype(jnp.float32)
        rescale_grad = rescale_grad + jnp.sum(incoming * second_normed, axis=0)
        reshift_grad = reshift_grad + jnp.sum(incoming, axis=0)
        d_second = norm_backward(
            incoming, second_normed, second_recip, gain_two_back.astype(jnp.float32)
        )
        d_outer = d_second.astype(jnp.bfloat16)
        return_grad = return_grad + jnp.sum(d_outer.astype(jnp.float32), axis=0)
        outer_grad = outer_grad + jnp.dot(
            activated_low.T, d_outer, preferred_element_type=jnp.float32
        )
        d_inner = (
            jnp.dot(d_outer, outer_back.T, preferred_element_type=jnp.float32) * gelu_slope
        ).astype(jnp.bfloat16)
        hidden_grad = hidden_grad + jnp.sum(d_inner.astype(jnp.float32), axis=0)
        inner_grad = inner_grad + jnp.dot(first_low.T, d_inner, preferred_element_type=jnp.float32)
        d_first = d_second + jnp.dot(d_inner, inner_back.T, preferred_element_type=jnp.float32)
        scale_grad = scale_grad + jnp.sum(d_first * first_normed, axis=0)
        shift_grad = shift_grad + jnp.sum(d_first, axis=0)
        d_residual = norm_backward(
            d_first, first_normed, first_recip, gain_one_back.astype(jnp.float32)
        )
        d_branch = d_residual.astype(jnp.bfloat16)
        mixing_grad = mixing_grad + jnp.sum(d_branch.astype(jnp.float32), axis=0)
        mixer_grad = mixer_grad + jnp.dot(attended.T, d_branch, preferred_element_type=jnp.float32)
        flow_rows = jnp.dot(d_branch, mixer_back.T, preferred_element_type=jnp.float32).astype(
            jnp.bfloat16
        )
        flow = flow_rows.reshape(rows, H, HD)

        def spread_pass(begin, width, running):
            key_block, value_block, block_docs = block_slices(
                key_heads, value_heads, key_docs, begin, width
            )
            probs, pressure = probs_pressure(
                query_heads, flow, key_block, value_block, query_docs, block_docs, log_total
            )
            return running + jnp.sum(probs * pressure, axis=-1)

        spread = over_blocks(key_docs, spread_pass, jnp.zeros(log_total.shape, jnp.float32))

        def query_pass(begin, width, running):
            key_block, value_block, block_docs = block_slices(
                key_heads, value_heads, key_docs, begin, width
            )
            probs, pressure = probs_pressure(
                query_heads, flow, key_block, value_block, query_docs, block_docs, log_total
            )
            d_scores = (SCALE * probs * (pressure - spread[:, :, None])).astype(jnp.bfloat16)
            return running + jnp.einsum(
                "hij,jhd->ihd", d_scores, key_block, preferred_element_type=jnp.float32
            )

        d_queries = (
            over_blocks(key_docs, query_pass, jnp.zeros(query_heads.shape, jnp.float32))
            .reshape(rows, D)
            .astype(jnp.bfloat16)
        )
        every_query, every_flow = (
            lax.all_gather(queries, "ctx", axis=0, tiled=True),
            lax.all_gather(flow_rows, "ctx", axis=0, tiled=True),
        )
        every_total, every_spread = (
            lax.all_gather(log_total.T, "ctx", axis=0, tiled=True),
            lax.all_gather(spread.T, "ctx", axis=0, tiled=True),
        )
        query_all = every_query.reshape(length, H, HD)
        flow_all = every_flow.reshape(length, H, HD)
        key_own = key_local.reshape(rows, H, HD)
        value_own = value_local.reshape(rows, H, HD)

        def key_side(begin, width, running):
            query_block = lax.dynamic_slice_in_dim(query_all, begin, width, 0)
            flow_block = lax.dynamic_slice_in_dim(flow_all, begin, width, 0)
            total_block = lax.dynamic_slice_in_dim(every_total, begin, width, 0).T
            spread_block = lax.dynamic_slice_in_dim(every_spread, begin, width, 0).T
            block_docs = lax.dynamic_slice_in_dim(key_docs, begin, width, 0)
            return running + key_value_terms(
                query_block,
                flow_block,
                key_own,
                value_own,
                block_docs,
                query_docs,
                total_block,
                spread_block,
            )

        key_value = over_blocks(key_docs, key_side, jnp.zeros((rows, 2, D), jnp.float32))
        d_keys = key_value[:, 0].astype(jnp.bfloat16)
        d_values = key_value[:, 1].astype(jnp.bfloat16)
        d_joint = jnp.concatenate([d_queries, d_keys, d_values], axis=1)
        query_grad = query_grad + jnp.sum(d_queries.astype(jnp.float32), axis=0)
        values_grad = values_grad + jnp.sum(d_values.astype(jnp.float32), axis=0)
        joint_grad = joint_grad + jnp.dot(source.T, d_joint, preferred_element_type=jnp.float32)
        input_rows.append(
            d_residual + jnp.dot(d_joint, joint_back.T, preferred_element_type=jnp.float32)
        )
    summed_ctx = (
        lax.psum_scatter(joint_grad, "ctx", scatter_dimension=1, tiled=True),
        lax.psum_scatter(mixer_grad, "ctx", scatter_dimension=1, tiled=True),
        lax.psum_scatter(inner_grad, "ctx", scatter_dimension=1, tiled=True),
        lax.psum_scatter(outer_grad, "ctx", scatter_dimension=1, tiled=True),
        lax.psum_scatter(query_grad, "ctx", scatter_dimension=0, tiled=True),
        lax.psum_scatter(values_grad, "ctx", scatter_dimension=0, tiled=True),
        lax.psum_scatter(mixing_grad, "ctx", scatter_dimension=0, tiled=True),
        lax.psum_scatter(scale_grad, "ctx", scatter_dimension=0, tiled=True),
        lax.psum_scatter(shift_grad, "ctx", scatter_dimension=0, tiled=True),
        lax.psum_scatter(hidden_grad, "ctx", scatter_dimension=0, tiled=True),
        lax.psum_scatter(return_grad, "ctx", scatter_dimension=0, tiled=True),
        lax.psum_scatter(rescale_grad, "ctx", scatter_dimension=0, tiled=True),
        lax.psum_scatter(reshift_grad, "ctx", scatter_dimension=0, tiled=True),
    )
    (
        joint_part,
        mixer_part,
        inner_part,
        outer_part,
        query_part,
        values_part,
        mixing_part,
        scale_part,
        shift_part,
        hidden_part,
        return_part,
        rescale_part,
        reshift_part,
    ) = summed_ctx
    summed_all = (
        lax.psum_scatter(
            joint_part.astype(jnp.bfloat16), "fsdp", scatter_dimension=0, tiled=True
        ).astype(jnp.float32),
        lax.psum_scatter(
            mixer_part.astype(jnp.bfloat16), "fsdp", scatter_dimension=0, tiled=True
        ).astype(jnp.float32),
        lax.psum_scatter(
            inner_part.astype(jnp.bfloat16), "fsdp", scatter_dimension=0, tiled=True
        ).astype(jnp.float32),
        lax.psum_scatter(
            outer_part.astype(jnp.bfloat16), "fsdp", scatter_dimension=0, tiled=True
        ).astype(jnp.float32),
        lax.psum_scatter(
            query_part.astype(jnp.bfloat16), "fsdp", scatter_dimension=0, tiled=True
        ).astype(jnp.float32),
        lax.psum_scatter(
            values_part.astype(jnp.bfloat16), "fsdp", scatter_dimension=0, tiled=True
        ).astype(jnp.float32),
        lax.psum_scatter(
            mixing_part.astype(jnp.bfloat16), "fsdp", scatter_dimension=0, tiled=True
        ).astype(jnp.float32),
        lax.psum_scatter(
            scale_part.astype(jnp.bfloat16), "fsdp", scatter_dimension=0, tiled=True
        ).astype(jnp.float32),
        lax.psum_scatter(
            shift_part.astype(jnp.bfloat16), "fsdp", scatter_dimension=0, tiled=True
        ).astype(jnp.float32),
        lax.psum_scatter(
            hidden_part.astype(jnp.bfloat16), "fsdp", scatter_dimension=0, tiled=True
        ).astype(jnp.float32),
        lax.psum_scatter(
            return_part.astype(jnp.bfloat16), "fsdp", scatter_dimension=0, tiled=True
        ).astype(jnp.float32),
        lax.psum_scatter(
            rescale_part.astype(jnp.bfloat16), "fsdp", scatter_dimension=0, tiled=True
        ).astype(jnp.float32),
        lax.psum_scatter(
            reshift_part.astype(jnp.bfloat16), "fsdp", scatter_dimension=0, tiled=True
        ).astype(jnp.float32),
    )
    result = jnp.stack(result_rows, axis=0)[:, None]
    tokens_gradient = jnp.stack(input_rows, axis=0)[:, None]
    (
        joint_out,
        mixer_out,
        inner_out,
        outer_out_grad,
        query_out,
        values_out,
        mixing_out,
        scale_out,
        shift_out,
        hidden_out,
        return_out,
        rescale_out,
        reshift_out,
    ) = summed_all
    return (
        result,
        tokens_gradient,
        joint_out,
        mixer_out,
        inner_out,
        outer_out_grad,
        query_out,
        values_out,
        mixing_out,
        scale_out,
        shift_out,
        hidden_out,
        return_out,
        rescale_out,
        reshift_out,
    )


def solution(mesh):
    in_specs = (
        P(None, "fsdp", "ctx", None),
        P(None, "fsdp", None),
        P("fsdp", None),
        P("fsdp", None),
        P("fsdp", None),
        P("fsdp", None),
        P("fsdp"),
        P("fsdp"),
        P("fsdp"),
        P("fsdp"),
        P("fsdp"),
        P("fsdp"),
        P("fsdp"),
        P("fsdp"),
        P("fsdp"),
        P(None, "fsdp", "ctx", None),
    )
    out_specs = (
        P(None, "fsdp", "ctx", None),
        P(None, "fsdp", "ctx", None),
        P("fsdp", "ctx"),
        P("fsdp", "ctx"),
        P("fsdp", "ctx"),
        P("fsdp", "ctx"),
        P(("ctx", "fsdp")),
        P(("ctx", "fsdp")),
        P(("ctx", "fsdp")),
        P(("ctx", "fsdp")),
        P(("ctx", "fsdp")),
        P(("ctx", "fsdp")),
        P(("ctx", "fsdp")),
        P(("ctx", "fsdp")),
        P(("ctx", "fsdp")),
    )
    return jax.shard_map(
        on_device, mesh=mesh, in_specs=in_specs, out_specs=out_specs, check_vma=False
    )
```

profile of v0, /device:TPU:0, one launch (start us, length us, event | category | flops | bytes accessed | tf_op | source)
XLA Modules:
  0.0 1412.6 jit_solution(9092130529474369704)
XLA Ops:
  8.0 35.1 %all-gather.18.cloned.1.call-done = bf16[768,2304]{1,0:T(8,128)(2,1)} async-done(((bf16[192,2304]{1,0:T(8,128)(2,1)}), bf16[768,2304]{1,0:T(8,128)(2,1)}) %all-gather.18.cloned.1.call-update) | async-done | bytes 3538960 | tf_op jit(solution)/shard_map/all_gather | solution.py:167
  43.1 2.9 fusion.141
  56.4 12.3 all-reduce.28
  83.4 5.2 all-gather
  97.6 40.1 %all-gather.20.cloned.1.call-done = bf16[1024,768]{1,0:T(8,128)(2,1)} async-done(((bf16[128,768]{1,0:T(8,128)(2,1)}), bf16[1024,768]{1,0:T(8,128)(2,1)}) %all-gather.20.cloned.1.call-update) | async-done | bytes 1572880 | tf_op jit(solution)/shard_map/all_gather | solution.py:206
  139.4 5.0 fusion.84
  144.5 10.9 all-gather.24.cloned.1.call-done
  157.9 43.8 %all-gather.36.cloned.1.call-done = bf16[1024,768]{1,0:T(8,128)(2,1)} async-done(((bf16[128,768]{1,0:T(8,128)(2,1)}), bf16[1024,768]{1,0:T(8,128)(2,1)}) %all-gather.36.cloned.1.call-update) | async-done | bytes 1572880 | tf_op jit(solution)/shard_map/all_gather | solution.py:205
  203.4 2.4 fusion.2
  208.4 38.3 %all-gather.32.cloned.1.call-done = bf16[1024,768]{1,0:T(8,128)(2,1)} async-done(((bf16[128,768]{1,0:T(8,128)(2,1)}), bf16[1024,768]{1,0:T(8,128)(2,1)}) %all-gather.32.cloned.1.call-update) | async-done | bytes 1572880 | tf_op jit(solution)/shard_map/all_gather | solution.py:205
  252.5 39.4 %all-gather.30.cloned.1.call-done = bf16[1024,768]{1,0:T(8,128)(2,1)} async-done(((bf16[128,768]{1,0:T(8,128)(2,1)}), bf16[1024,768]{1,0:T(8,128)(2,1)}) %all-gather.30.cloned.1.call-update) | async-done | bytes 1572880 | tf_op jit(solution)/shard_map/all_gather | solution.py:206
  291.9 2.6 copy.124
  294.5 5.0 fusion.87
  300.2 37.5 %all-gather.34.cloned.1.call-done = bf16[1024,768]{1,0:T(8,128)(2,1)} async-done(((bf16[128,768]{1,0:T(8,128)(2,1)}), bf16[1024,768]{1,0:T(8,128)(2,1)}) %all-gather.34.cloned.1.call-update) | async-done | bytes 1572880 | tf_op jit(solution)/shard_map/all_gather | solution.py:206
  337.7 2.8 copy.127
  340.5 4.9 fusion.90
  347.2 28.4 %all-gather.26.cloned.1.call-done = bf16[768,3072]{1,0:T(8,128)(2,1)} async-done(((bf16[192,3072]{1,0:T(8,128)(2,1)}), bf16[768,3072]{1,0:T(8,128)(2,1)}) %all-gather.26.cloned.1.call-update) | async-done | bytes 4718608 | tf_op jit(solution)/shard_map/all_gather | solution.py:169
  375.6 4.4 convolution_add_fusion
  380.0 34.5 %all-gather.28.cloned.1.call-done = bf16[3072,768]{1,0:T(8,128)(2,1)} async-done(((bf16[768,768]{1,0:T(8,128)(2,1)}), bf16[3072,768]{1,0:T(8,128)(2,1)}) %all-gather.28.cloned.1.call-update) | async-done | bytes 4718608 | tf_op jit(solution)/shard_map/all_gather | solution.py:170
  414.5 3.9 fusion.221
  432.5 2.7 convert_reduce_fusion.2
  439.4 2.5 convert_reduce_fusion.10
  465.1 2.9 fusion.177
  470.0 7.2 multiply_reduce_fusion
  477.2 4.7 multiply_reduce_fusion.2
  482.0 4.7 multiply_reduce_fusion.1
  488.7 3.7 fusion.227
  492.4 14.1 %all-gather.38.cloned.1.call-done = bf16[1024,768]{1,0:T(8,128)(2,1)} async-done(((bf16[128,768]{1,0:T(8,128)(2,1)}), bf16[1024,768]{1,0:T(8,128)(2,1)}) %all-gather.38.cloned.1.call-update) | async-done | bytes 1572880 | tf_op jit(solution)/shard_map/all_gather | solution.py:326
  508.3 3.8 fusion.225
  512.1 39.7 %all-gather.42.cloned.1.call-done = bf16[1024,768]{1,0:T(8,128)(2,1)} async-done(((bf16[128,768]{1,0:T(8,128)(2,1)}), bf16[1024,768]{1,0:T(8,128)(2,1)}) %all-gather.42.cloned.1.call-update) | async-done | bytes 1572880 | tf_op jit(solution)/shard_map/all_gather | solution.py:326
  554.7 3.8 fusion.226
  561.1 32.7 %all_gather.165 = f32[1024,12]{0,1:T(8,128)} all-gather(f32[128,12]{0,1:T(8,128)} %fusion.150), channel_id=1, replica_groups=mesh['ctx'=8,'fsdp'=4] {'ctx'}, dimensions={0}, use_global_device_ids=true | all-gather | bytes 55296 | tf_op jit(solution)/shard_map/all_gather | solution.py:330
  593.9 32.7 %all_gather.157 = f32[1024,12]{0,1:T(8,128)} all-gather(f32[128,12]{0,1:T(8,128)} %fusion.158), channel_id=1, replica_groups=mesh['ctx'=8,'fsdp'=4] {'ctx'}, dimensions={0}, use_global_device_ids=true | all-gather | bytes 55296 | tf_op jit(solution)/shard_map/all_gather | solution.py:330
  626.6 32.2 %all_gather.161 = f32[1024,12]{0,1:T(8,128)} all-gather(f32[128,12]{0,1:T(8,128)S(1)} %fusion.154), channel_id=1, replica_groups=mesh['ctx'=8,'fsdp'=4] {'ctx'}, dimensions={0}, use_global_device_ids=true | all-gather | bytes 55296 | tf_op jit(solution)/shard_map/all_gather | solution.py:330
  658.8 32.3 %all_gather.167 = f32[1024,12]{0,1:T(8,128)} all-gather(f32[128,12]{0,1:T(8,128)} %bitcast.387), channel_id=1, replica_groups=mesh['ctx'=8,'fsdp'=4] {'ctx'}, dimensions={0}, use_global_device_ids=true | all-gather | bytes 55296 | tf_op jit(solution)/shard_map/all_gather | solution.py:331
  691.1 32.7 %all_gather.163 = f32[1024,12]{0,1:T(8,128)} all-gather(f32[128,12]{0,1:T(8,128)} %bitcast.385), channel_id=1, replica_groups=mesh['ctx'=8,'fsdp'=4] {'ctx'}, dimensions={0}, use_global_device_ids=true | all-gather | bytes 55296 | tf_op jit(solution)/shard_map/all_gather | solution.py:331
  723.8 32.9 %all_gather.159 = f32[1024,12]{0,1:T(8,128)} all-gather(f32[128,12]{0,1:T(8,128)} %bitcast.386), channel_id=1, replica_groups=mesh['ctx'=8,'fsdp'=4] {'ctx'}, dimensions={0}, use_global_device_ids=true | all-gather | bytes 55296 | tf_op jit(solution)/shard_map/all_gather | solution.py:331
  756.8 8.0 convert_reduce_fusion.15
  764.9 6.5 convert_reduce_fusion.17
  771.5 3.0 convert_reduce_fusion.16
  774.9 2.9 copy.133
  777.8 7.7 fusion.73
  785.5 2.7 copy.143
  788.2 2.6 copy.138
  790.9 6.4 convert_reduce_fusion.14
  797.3 5.1 fusion.130
  802.4 2.8 convert_reduce_fusion.13
  805.3 8.0 fusion.71
  813.3 5.0 fusion.129
  818.3 6.1 convert_reduce_fusion.12
  824.4 7.9 fusion.69
  832.3 9.2 add_bitcast_fusion
  845.8 5.1 add_add_fusion.1
  855.3 4.6 add_add_fusion
  866.2 108.3 %reduce-scatter.13.cloned.1.call-done = f32[768,288]{0,1:T(8,128)} async-done(((f32[768,2304]{0,1:T(8,128)}), f32[768,288]{0,1:T(8,128)}) %reduce-scatter.13.cloned.1.call-update) | async-done | bytes 884752 | tf_op jit(solution)/shard_map/reduce_scatter | solution.py:366
  977.1 37.9 %all-reduce.26 = (bf16[768]{0:T(1024)(128)(2,1)S(1)}, bf16[768]{0:T(1024)(128)(2,1)S(1)}, bf16[768]{0:T(1024)(128)(2,1)S(1)}, bf16[768]{0:T(1024)(128)(2,1)S(1)}...) all-reduce(f32[768]{0:T(1024)S(1)} %add.702, ...), channel_id=10, replica_groups=mesh['ctx'=8,'fsdp'=4] {'ctx'}, use_global_device_ids=true, to_apply=%region_47.48.clone | all-reduce | flops 9216 | bytes 55296
  1015.7 6.7 all-reduce.27
  1023.0 119.0 %reduce-scatter.17.cloned.1.call-done = f32[768,384]{1,0:T(8,128)} async-done(((f32[768,3072]{1,0:T(8,128)}), f32[768,384]{1,0:T(8,128)}) %reduce-scatter.17.cloned.1.call-update) | async-done | bytes 1179664 | tf_op jit(solution)/shard_map/reduce_scatter | solution.py:368
  1154.9 153.4 %reduce-scatter.21.cloned.1.call-done = f32[3072,96]{0,1:T(8,128)} async-done(((f32[3072,768]{0,1:T(8,128)}), f32[3072,96]{0,1:T(8,128)}) %reduce-scatter.21.cloned.1.call-update) | async-done | bytes 1179664 | tf_op jit(solution)/shard_map/reduce_scatter | solution.py:369
  1311.1 2.6 fusion.63
  1317.5 12.3 reduce-scatter.27.cloned.1.call-done
  1331.4 23.1 %reduce-scatter.25.cloned.1.call-done = bf16[192,288]{1,0:T(8,128)(2,1)} async-done(((bf16[768,288]{1,0:T(8,128)(2,1)}), bf16[192,288]{1,0:T(8,128)(2,1)}) %reduce-scatter.25.cloned.1.call-update) | async-done | bytes 110608
  1356.4 22.9 %reduce-scatter.19.cloned.1.call-done = bf16[192,384]{1,0:T(8,128)(2,1)} async-done(((bf16[768,384]{1,0:T(8,128)(2,1)}), bf16[192,384]{1,0:T(8,128)(2,1)}) %reduce-scatter.19.cloned.1.call-update) | async-done | bytes 147472 | tf_op jit(solution)/shard_map/reduce_scatter | solution.py:402
  1380.9 23.0 %reduce-scatter.23.cloned.1.call-done = bf16[768,96]{0,1:T(8,128)(2,1)} async-done(((bf16[3072,96]{0,1:T(8,128)(2,1)}), bf16[768,96]{0,1:T(8,128)(2,1)}) %reduce-scatter.23.cloned.1.call-update) | async-done | bytes 147472 | tf_op jit(solution)/shard_map/reduce_scatter | solution.py:405
  (621 shorter events, 144.4 us)
Async XLA Ops:
  7.2 40.6 %copy-start.171 = (u32[32]{0:T(128)S(1)}, u32[32]{0:T(128)}, u32[]{:S(2)}) copy-start(u32[32]{0:T(128)} %constant.253) | copy-start | bytes 388
  7.2 41.9 %copy-start.174 = (bf16[192]{0:T(256)(128)(2,1)S(1)}, bf16[192]{0:T(256)(128)(2,1)}, u32[]{:S(2)}) copy-start(bf16[192]{0:T(256)(128)(2,1)} %param.23) | copy-start | bytes 1156
  7.2 42.1 %copy-start.175 = (bf16[192]{0:T(256)(128)(2,1)S(1)}, bf16[192]{0:T(256)(128)(2,1)}, u32[]{:S(2)}) copy-start(bf16[192]{0:T(256)(128)(2,1)} %param.22) | copy-start | bytes 1156
  7.2 42.3 %copy-start.176 = (bf16[192]{0:T(256)(128)(2,1)S(1)}, bf16[192]{0:T(256)(128)(2,1)}, u32[]{:S(2)}) copy-start(bf16[192]{0:T(256)(128)(2,1)} %param.24) | copy-start | bytes 1156
  7.2 35.9 %all-gather.18.cloned.1.call-start = ((), (), s32[]{:S(2)}) async-start(), calls=%async_computation.8 | async-start | bytes 4423680 | tf_op jit(solution)/shard_map/all_gather | solution.py:167
  8.0 83.9 %all-gather.22.cloned.1.call-start = ((), (), s32[]{:S(2)}) async-start(), calls=%async_computation.10 | async-start | bytes 1769472 | tf_op jit(solution)/shard_map/all_gather | solution.py:205
  43.1 26.9 %copy-start.1 = (bf16[768,2304]{1,0:T(8,128)(2,1)S(1)}, bf16[768,2304]{1,0:T(8,128)(2,1)}, u32[]{:S(2)}) copy-start(bf16[768,2304]{1,0:T(8,128)(2,1)} %all-gather.18.cloned.1.call-done) | copy-start | bytes 10616836
  47.7 89.9 %all-gather.20.cloned.1.call-start = ((), (), s32[]{:S(2)}) async-start(), calls=%async_computation.9 | async-start | bytes 1769472 | tf_op jit(solution)/shard_map/all_gather | solution.py:206
  75.0 80.4 %all-gather.24.cloned.1.call-start = ((), (), s32[]{:S(2)}) async-start(), calls=%async_computation.11 | async-start | bytes 1474560 | tf_op jit(solution)/shard_map/all_gather | solution.py:168
  75.6 126.1 %all-gather.36.cloned.1.call-start = ((), (), s32[]{:S(2)}) async-start(), calls=%async_computation.17 | async-start | bytes 1769472 | tf_op jit(solution)/shard_map/all_gather | solution.py:205
  77.4 169.4 %all-gather.32.cloned.1.call-start = ((), (), s32[]{:S(2)}) async-start(), calls=%async_computation.15 | async-start | bytes 1769472 | tf_op jit(solution)/shard_map/all_gather | solution.py:205
  79.1 212.8 %all-gather.30.cloned.1.call-start = ((), (), s32[]{:S(2)}) async-start(), calls=%async_computation.14 | async-start | bytes 1769472 | tf_op jit(solution)/shard_map/all_gather | solution.py:206
  79.9 257.8 %all-gather.34.cloned.1.call-start = ((), (), s32[]{:S(2)}) async-start(), calls=%async_computation.16 | async-start | bytes 1769472 | tf_op jit(solution)/shard_map/all_gather | solution.py:206
  80.6 294.9 %all-gather.26.cloned.1.call-start = ((), (), s32[]{:S(2)}) async-start(), calls=%async_computation.12 | async-start | bytes 5898240 | tf_op jit(solution)/shard_map/all_gather | solution.py:169
  81.4 333.1 %all-gather.28.cloned.1.call-start = ((), (), s32[]{:S(2)}) async-start(), calls=%async_computation.13 | async-start | bytes 5898240 | tf_op jit(solution)/shard_map/all_gather | solution.py:170
  82.0 404.8 %all-gather.46.cloned.1.call-start = ((), (), s32[]{:S(2)}) async-start(), calls=%async_computation.22 | async-start | bytes 1769472 | tf_op jit(solution)/shard_map/all_gather | solution.py:326
  82.7 423.8 %all-gather.38.cloned.1.call-start = ((), (), s32[]{:S(2)}) async-start(), calls=%async_computation.18 | async-start | bytes 1769472 | tf_op jit(solution)/shard_map/all_gather | solution.py:326
  83.3 468.5 %all-gather.42.cloned.1.call-start = ((), (), s32[]{:S(2)}) async-start(), calls=%async_computation.20 | async-start | bytes 1769472 | tf_op jit(solution)/shard_map/all_gather | solution.py:326
  89.1 337.5 %copy-start.102 = (f32[768]{0:T(1024)}, f32[768]{0:T(1024)S(1)}, u32[]{:S(2)}) copy-start(f32[768]{0:T(1024)S(1)} %convert_element_type.491) | copy-start | bytes 9220
  89.2 50.2 %copy-start.60 = (pred[128,1024]{1,0:T(8,128)(4,1)}, pred[128,1024]{1,0:T(8,128)(4,1)S(1)}, u32[]{:S(2)}) copy-start(pred[128,1024]{1,0:T(8,128)(4,1)S(1)} %broadcast_compare_fusion.5) | copy-start | bytes 393220
  89.4 251.1 %copy-start.62 = (pred[128,1024]{1,0:T(8,128)(4,1)}, pred[128,1024]{1,0:T(8,128)(4,1)S(1)}, u32[]{:S(2)}) copy-start(pred[128,1024]{1,0:T(8,128)(4,1)S(1)} %broadcast_compare_fusion.3) | copy-start | bytes 393220
  89.6 392.4 %copy-start.58 = (pred[128,1024]{1,0:T(8,128)(4,1)}, pred[128,1024]{1,0:T(8,128)(4,1)S(1)}, u32[]{:S(2)}) copy-start(pred[128,1024]{1,0:T(8,128)(4,1)S(1)} %broadcast_compare_fusion.4) | copy-start | bytes 393220
  90.8 684.1 %all-gather.40.cloned.1.call-start = ((), (), s32[]{:S(2)}) async-start(), calls=%async_computation.19 | async-start | bytes 1769472 | tf_op jit(solution)/shard_map/all_gather | solution.py:327
  97.6 46.9 %copy-start.101 = (f32[12,128]{1,0:T(8,128)}, f32[12,128]{1,0:T(8,128)S(1)}, u32[]{:S(2)}) copy-start(f32[12,128]{1,0:T(8,128)S(1)} %exponential_reduce_fusion.2) | copy-start | bytes 18436
  97.6 46.9 %copy-start.107 = (f32[12,128]{1,0:T(8,128)}, f32[12,128]{1,0:T(8,128)S(1)}, u32[]{:S(2)}) copy-start(f32[12,128]{1,0:T(8,128)S(1)} %log_add_fusion.2) | copy-start | bytes 18436
  144.5 61.3 %copy-start.87 = (bf16[12,64,128]{2,1,0:T(8,128)(2,1)}, bf16[12,64,128]{2,1,0:T(8,128)(2,1)S(1)}, u32[]{:S(2)}) copy-start(bf16[12,64,128]{2,1,0:T(8,128)(2,1)S(1)} %fusion.84) | copy-start | bytes 589828
  157.2 284.9 %copy-start.117 = (f32[128]{0:T(128)}, f32[128]{0:T(128)S(1)}, u32[]{:S(2)}) copy-start(f32[128]{0:T(128)S(1)} %broadcast_multiply_fusion.17) | copy-start | bytes 1540
  208.4 132.1 %copy-start.113 = (f32[12,128]{1,0:T(8,128)}, f32[12,128]{1,0:T(8,128)S(1)}, u32[]{:S(2)}) copy-start(f32[12,128]{1,0:T(8,128)S(1)} %log_add_fusion) | copy-start | bytes 18436
  252.5 47.0 %copy-start.100 = (f32[12,128]{1,0:T(8,128)}, f32[12,128]{1,0:T(8,128)S(1)}, u32[]{:S(2)}) copy-start(f32[12,128]{1,0:T(8,128)S(1)} %exponential_reduce_fusion.1) | copy-start | bytes 18436
  252.5 47.0 %copy-start.110 = (f32[12,128]{1,0:T(8,128)}, f32[12,128]{1,0:T(8,128)S(1)}, u32[]{:S(2)}) copy-start(f32[12,128]{1,0:T(8,128)S(1)} %log_add_fusion.1) | copy-start | bytes 18436
  299.5 45.9 %copy-start.88 = (bf16[12,64,128]{2,1,0:T(8,128)(2,1)}, bf16[12,64,128]{2,1,0:T(8,128)(2,1)S(1)}, u32[]{:S(2)}) copy-start(bf16[12,64,128]{2,1,0:T(8,128)(2,1)S(1)} %fusion.87) | copy-start | bytes 589828
  300.0 139.4 %copy-start.119 = (f32[128]{0:T(128)}, f32[128]{0:T(128)S(1)}, u32[]{:S(2)}) copy-start(f32[128]{0:T(128)S(1)} %broadcast_multiply_fusion.15) | copy-start | bytes 1540
  300.2 118.5 %copy-start.125 = (f32[128]{0:T(128)}, f32[128]{0:T(128)S(1)}, u32[]{:S(2)}) copy-start(f32[128]{0:T(128)S(1)} %add_rsqrt_fusion.3) | copy-start | bytes 1540
  345.5 34.5 %copy-start.93 = (bf16[12,64,128]{2,1,0:T(8,128)(2,1)}, bf16[12,64,128]{2,1,0:T(8,128)(2,1)S(1)}, u32[]{:S(2)}) copy-start(bf16[12,64,128]{2,1,0:T(8,128)(2,1)S(1)} %fusion.90) | copy-start | bytes 589828
  347.0 95.0 %copy-start.123 = (f32[128]{0:T(128)}, f32[128]{0:T(128)S(1)}, u32[]{:S(2)}) copy-start(f32[128]{0:T(128)S(1)} %broadcast_multiply_fusion.13) | copy-start | bytes 1540
  347.2 67.3 %copy-start.143 = (f32[128]{0:T(128)}, f32[128]{0:T(128)S(1)}, u32[]{:S(2)}) copy-start(f32[128]{0:T(128)S(1)} %add_rsqrt_fusion.1) | copy-start | bytes 1540
  441.9 26.1 %copy-start.19 = (f32[128,768]{1,0:T(8,128)}, f32[128,768]{1,0:T(8,128)S(1)}, u32[]{:S(2)}) copy-start(f32[128,768]{1,0:T(8,128)S(1)} %get-tuple-element.566) | copy-start | bytes 1179652
  444.9 340.6 %all-gather.48.cloned.1.call-start = ((), (), s32[]{:S(2)}) async-start(), calls=%async_computation.23 | async-start | bytes 1769472 | tf_op jit(solution)/shard_map/all_gather | solution.py:327
  459.4 328.9 %all-gather.44.cloned.1.call-start = ((), (), s32[]{:S(2)}) async-start(), calls=%async_computation.21 | async-start | bytes 1769472 | tf_op jit(solution)/shard_map/all_gather | solution.py:327
  486.7 377.5 %reduce-scatter.15.cloned.1.call-start = ((), (), s32[]{:S(2)}) async-start(), calls=%async_computation.25 | async-start | bytes 2654208 | tf_op jit(solution)/shard_map/reduce_scatter | solution.py:367
  512.1 42.6 %copy-start.90 = (bf16[128,768]{0,1:T(8,128)(2,1)S(1)}, bf16[128,768]{0,1:T(8,128)(2,1)}, u32[]{:S(2)}) copy-start(bf16[128,768]{0,1:T(8,128)(2,1)} %copy.137) | copy-start | bytes 589828
  558.4 206.4 %slice-start.2 = ((s8[6291456]{0:T(1024)(128)(4,1)}), s8[2097152]{0:T(1024)(128)(4,1)S(1)}, s32[]{:S(2)}) async-start(s8[6291456]{0:T(1024)(128)(4,1)} %bitcast.303), calls=%async_computation.34 | async-start | bytes 4194304
  774.5 38.8 %copy-start.77 = (bf16[12,64,128]{2,1,0:T(8,128)(2,1)}, bf16[12,64,128]{2,1,0:T(8,128)(2,1)S(1)}, u32[]{:S(2)}) copy-start(bf16[12,64,128]{2,1,0:T(8,128)(2,1)S(1)} %get-tuple-element.645) | copy-start | bytes 589828
  774.5 200.0 %reduce-scatter.13.cloned.1.call-start = ((), (), s32[]{:S(2)}) async-start(), calls=%async_computation.24 | async-start | bytes 7962624 | tf_op jit(solution)/shard_map/reduce_scatter | solution.py:366
  841.6 300.4 %reduce-scatter.17.cloned.1.call-start = ((), (), s32[]{:S(2)}) async-start(), calls=%async_computation.26 | async-start | bytes 10616832 | tf_op jit(solution)/shard_map/reduce_scatter | solution.py:368
  850.9 457.3 %reduce-scatter.21.cloned.1.call-start = ((), (), s32[]{:S(2)}) async-start(), calls=%async_computation.28 | async-start | bytes 10616832 | tf_op jit(solution)/shard_map/reduce_scatter | solution.py:369
  860.0 116.8 %copy-start.136 = (f32[768]{0:T(1024)S(1)}, f32[768]{0:T(1024)}, u32[]{:S(2)}) copy-start(f32[768]{0:T(1024)} %get-tuple-element.548) | copy-start | bytes 9220
  860.0 116.8 %copy-start.137 = (f32[768]{0:T(1024)S(1)}, f32[768]{0:T(1024)}, u32[]{:S(2)}) copy-start(f32[768]{0:T(1024)} %get-tuple-element.588) | copy-start | bytes 9220
  860.1 116.8 %copy-start.138 = (f32[768]{0:T(1024)S(1)}, f32[768]{0:T(1024)}, u32[]{:S(2)}) copy-start(f32[768]{0:T(1024)} %get-tuple-element.590) | copy-start | bytes 9220
  860.1 116.9 %copy-start.133 = (f32[768]{0:T(1024)S(1)}, f32[768]{0:T(1024)}, u32[]{:S(2)}) copy-start(f32[768]{0:T(1024)} %get-tuple-element.447) | copy-start | bytes 9220
  860.1 116.9 %copy-start.134 = (f32[768]{0:T(1024)S(1)}, f32[768]{0:T(1024)}, u32[]{:S(2)}) copy-start(f32[768]{0:T(1024)} %get-tuple-element.465) | copy-start | bytes 9220
  860.1 116.9 %copy-start.135 = (f32[768]{0:T(1024)S(1)}, f32[768]{0:T(1024)}, u32[]{:S(2)}) copy-start(f32[768]{0:T(1024)} %get-tuple-element.467) | copy-start | bytes 9220
  860.1 116.9 %copy-start.146 = (f32[3072]{0:T(1024)S(1)}, f32[3072]{0:T(1024)}, u32[]{:S(2)}) copy-start(f32[3072]{0:T(1024)} %get-tuple-element.656) | copy-start | bytes 36868
  860.1 116.9 %copy-start.147 = (f32[3072]{0:T(1024)S(1)}, f32[3072]{0:T(1024)}, u32[]{:S(2)}) copy-start(f32[3072]{0:T(1024)} %get-tuple-element.654) | copy-start | bytes 36868
  860.1 116.9 %copy-start.148 = (f32[3072]{0:T(1024)S(1)}, f32[3072]{0:T(1024)}, u32[]{:S(2)}) copy-start(f32[3072]{0:T(1024)} %get-tuple-element.652) | copy-start | bytes 36868
  860.1 116.9 %copy-start.150 = (f32[12,64]{1,0:T(8,128)S(1)}, f32[12,64]{1,0:T(8,128)}, u32[]{:S(2)}) copy-start(f32[12,64]{1,0:T(8,128)} %get-tuple-element.648) | copy-start | bytes 9220
  860.1 116.9 %copy-start.152 = (f32[12,64]{1,0:T(8,128)S(1)}, f32[12,64]{1,0:T(8,128)}, u32[]{:S(2)}) copy-start(f32[12,64]{1,0:T(8,128)} %get-tuple-element.650) | copy-start | bytes 9220
  860.1 116.9 %copy-start.153 = (f32[12,64]{1,0:T(8,128)S(1)}, f32[12,64]{1,0:T(8,128)}, u32[]{:S(2)}) copy-start(f32[12,64]{1,0:T(8,128)} %get-tuple-element.646) | copy-start | bytes 9220
  860.2 469.6 %reduce-scatter.27.cloned.1.call-start = ((), (), s32[]{:S(2)}) async-start(), calls=%async_computation.31 | async-start | bytes 245760
  865.2 287.2 %copy-start.103 = (f32[768]{0:T(1024)S(1)}, f32[768]{0:T(1024)}, u32[]{:S(2)}) copy-start(f32[768]{0:T(1024)} %copy-done.102) | copy-start | bytes 9220
  866.1 488.4 %reduce-scatter.25.cloned.1.call-start = ((), (), s32[]{:S(2)}) async-start(), calls=%async_computation.30 | async-start | bytes 737280
  976.8 402.5 %reduce-scatter.19.cloned.1.call-start = ((), (), s32[]{:S(2)}) async-start(), calls=%async_computation.27 | async-start | bytes 737280 | tf_op jit(solution)/shard_map/reduce_scatter | solution.py:402
  1144.2 166.9 %copy-start.2 = (bf16[768,2304]{1,0:T(8,128)(2,1)S(1)}, bf16[768,2304]{1,0:T(8,128)(2,1)}, u32[]{:S(2)}) copy-start(bf16[768,2304]{1,0:T(8,128)(2,1)} %all-gather.18.cloned.1.call-done) | copy-start | bytes 10616836
  1144.2 259.7 %reduce-scatter.23.cloned.1.call-start = ((), (), s32[]{:S(2)}) async-start(), calls=%async_computation.29 | async-start | bytes 737280 | tf_op jit(solution)/shard_map/reduce_scatter | solution.py:405
  (151 other events, 836.4 us)
Sparse Core Ops, SparseCore 0:
  9.6 33.4 all-gather.17
  47.9 43.9 all-gather.21
  94.7 42.9 all-gather.19
  139.1 16.2 all-gather.23
  157.4 44.1 all-gather.35
  203.7 42.9 all-gather.31
  248.9 42.9 all-gather.29
  294.7 42.9 all-gather.33
  339.3 36.2 all-gather.25
  377.0 37.4 all-gather.27
  417.3 44.1 all-gather.45
  463.5 42.9 all-gather.37
  508.7 42.9 all-gather.41
  553.8 43.3 all-gather.39
  599.8 43.6 all-gather.47
  645.5 43.6 all-gather.43
  774.6 68.2 reduce-scatter.14
  846.4 128.0 reduce-scatter.12
  978.5 163.4 reduce-scatter.16
  1145.9 162.3 reduce-scatter.20
  1310.9 18.8 reduce-scatter.26
  1332.4 22.0 reduce-scatter.24
  1357.2 22.0 reduce-scatter.18
  1381.8 22.0 reduce-scatter.22
where the time goes:
time: 1420 us; the launch traced here: 1410 us
  waiting for transfers between devices  830 us (58%)
  blocking collectives  258 us (18%)
  matrix products  192 us (14%)
  local copies, waits for them, and re-layouts  68.2 us (5%)
  other arithmetic  42.1 us (3%)
  between operations  20.6 us (1%)
    reduce_scatter x1, waiting for transfers between devices, on_device(): lax.psum_scatter(outer_grad, 'ctx', scatter_dimension=1, tiled=True)  153 us
    reduce_scatter x1, waiting for transfers between devices, on_device(): lax.psum_scatter(inner_grad, 'ctx', scatter_dimension=1, tiled=True)  119 us
    all_gather x3, waiting for transfers between devices, on_device(): lax.all_gather(value_local, 'ctx', axis=0, tiled=True)  117 us
    reduce_scatter x1, waiting for transfers between devices, on_device(): lax.psum_scatter(joint_grad, 'ctx', scatter_dimension=1, tiled=True)  108 us
    all_gather x3, blocking collectives, on_device(): lax.all_gather(spread.T, 'ctx', axis=0, tiled=True)  97.9 us
    all_gather x3, blocking collectives, on_device(): lax.all_gather(log_total.T, 'ctx', axis=0, tiled=True)  97.7 us
    all_gather x3, waiting for transfers between devices, on_device(): lax.all_gather(key_local, 'ctx', axis=0, tiled=True)  83 us
    unnamed x3, blocking collectives  56.8 us
  transfers between devices with their start and end apart: 24, of which 19 were waited for; matrix products, arithmetic and copies ran while one was open for 20% of the time, Pallas kernels for 0%

commit v1 on v0

v1 whole, which is shorter than its diff:
```python
import functools
import math

import jax
import jax.numpy as jnp
from jax import lax
from jax.experimental import pallas as pl
from jax.experimental.pallas import tpu as pltpu
from jax.sharding import PartitionSpec as P

D = 768
H = 12
HD = 64
FF = 3072
MB = 3

SCALE = 0.125
EPSILON = 1e-12
MASKED = -1000000000.0
ROOT_HALF = 0.7071067811865476
GAUSS_PEAK = 0.3989422804014327

F32 = jnp.float32
BF16 = jnp.bfloat16


def doc_index(positions, starts_row):
    return jnp.sum((starts_row[None, :] <= positions[:, None]).astype(jnp.int32), axis=1) - 1


def norm_forward(hidden, gain, shift):
    average = jnp.mean(hidden, axis=-1, keepdims=True)
    centred = hidden - average
    reciprocal = lax.rsqrt(jnp.mean(centred * centred, axis=-1, keepdims=True) + EPSILON)
    normed = centred * reciprocal
    return (normed * gain + shift, normed, reciprocal)


def norm_backward(incoming, normed, reciprocal, gain):
    scaled = incoming * gain
    return reciprocal * (
        scaled
        - jnp.mean(scaled, axis=-1, keepdims=True)
        - normed * jnp.mean(scaled * normed, axis=-1, keepdims=True)
    )


def gelu_parts(inner):
    cumulative = 0.5 * (1.0 + lax.erf(inner * ROOT_HALF))
    return (inner * cumulative, cumulative + inner * jnp.exp(-0.5 * inner * inner) * GAUSS_PEAK)


def exchange_kernel(count, x_ref, y_ref, held, send_sem, recv_sem, own_sem):
    me = lax.axis_index("ctx")
    barrier = pltpu.get_barrier_semaphore()

    def greet(step, carry):
        peer = lax.rem(me + step, count)
        pl.semaphore_signal(barrier, inc=1, device_id={"ctx": peer})
        return carry

    lax.fori_loop(1, count, greet, 0)
    own_in = pltpu.make_async_copy(x_ref.at[me], held, own_sem)
    own_in.start()
    pl.semaphore_wait(barrier, count - 1)

    def transfer(step):
        peer = lax.rem(me + step, count)
        return pltpu.make_async_remote_copy(
            src_ref=x_ref.at[peer],
            dst_ref=y_ref.at[me],
            send_sem=send_sem.at[step],
            recv_sem=recv_sem.at[step],
            device_id={"ctx": peer},
        )

    def begin(step, carry):
        transfer(step).start()
        return carry

    lax.fori_loop(1, count, begin, 0)
    own_in.wait()
    own_out = pltpu.make_async_copy(held, y_ref.at[me], own_sem)
    own_out.start()
    own_out.wait()

    def finish(step, carry):
        transfer(step).wait()
        return carry

    lax.fori_loop(1, count, finish, 0)


def exchange(x, number):
    count = x.shape[0]
    return pl.pallas_call(
        functools.partial(exchange_kernel, count),
        out_shape=jax.ShapeDtypeStruct(x.shape, x.dtype),
        in_specs=[pl.BlockSpec(memory_space=pl.ANY)],
        out_specs=pl.BlockSpec(memory_space=pl.ANY),
        scratch_shapes=[
            pltpu.VMEM(x.shape[1:], x.dtype),
            pltpu.SemaphoreType.DMA((count,)),
            pltpu.SemaphoreType.DMA((count,)),
            pltpu.SemaphoreType.DMA,
        ],
        compiler_params=pltpu.CompilerParams(collective_id=number, has_side_effects=True),
        name=f"exchange_{number}",
    )(x)


def across(ref, first, rows, width, lanes):
    parts = [ref[first + i, 0, rows, :] for i in range(width // lanes)]
    return parts[0] if len(parts) == 1 else jnp.concatenate(parts, axis=1)


def key_documents(starts_ref, unit, length, lanes, key_docs):
    position = lax.broadcasted_iota(jnp.int32, (length, lanes), 0)
    docs = jnp.zeros((length, lanes), jnp.int32) - 1
    for j in range(starts_ref.shape[1]):
        docs = docs + jnp.where(position >= starts_ref[unit, j], 1, 0)
    key_docs[...] = docs


def same_document(key_docs, first, width, query_docs):
    keys = key_docs[pl.ds(first, width), :]
    lanes = keys.shape[1]
    parts = [keys == query_docs[:, i : i + lanes] for i in range(0, query_docs.shape[1], lanes)]
    return parts[0] if len(parts) == 1 else jnp.concatenate(parts, axis=1)


def over_chunks(chunks, body, carry):
    if chunks == 1:
        return body(0, carry)
    return lax.fori_loop(0, chunks, body, carry)


def attend_kernel(
    width, starts_ref, x_ref, docs_ref, o_ref, wide_ref, lse_ref, key_rows, value_t, key_docs
):
    count, _, _, lanes = x_ref.shape
    length = count * lanes
    depth = min(length, 1024)
    unit = pl.program_id(0)
    for i in range(count):
        rows = slice(i * lanes, (i + 1) * lanes)
        key_rows[rows, :] = x_ref[i, 0, HD : 2 * HD, :].T
        value_t[:, rows] = x_ref[i, 0, 2 * HD : 3 * HD, :]
    key_documents(starts_ref, unit, length, lanes, key_docs)
    group = width // lanes

    def block(number, carry):
        begin = pl.multiple_of(number * width, width)
        queries = across(x_ref, number * group, slice(0, HD), width, lanes) * SCALE
        query_docs = docs_ref[0, :, pl.ds(begin, width)]

        def chunk(index, running):
            peak, total, mixed = running
            first = pl.multiple_of(index * depth, depth)
            scores = jnp.dot(
                key_rows[pl.ds(first, depth), :], queries, preferred_element_type=F32
            )
            same = same_document(key_docs, first, depth, query_docs)
            scores = jnp.where(same, scores, MASKED)
            new_peak = jnp.maximum(peak, jnp.max(scores, axis=0, keepdims=True))
            scaling = jnp.exp(peak - new_peak)
            weights = jnp.exp(scores - new_peak)
            return (
                new_peak,
                total * scaling + jnp.sum(weights, axis=0, keepdims=True),
                mixed * scaling
                + jnp.dot(
                    value_t[:, pl.ds(first, depth)],
                    weights.astype(BF16),
                    preferred_element_type=F32,
                ),
            )

        peak, total, mixed = over_chunks(
            length // depth,
            chunk,
            (
                jnp.full((1, width), -jnp.inf, F32),
                jnp.zeros((1, width), F32),
                jnp.zeros((HD, width), F32),
            ),
        )
        mixed = mixed / total
        wide_ref[0, :, pl.ds(begin, width)] = mixed
        lse_ref[0, :, pl.ds(begin, width)] = peak + jnp.log(total)
        low = mixed.astype(BF16)
        for i in range(group):
            o_ref[number * group + i, 0] = low[:, i * lanes : (i + 1) * lanes]
        return carry

    lax.fori_loop(0, length // width, block, 0)


def attend_back_kernel(
    width,
    starts_ref,
    x_ref,
    flow_ref,
    docs_ref,
    wide_ref,
    lse_ref,
    d_ref,
    key_rows,
    value_rows,
    key_t,
    key_docs,
    d_key,
    d_value,
):
    count, _, _, lanes = x_ref.shape
    length = count * lanes
    depth = min(length, 1024)
    unit = pl.program_id(0)
    for i in range(count):
        rows = slice(i * lanes, (i + 1) * lanes)
        key_rows[rows, :] = x_ref[i, 0, HD : 2 * HD, :].T
        value_rows[rows, :] = x_ref[i, 0, 2 * HD : 3 * HD, :].T
        key_t[:, rows] = x_ref[i, 0, HD : 2 * HD, :]
    key_documents(starts_ref, unit, length, lanes, key_docs)
    d_key[...] = jnp.zeros_like(d_key)
    d_value[...] = jnp.zeros_like(d_value)
    group = width // lanes

    def block(number, carry):
        begin = pl.multiple_of(number * width, width)
        queries = across(x_ref, number * group, slice(0, HD), width, lanes) * SCALE
        flow = across(flow_ref, number * group, slice(0, HD), width, lanes)
        query_rows = queries.T
        flow_rows = flow.T
        query_docs = docs_ref[0, :, pl.ds(begin, width)]
        log_total = lse_ref[0, :, pl.ds(begin, width)]
        spread = jnp.sum(
            flow.astype(F32) * wide_ref[0, :, pl.ds(begin, width)], axis=0, keepdims=True
        )

        def chunk(index, d_query):
            first = pl.multiple_of(index * depth, depth)
            rows = pl.ds(first, depth)
            scores = jnp.dot(key_rows[rows, :], queries, preferred_element_type=F32)
            same = same_document(key_docs, first, depth, query_docs)
            probs = jnp.exp(jnp.where(same, scores, MASKED) - log_total)
            pressure = jnp.dot(value_rows[rows, :], flow, preferred_element_type=F32)
            d_scores = (probs * (pressure - spread)).astype(BF16)
            d_value[rows, :] += jnp.dot(
                probs.astype(BF16), flow_rows, preferred_element_type=F32
            )
            d_key[rows, :] += jnp.dot(d_scores, query_rows, preferred_element_type=F32)
            return d_query + jnp.dot(key_t[:, rows], d_scores, preferred_element_type=F32)

        d_query = over_chunks(length // depth, chunk, jnp.zeros((HD, width), F32))
        low = (d_query * SCALE).astype(BF16)
        for i in range(group):
            d_ref[number * group + i, 0, 0:HD, :] = low[:, i * lanes : (i + 1) * lanes]
        return carry

    lax.fori_loop(0, length // width, block, 0)
    for i in range(count):
        rows = slice(i * lanes, (i + 1) * lanes)
        d_ref[i, 0, HD : 2 * HD, :] = d_key[rows, :].T.astype(BF16)
        d_ref[i, 0, 2 * HD : 3 * HD, :] = d_value[rows, :].T.astype(BF16)


def unit_block(*dims):
    return pl.BlockSpec(dims, lambda u, starts: (0, u) + (0,) * (len(dims) - 2))


def own_block(*dims):
    return pl.BlockSpec(dims, lambda u, starts: (u,) + (0,) * (len(dims) - 1))


def attend(x, starts, docs):
    count, units, _, lanes = x.shape
    length = count * lanes
    width = 2 * lanes if count % 2 == 0 else lanes
    return pl.pallas_call(
        functools.partial(attend_kernel, width),
        out_shape=(
            jax.ShapeDtypeStruct((count, units, HD, lanes), BF16),
            jax.ShapeDtypeStruct((units, HD, length), F32),
            jax.ShapeDtypeStruct((units, 1, length), F32),
        ),
        grid_spec=pltpu.PrefetchScalarGridSpec(
            num_scalar_prefetch=1,
            grid=(units,),
            in_specs=[unit_block(count, 1, 3 * HD, lanes), own_block(1, 1, length)],
            out_specs=[
                unit_block(count, 1, HD, lanes),
                own_block(1, HD, length),
                own_block(1, 1, length),
            ],
            scratch_shapes=[
                pltpu.VMEM((length, HD), BF16),
                pltpu.VMEM((HD, length), BF16),
                pltpu.VMEM((length, lanes), jnp.int32),
            ],
        ),
        compiler_params=pltpu.CompilerParams(dimension_semantics=("arbitrary",)),
        name="attend",
    )(starts, x, docs)


def attend_back(x, flow, starts, docs, wide, lse):
    count, units, _, lanes = x.shape
    length = count * lanes
    width = 2 * lanes if count % 2 == 0 else lanes
    return pl.pallas_call(
        functools.partial(attend_back_kernel, width),
        out_shape=jax.ShapeDtypeStruct(x.shape, BF16),
        grid_spec=pltpu.PrefetchScalarGridSpec(
            num_scalar_prefetch=1,
            grid=(units,),
            in_specs=[
                unit_block(count, 1, 3 * HD, lanes),
                unit_block(count, 1, HD, lanes),
                own_block(1, 1, length),
                own_block(1, HD, length),
                own_block(1, 1, length),
            ],
            out_specs=unit_block(count, 1, 3 * HD, lanes),
            scratch_shapes=[
                pltpu.VMEM((length, HD), BF16),
                pltpu.VMEM((length, HD), BF16),
                pltpu.VMEM((HD, length), BF16),
                pltpu.VMEM((length, lanes), jnp.int32),
                pltpu.VMEM((length, HD), F32),
                pltpu.VMEM((length, HD), F32),
            ],
        ),
        compiler_params=pltpu.CompilerParams(dimension_semantics=("arbitrary",)),
        name="attend_back",
    )(starts, x, flow, docs, wide, lse)


def to_units(columns, parts, count, units):
    rows = columns.shape[1] // MB
    x = columns.reshape(parts, H, HD, MB, rows).transpose(3, 1, 0, 2, 4)
    x = x.reshape(MB * H, parts * HD, rows)
    x = jnp.pad(x, ((0, units * count - MB * H), (0, 0), (0, 0)))
    return x.reshape(units, count, parts * HD, rows).transpose(1, 0, 2, 3)


def from_units(x, parts):
    count, units, _, rows = x.shape
    x = x.transpose(1, 0, 2, 3).reshape(units * count, parts * HD, rows)[: MB * H]
    x = x.reshape(MB, H, parts, HD, rows).transpose(2, 1, 3, 0, 4)
    return x.reshape(parts * D, MB * rows)


def mul_nn(a, b):
    return jnp.dot(a, b, preferred_element_type=F32)


def mul_tn(a, b):
    return lax.dot_general(a, b, (((0,), (0,)), ((), ())), preferred_element_type=F32)


def mul_nt(a, b):
    return lax.dot_general(a, b, (((1,), (1,)), ((), ())), preferred_element_type=F32)


def mul_tt(a, b):
    return lax.dot_general(a, b, (((0,), (1,)), ((), ())), preferred_element_type=F32)


def on_device(
    count,
    shards,
    tokens,
    doc_starts,
    joint_weight,
    mixer_weight,
    inner_weight,
    outer_weight,
    query_bias,
    value_bias,
    mixer_bias,
    first_gain,
    first_shift,
    inner_bias,
    outer_bias,
    second_gain,
    second_shift,
    upstream,
):
    rows = tokens.shape[2]
    length = rows * count
    units = -(-MB * H // count)
    me = lax.axis_index("ctx")

    joint = lax.all_gather(joint_weight, "fsdp", axis=0, tiled=True)
    vectors = jnp.concatenate(
        [
            query_bias,
            value_bias,
            mixer_bias,
            first_gain,
            first_shift,
            outer_bias,
            second_gain,
            second_shift,
            inner_bias,
        ]
    )
    vectors = lax.all_gather(vectors, "fsdp", axis=0)
    part = D // shards
    names = [vectors[:, i * part : (i + 1) * part].reshape(D).astype(F32) for i in range(8)]
    qbias, vbias, mbias, gain_one, shift_one, obias, gain_two, shift_two = names
    ibias = vectors[:, 8 * part :].reshape(FF).astype(F32)
    mixer = lax.all_gather(mixer_weight, "fsdp", axis=0, tiled=True)
    inner = lax.all_gather(inner_weight, "fsdp", axis=0, tiled=True)
    outer = lax.all_gather(outer_weight, "fsdp", axis=0, tiled=True)

    source = tokens.reshape(MB * rows, D)
    unit_ids = jnp.arange(units, dtype=jnp.int32) * count + me
    unit_starts = doc_starts[:, 0][jnp.minimum(unit_ids // H, MB - 1)]
    positions = jnp.arange(length, dtype=jnp.int32)
    unit_docs = jax.vmap(lambda s: doc_index(positions, s))(unit_starts)[:, None, :]

    joint_bias = jnp.concatenate([qbias, jnp.zeros((D,), F32), vbias])
    projected = (mul_tt(joint, source) + joint_bias[:, None]).astype(BF16)
    received = exchange(to_units(projected, 3, count, units), 0)
    mixed, wide, lse = attend(received, unit_starts, unit_docs)
    attended = from_units(exchange(mixed, 1), 1)

    branch = mul_tn(attended, mixer) + mbias
    first, first_normed, first_recip = norm_forward(
        source.astype(F32) + branch, gain_one, shift_one
    )
    first_low = first.astype(BF16)
    inner_pre = mul_nn(first_low, inner) + ibias
    activated, gelu_slope = gelu_parts(inner_pre)
    activated_low = activated.astype(BF16)
    outer_out = mul_nn(activated_low, outer) + obias
    final, second_normed, second_recip = norm_forward(first + outer_out, gain_two, shift_two)
    result = final.astype(BF16).reshape(MB, 1, rows, D)

    incoming = upstream.reshape(MB * rows, D).astype(F32)
    rescale_grad = jnp.sum(incoming * second_normed, axis=0)
    reshift_grad = jnp.sum(incoming, axis=0)
    d_second = norm_backward(incoming, second_normed, second_recip, gain_two)
    d_outer = d_second.astype(BF16)
    return_grad = jnp.sum(d_outer.astype(F32), axis=0)
    outer_grad = mul_tn(activated_low, d_outer)
    d_inner = (mul_nt(d_outer, outer) * gelu_slope).astype(BF16)
    hidden_grad = jnp.sum(d_inner.astype(F32), axis=0)
    inner_grad = mul_tn(first_low, d_inner)
    d_first = d_second + mul_nt(d_inner, inner)
    scale_grad = jnp.sum(d_first * first_normed, axis=0)
    shift_grad = jnp.sum(d_first, axis=0)
    d_residual = norm_backward(d_first, first_normed, first_recip, gain_one)
    d_branch = d_residual.astype(BF16)
    mixing_grad = jnp.sum(d_branch.astype(F32), axis=0)
    mixer_grad = mul_nn(attended, d_branch)
    flow = mul_nt(mixer, d_branch).astype(BF16)
    flow_units = exchange(to_units(flow, 1, count, units), 2)
    d_units = attend_back(received, flow_units, unit_starts, unit_docs, wide, lse)
    d_joint = from_units(exchange(d_units, 3), 3)
    bias_sums = jnp.sum(d_joint.astype(F32), axis=1)
    query_grad = bias_sums[0:D]
    values_grad = bias_sums[2 * D :]
    joint_grad = lax.dot_general(
        source, d_joint, (((0,), (1,)), ((), ())), preferred_element_type=F32
    )
    tokens_grad = d_residual + mul_tt(d_joint, joint)
    tokens_grad = tokens_grad.reshape(MB, 1, rows, D)

    def reduced(grad):
        over_rows = lax.psum_scatter(
            grad.astype(BF16), "fsdp", scatter_dimension=0, tiled=True
        )
        return lax.psum_scatter(over_rows, "ctx", scatter_dimension=1, tiled=True).astype(F32)

    outer_out_grad = reduced(outer_grad)
    inner_out = reduced(inner_grad)
    mixer_out = reduced(mixer_grad)
    joint_out = reduced(joint_grad)

    world = count * shards
    small = [
        query_grad,
        values_grad,
        mixing_grad,
        scale_grad,
        shift_grad,
        hidden_grad,
        return_grad,
        rescale_grad,
        reshift_grad,
    ]
    packed = jnp.concatenate([v.reshape(world, -1) for v in small], axis=1)
    packed = lax.psum(packed, ("ctx", "fsdp"))
    index = me * shards + lax.axis_index("fsdp")
    own = lax.dynamic_slice_in_dim(packed, index, 1, 0)[0]
    sums = []
    begin = 0
    for v in small:
        size = v.shape[0] // world
        sums.append(own[begin : begin + size])
        begin += size
    return (result, tokens_grad, joint_out, mixer_out, inner_out, outer_out_grad, *sums)


def solution(mesh):
    in_specs = (
        P(None, "fsdp", "ctx", None),
        P(None, "fsdp", None),
        P("fsdp", None),
        P("fsdp", None),
        P("fsdp", None),
        P("fsdp", None),
        P("fsdp"),
        P("fsdp"),
        P("fsdp"),
        P("fsdp"),
        P("fsdp"),
        P("fsdp"),
        P("fsdp"),
        P("fsdp"),
        P("fsdp"),
        P(None, "fsdp", "ctx", None),
    )
    out_specs = (
        P(None, "fsdp", "ctx", None),
        P(None, "fsdp", "ctx", None),
        P("fsdp", "ctx"),
        P("fsdp", "ctx"),
        P("fsdp", "ctx"),
        P("fsdp", "ctx"),
        P(("ctx", "fsdp")),
        P(("ctx", "fsdp")),
        P(("ctx", "fsdp")),
        P(("ctx", "fsdp")),
        P(("ctx", "fsdp")),
        P(("ctx", "fsdp")),
        P(("ctx", "fsdp")),
        P(("ctx", "fsdp")),
        P(("ctx", "fsdp")),
    )
    return jax.shard_map(
        functools.partial(on_device, mesh.shape["ctx"], mesh.shape["fsdp"]),
        mesh=mesh,
        in_specs=in_specs,
        out_specs=out_specs,
        check_vma=False,
    )
```

time: 1420 us -> 696 us (0.49)
  waiting for transfers between devices: 830 us -> 363 us
  blocking collectives: 258 us -> 46.4 us
  Pallas kernels: 0 us -> 164 us
  matrix products: 192 us -> 51.2 us
  other arithmetic: 42.1 us -> 9.91 us
  local copies, waits for them, and re-layouts: 68.2 us -> 41.8 us
    all_gather x16 -> x4, waiting for transfers between devices: 363 us -> 24.2 us  [the longest x1 24.1 us: on_device(): joint = lax.all_gather(joint_weight, 'fsdp', axis=0, tiled=True)]
    reduce_scatter x6 -> x4, waiting for transfers between devices: 427 us -> 161 us  [the longest x3 96.1 us: reduced(): lax.psum_scatter(grad.astype(BF16), 'fsdp', scatter_dimension=0, tiled=True)]
    all_gather x7 -> x1, blocking collectives: 201 us -> 6.2 us  [on_device(): vectors = lax.all_gather(vectors, 'fsdp', axis=0)]
    pallas_call x0 -> x6, Pallas kernels: none -> 164 us  [the longest x4 116 us: exchange(): pl.pallas_call(functools.partial(exchange_kernel, count), out_shape=jax.S...]
    dot_general x57 -> x12, matrix products: 192 us -> 51.2 us  [the longest x3 16 us: mul_tn(): lax.dot_general(a, b, (((0,), (0,)), ((), ())), preferred_element_type=F32)]
    unnamed x26 -> x16, waiting for transfers between devices: 40.6 us -> 178 us
    unnamed x3 -> x0, blocking collectives: 56.8 us -> none
    psum x0 -> x1, blocking collectives: none -> 40.2 us  [on_device(): packed = lax.psum(packed, ('ctx', 'fsdp'))]
  transfers between devices with their start and end apart: 24 -> 12, of which waited for: 19 -> 8; matrix products, arithmetic and copies ran while one was open for 20% -> 12% of each run, Pallas kernels for 0% -> 24%
where the time goes in v1:
time: 696 us; the launch traced here: 692 us
  waiting for transfers between devices  363 us (52%)
  Pallas kernels  164 us (24%)
  matrix products  51.2 us (7%)
  blocking collectives  46.4 us (7%)
  local copies, waits for them, and re-layouts  41.8 us (6%)
  between operations  15.1 us (2%)
  other arithmetic  9.91 us (1%)
    unnamed x16, waiting for transfers between devices  178 us
    pallas_call x4, Pallas kernels, exchange(): pl.pallas_call(functools.partial(exchange_kernel, count), out_shape=jax.S...  116 us
    reduce_scatter x3, waiting for transfers between devices, reduced(): lax.psum_scatter(grad.astype(BF16), 'fsdp', scatter_dimension=0, tiled=True)  96.1 us
    reduce_scatter x1, waiting for transfers between devices, reduced(): lax.psum_scatter(over_rows, 'ctx', scatter_dimension=1, tiled=True)  64.7 us
    psum x1, blocking collectives, on_device(): packed = lax.psum(packed, ('ctx', 'fsdp'))  40.2 us
    pallas_call x1, Pallas kernels, attend_back(): pl.pallas_call(functools.partial(attend_back_kernel, width), out_shape=ja...  25.1 us
    all_gather x1, waiting for transfers between devices, on_device(): joint = lax.all_gather(joint_weight, 'fsdp', axis=0, tiled=True)  24.1 us
    unnamed x59, local copies, waits for them, and re-layouts  23.9 us
  transfers between devices with their start and end apart: 12, of which 8 were waited for; matrix products, arithmetic and copies ran while one was open for 12% of the time, Pallas kernels for 24%

profile of v1, /device:TPU:0, one launch (start us, length us, event | category | flops | bytes accessed | tf_op | source)
XLA Modules:
  0.0 691.9 jit_solution(13503172947176099718)
XLA Ops:
  7.2 0.7 all-gather.7.cloned.1.call-update
  8.0 0.7 all-gather.9.cloned.1.call-update
  8.8 0.7 all-gather.11.cloned.1.call-update
  9.6 0.5 all-gather.13.cloned.1.call-update
  10.3 6.2 all-gather.1
  16.8 0.6 gather_fusion
  17.5 0.6 sub.50.docs_ref
  19.0 24.1 %all-gather.7.cloned.1.call-done = bf16[768,2304]{1,0:T(8,128)(2,1)} async-done(((bf16[192,2304]{1,0:T(8,128)(2,1)}), bf16[768,2304]{1,0:T(8,128)(2,1)}) %all-gather.7.cloned.1.call-update) | async-done | bytes 3538960 | tf_op jit(solution)/shard_map/all_gather | solution.py:395
  43.1 5.5 fusion.7
  48.6 5.1 reshape.292
  53.7 0.5 copy.61
  54.5 1.4 copy.109
  55.9 36.7 %exchange_0.1.x_ref = bf16[8,5,192,128]{3,2,1,0:T(8,128)(2,1)} custom-call(bf16[8,5,192,128]{3,2,1,0:T(8,128)(2,1)} %bitcast.119), custom_call_target="tpu_custom_call" | custom-call | tf_op jit(solution)/shard_map/exchange_0/pallas_call | solution.py:96
  92.5 22.8 %attend.1 = (bf16[8,5,64,128]{3,2,1,0:T(8,128)(2,1)}, f32[5,64,1024]{2,1,0:T(8,128)}, f32[5,1,1024]{2,1,0:T(1,128)}) custom-call(s32[5,8]{1,0:T(8,128)} %copy-done.5, bf16[8,5,192,128]{3,2,1,0:T(8,128)(2,1)} %exchange_0.1.x_ref, s32[5,1,1024]{2,1,0:T(1,128)} %sub.50.docs_ref), custom_call_target="tpu_custom_call" | custom-call | tf_op jit(solution)/shard_map/attend/pallas_call | solution.py:280
  115.3 25.5 %exchange_1.1 = bf16[8,5,64,128]{3,2,1,0:T(8,128)(2,1)} custom-call(bf16[8,5,64,128]{3,2,1,0:T(8,128)(2,1)} %get-tuple-element.18.x_ref), custom_call_target="tpu_custom_call" | custom-call | tf_op jit(solution)/shard_map/exchange_1/pallas_call | solution.py:96
  140.8 1.1 copy.63
  142.0 0.5 copy.64
  142.6 2.2 fusion.40
  145.0 6.9 %multiply_convert_fusion = (bf16[384,3072]{1,0:T(8,128)(2,1)}, f32[384,3072]{1,0:T(8,128)}) fusion(f32[3072]{0:T(1024)S(1)} %reshape.318, bf16[768,3072]{1,0:T(8,128)(2,1)} %all-gather.11.cloned.1.call-done, f32[384,768]{1,0:T(8,128)S(1)} %get-tuple-element.113, f32[768]{0:T(1024)S(1)} %reshape.317, f32[768]{0:T(1024)S(1)} %reshape.316, ...), kind=kOutput, calls=%fused_computation.13 | convolution fusion | flops 1820491776 | bytes 12997632 | tf_op jit(solution)/shard_map/dot_general | solution.py:355
  152.0 5.3 fusion.41
  157.6 0.6 fusion.25
  158.2 1.3 convert_reduce_fusion.3
  159.5 0.6 copy-done.16
  160.1 3.6 convert_reduce_fusion
  163.8 2.4 multiply_reduce_fusion
  166.2 0.4 convert_reduce_fusion.4
  166.6 1.8 convolution_convert_fusion.3
  168.5 1.2 copy-done.3
  169.7 0.7 fusion.18
  170.4 0.3 copy.65
  171.1 0.9 copy.110
  172.0 17.5 %exchange_2.1.flow_ref = bf16[8,5,64,128]{3,2,1,0:T(8,128)(2,1)} custom-call(bf16[8,5,64,128]{3,2,1,0:T(8,128)(2,1)} %bitcast.128), custom_call_target="tpu_custom_call" | custom-call | tf_op jit(solution)/shard_map/exchange_2/pallas_call | solution.py:96
  189.5 25.1 %attend_back.1.x_ref = bf16[8,5,192,128]{3,2,1,0:T(8,128)(2,1)} custom-call(s32[5,8]{1,0:T(8,128)} %copy-done.5, bf16[8,5,192,128]{3,2,1,0:T(8,128)(2,1)} %exchange_0.1.x_ref, bf16[8,5,64,128]{3,2,1,0:T(8,128)(2,1)} %exchange_2.1.flow_ref, s32[5,1,1024]{2,1,0:T(1,128)} %sub.50.docs_ref, f32[5,64,1024]{2,1,0:T(8,128)} %get-tuple-element.19.wide_ref, ...), custom_call_target="tpu_custom_call" | custom-call | tf_op jit(solution)/shard_map/attend_back/pallas_call | solution.py:311
  214.6 36.7 %exchange_3.1 = bf16[8,5,192,128]{3,2,1,0:T(8,128)(2,1)} custom-call(bf16[8,5,192,128]{3,2,1,0:T(8,128)(2,1)} %attend_back.1.x_ref), custom_call_target="tpu_custom_call" | custom-call | tf_op jit(solution)/shard_map/exchange_3/pallas_call | solution.py:96
  251.3 1.7 copy.68
  253.1 1.7 copy.69
  254.8 1.4 copy-done.2
  256.2 3.8 fusion.6
  260.0 5.8 copy.74
  266.1 7.0 %convolution_convert_fusion.1 = bf16[768,3072]{1,0:T(8,128)(2,1)} fusion(bf16[384,3072]{1,0:T(8,128)(2,1)} %copy-done.19, f32[384,768]{1,0:T(8,128)} %copy-done.1, f32[768]{0:T(1024)S(1)} %reshape.317, f32[768]{0:T(1024)S(1)} %reshape.316, f32[384]{0:T(512)S(1)} %add_rsqrt_fusion.1, f32[384]{0:T(512)S(1)} %broadcast_multiply_fusion.4), kind=kOutput, calls=%fused_computation.3 | convolution fusion | flops 1815773184 | bytes 8266752 | tf_op jit(solution)/shard_map/dot_general | solution.py:359
  273.1 6.8 convolution_convert_fusion
  280.0 1.9 copy.76
  282.0 34.9 %reduce-scatter.25.cloned.1.call-done = bf16[192,2304]{1,0:T(8,128)(2,1)} async-done(((bf16[768,2304]{1,0:T(8,128)(2,1)}), bf16[192,2304]{1,0:T(8,128)(2,1)}) %reduce-scatter.25.cloned.1.call-update) | async-done | bytes 884752
  316.9 2.3 copy.75
  319.3 48.0 %reduce-scatter.21.cloned.1.call-done = bf16[192,3072]{1,0:T(8,128)(2,1)} async-done(((bf16[768,3072]{1,0:T(8,128)(2,1)}), bf16[192,3072]{1,0:T(8,128)(2,1)}) %reduce-scatter.21.cloned.1.call-update) | async-done | bytes 1179664 | tf_op jit(solution)/shard_map/reduce_scatter | solution.py:473
  367.3 2.5 copy.78
  369.9 48.0 %reduce-scatter.23.cloned.1.call-done = bf16[768,768]{1,0:T(8,128)(2,1)} async-done(((bf16[3072,768]{1,0:T(8,128)(2,1)}), bf16[768,768]{1,0:T(8,128)(2,1)}) %reduce-scatter.23.cloned.1.call-update) | async-done | bytes 1179664 | tf_op jit(solution)/shard_map/reduce_scatter | solution.py:473
  417.9 2.4 copy.80
  420.4 5.1 convert_reduce_fusion.1
  426.3 40.2 %psum.7 = f32[32,288]{1,0:T(8,128)S(1)} all-reduce(f32[32,288]{1,0:T(8,128)S(1)} %concatenate.11), channel_id=1, replica_groups=mesh['ctx'=8,'fsdp'=4] {'ctx','fsdp'}, use_global_device_ids=true, to_apply=%region_25.26 | all-reduce | flops 9216 | bytes 73728 | tf_op jit(solution)/shard_map/psum | solution.py:496
  466.5 0.6 dynamic-slice_bitcast_fusion.3
  467.1 0.6 dynamic-slice_bitcast_fusion
  467.7 5.3 fusion.12
  473.0 9.6 %reduce-scatter.27.cloned.1.call-done = bf16[96,192]{1,0:T(8,128)(2,1)} async-done(((bf16[768,192]{1,0:T(8,128)(2,1)}), bf16[96,192]{1,0:T(8,128)(2,1)}) %reduce-scatter.27.cloned.1.call-update) | async-done | bytes 36880
  482.6 0.9 copy.77
  483.5 0.7 convert_element_type.205
  484.2 64.7 %reduce-scatter.17.cloned.1.call-done = bf16[192,288]{0,1:T(8,128)(2,1)} async-done(((bf16[192,2304]{0,1:T(8,128)(2,1)}), bf16[192,288]{0,1:T(8,128)(2,1)}) %reduce-scatter.17.cloned.1.call-update) | async-done | bytes 110608 | tf_op jit(solution)/shard_map/reduce_scatter | solution.py:476
  549.0 1.7 copy.72
  550.7 65.6 %reduce-scatter.29.cloned.1.call-done = bf16[384,192]{1,0:T(8,128)(2,1)} async-done(((bf16[3072,192]{1,0:T(8,128)(2,1)}), bf16[384,192]{1,0:T(8,128)(2,1)}) %reduce-scatter.29.cloned.1.call-update) | async-done | bytes 147472
  616.3 1.1 copy.79
  617.3 0.7 convert_element_type.207
  618.1 64.8 %reduce-scatter.31.cloned.1.call-done = bf16[96,768]{1,0:T(8,128)(2,1)} async-done(((bf16[768,768]{1,0:T(8,128)(2,1)}), bf16[96,768]{1,0:T(8,128)(2,1)}) %reduce-scatter.31.cloned.1.call-update) | async-done | bytes 147472
  682.8 1.1 copy.81
  683.9 0.9 copy.73
  (116 shorter events, 4.4 us)
Async XLA Ops:
  7.2 35.9 %all-gather.7.cloned.1.call-start = ((), (), s32[]{:S(2)}) async-start(), calls=%async_computation.8 | async-start | bytes 4423680 | tf_op jit(solution)/shard_map/all_gather | solution.py:395
  7.9 134.6 %all-gather.9.cloned.1.call-start = ((), (), s32[]{:S(2)}) async-start(), calls=%async_computation.9 | async-start | bytes 1474560 | tf_op jit(solution)/shard_map/all_gather | solution.py:414
  8.7 1.5 copy-start.6
  8.7 1.5 copy-start.8
  8.7 1.5 copy-start.9
  8.7 1.5 copy-start.10
  8.7 1.5 copy-start.11
  8.7 1.5 copy-start.12
  8.7 1.5 copy-start.13
  8.7 1.5 copy-start.14
  8.7 1.5 copy-start.15
  8.8 8.0 %copy-start.7 = (s32[3,1,8]{2,1,0:T(1,128)S(1)}, s32[3,1,8]{2,1,0:T(1,128)}, u32[]{:S(2)}) copy-start(s32[3,1,8]{2,1,0:T(1,128)} %param.17) | copy-start | bytes 292
  8.8 9.9 %copy-start = (bf16[3,1,128,768]{3,2,1,0:T(8,128)(2,1)S(1)}, bf16[3,1,128,768]{3,2,1,0:T(8,128)(2,1)}, u32[]{:S(2)}) copy-start(bf16[3,1,128,768]{3,2,1,0:T(8,128)(2,1)} %param.31) | copy-start | bytes 1769476
  8.8 136.3 %all-gather.11.cloned.1.call-start = ((), (), s32[]{:S(2)}) async-start(), calls=%async_computation.10 | async-start | bytes 5898240 | tf_op jit(solution)/shard_map/all_gather | solution.py:415
  9.5 33.6 %copy-start.17 = (bf16[3,1,128,768]{3,2,1,0:T(8,128)(2,1)S(1)}, bf16[3,1,128,768]{3,2,1,0:T(8,128)(2,1)}, u32[]{:S(2)}) copy-start(bf16[3,1,128,768]{3,2,1,0:T(8,128)(2,1)} %param.16) | copy-start | bytes 1769476
  9.5 142.5 %all-gather.13.cloned.1.call-start = ((), (), s32[]{:S(2)}) async-start(), calls=%async_computation.11 | async-start | bytes 5898240 | tf_op jit(solution)/shard_map/all_gather | solution.py:416
  10.1 269.9 %reduce-scatter.19.cloned.1.call-start = ((), (), s32[]{:S(2)}) async-start(), calls=%async_computation.13 | async-start | bytes 1474560 | tf_op jit(solution)/shard_map/reduce_scatter | solution.py:473
  17.4 31.2 %copy-start.5 = (s32[5,8]{1,0:T(8,128)}, s32[5,8]{1,0:T(8,128)S(1)}, u32[]{:S(2)}) copy-start(s32[5,8]{1,0:T(8,128)S(1)} %gather_fusion) | copy-start | bytes 484
  144.7 21.5 %copy-start.1 = (f32[384,768]{1,0:T(8,128)}, f32[384,768]{1,0:T(8,128)S(1)}, u32[]{:S(2)}) copy-start(f32[384,768]{1,0:T(8,128)S(1)} %get-tuple-element.113) | copy-start | bytes 3538948
  152.0 7.5 %copy-start.20 = (f32[384,3072]{1,0:T(8,128)S(1)}, f32[384,3072]{1,0:T(8,128)}, u32[]{:S(2)}) copy-start(f32[384,3072]{1,0:T(8,128)} %get-tuple-element.115) | copy-start | bytes 14155780
  157.6 2.6 copy-start.16
  158.2 5.6 slice-start
  159.5 4.3 copy-start.4
  160.1 3.6 slice-start.1
  163.7 2.5 copy-start.19
  168.4 1.3 copy-start.3
  168.5 148.5 %reduce-scatter.25.cloned.1.call-start = ((), (), s32[]{:S(2)}) async-start(), calls=%async_computation.16 | async-start | bytes 4423680
  253.1 3.1 copy-start.18
  254.8 1.4 copy-start.2
  265.8 101.5 %reduce-scatter.21.cloned.1.call-start = ((), (), s32[]{:S(2)}) async-start(), calls=%async_computation.14 | async-start | bytes 5898240 | tf_op jit(solution)/shard_map/reduce_scatter | solution.py:473
  273.1 144.9 %reduce-scatter.23.cloned.1.call-start = ((), (), s32[]{:S(2)}) async-start(), calls=%async_computation.15 | async-start | bytes 5898240 | tf_op jit(solution)/shard_map/reduce_scatter | solution.py:473
  279.9 202.7 %reduce-scatter.27.cloned.1.call-start = ((), (), s32[]{:S(2)}) async-start(), calls=%async_computation.17 | async-start | bytes 442368
  281.9 267.0 %reduce-scatter.17.cloned.1.call-start = ((), (), s32[]{:S(2)}) async-start(), calls=%async_computation.12 | async-start | bytes 1327104 | tf_op jit(solution)/shard_map/reduce_scatter | solution.py:476
  319.2 297.0 %reduce-scatter.29.cloned.1.call-start = ((), (), s32[]{:S(2)}) async-start(), calls=%async_computation.18 | async-start | bytes 1769472
  369.9 313.0 %reduce-scatter.31.cloned.1.call-start = ((), (), s32[]{:S(2)}) async-start(), calls=%async_computation.19 | async-start | bytes 1327104
Sparse Core Ops, SparseCore 0:
  9.6 33.4 all-gather.6
  44.7 17.4 all-gather.8
  63.7 37.4 all-gather.10
  102.6 37.4 all-gather.12
  168.6 29.0 reduce-scatter.18
  265.9 50.9 reduce-scatter.24
  319.4 47.8 reduce-scatter.20
  370.0 47.8 reduce-scatter.22
  421.2 61.4 reduce-scatter.26
  485.9 63.0 reduce-scatter.16
  552.4 63.8 reduce-scatter.28
  619.9 62.9 reduce-scatter.30

commit v2 on v1

--- a/solution.py
+++ b/solution.py
@@ -367,6 +367,217 @@
     return lax.dot_general(a, b, (((0,), (1,)), ((), ())), preferred_element_type=F32)
 
 
+def first_rows(half, tile):
+    return half if half <= tile else (half // tile + 1) // 2 * tile
+
+
+def reduce_kernel(count, heads, *refs):
+    jobs = len(heads)
+    grads, outs, scratch = refs[:jobs], refs[jobs : 2 * jobs], refs[2 * jobs :]
+    sets = [scratch[7 * j : 7 * j + 7] for j in range(jobs)]
+    load_sem, send_sem, recv_sem, z_send, z_recv = scratch[7 * jobs :]
+    me, shard = lax.axis_index("ctx"), lax.axis_index("fsdp")
+    depth = count // 2
+    y, core = shard // 2, lax.rem(shard, 2)
+    z, x = me // 2, lax.rem(me, 2)
+    other_core = {"fsdp": 2 * y + 1 - core}
+    other_y = {"fsdp": 2 * (1 - y) + core}
+    other_x = {"ctx": 2 * z + 1 - x}
+
+    def along_z(step):
+        return lax.rem(z + step, depth)
+
+    barrier = pltpu.get_barrier_semaphore()
+    for peer in (other_core, other_y, other_x):
+        pl.semaphore_signal(barrier, inc=1, device_id=peer)
+    for step in range(1, depth):
+        pl.semaphore_signal(barrier, inc=1, device_id={"ctx": 2 * along_z(step) + x})
+
+    def remote(src, dst, j, slot, peer):
+        return pltpu.make_async_remote_copy(
+            src_ref=src,
+            dst_ref=dst,
+            send_sem=send_sem.at[j, slot],
+            recv_sem=recv_sem.at[j, slot],
+            device_id=peer,
+        )
+
+    def plan(j):
+        own, got, y_one, x_one, x_two, y_two, z_got = sets[j]
+        half, lanes = own.shape[3], own.shape[4]
+        head = heads[j]
+        tail = head < half
+        loads, firsts = [], []
+        for side in range(2):
+            columns = pl.ds(side * lanes, lanes)
+            for low in range(2):
+                loads.append(
+                    pltpu.make_async_copy(
+                        grads[j].at[:, low, core, :, columns],
+                        own.at[side, :, low],
+                        load_sem.at[j, 2 * side + low],
+                    )
+                )
+            for low in range(2):
+                firsts.append(
+                    remote(
+                        grads[j].at[:, low, 1 - core, :, columns],
+                        got.at[side, :, low],
+                        j,
+                        2 * side + low,
+                        other_core,
+                    )
+                )
+        second = [remote(own.at[1 - y, :, :, 0:head, :], y_one, j, 4, other_y)]
+        third = [remote(own.at[y, :, 1 - x, 0:head, :], x_two, j, 5, other_x)]
+        if tail:
+            second.append(remote(own.at[:, :, 1 - x, head:half, :], x_one, j, 6, other_x))
+            third.append(remote(own.at[1 - y, :, x, head:half, :], y_two, j, 7, other_y))
+        fourth = [
+            pltpu.make_async_remote_copy(
+                src_ref=own.at[y, along_z(step), x],
+                dst_ref=z_got.at[z],
+                send_sem=z_send.at[j, step],
+                recv_sem=z_recv.at[j, step],
+                device_id={"ctx": 2 * along_z(step) + x},
+            )
+            for step in range(1, depth)
+        ]
+        last = [remote(outs[j].at[core], outs[j].at[core], j, 8, other_core)]
+        return (loads, firsts, second, third, fourth, last)
+
+    plans = [plan(j) for j in range(jobs)]
+
+    def add(a, b):
+        return (a.astype(F32) + b.astype(F32)).astype(a.dtype)
+
+    def start(copies):
+        for copy in copies:
+            copy.start()
+
+    def stage_one(j):
+        own, got = sets[j][0], sets[j][1]
+        for copy in plans[j][0]:
+            copy.wait()
+        for copy in plans[j][1]:
+            copy.wait_recv()
+
+        def body(block, carry):
+            for side in range(2):
+                for low in range(2):
+                    own[side, block, low] = add(own[side, block, low], got[side, block, low])
+            return carry
+
+        lax.fori_loop(0, depth, body, 0)
+        start(plans[j][2])
+
+    def stage_two(j):
+        own, _, y_one, x_one, _, _, _ = sets[j]
+        half, head = own.shape[3], heads[j]
+        for copy in plans[j][2]:
+            copy.wait()
+
+        def body(block, carry):
+            for low in range(2):
+                own[y, block, low, 0:head, :] = add(
+                    own[y, block, low, 0:head, :], y_one[block, low]
+                )
+            if head < half:
+                for side in range(2):
+                    own[side, block, x, head:half, :] = add(
+                        own[side, block, x, head:half, :], x_one[side, block]
+                    )
+            return carry
+
+        lax.fori_loop(0, depth, body, 0)
+        start(plans[j][3])
+
+    def stage_three(j):
+        own, _, _, _, x_two, y_two, _ = sets[j]
+        half, head = own.shape[3], heads[j]
+        for copy in plans[j][3]:
+            copy.wait()
+
+        def body(block, carry):
+            own[y, block, x, 0:head, :] = add(own[y, block, x, 0:head, :], x_two[block])
+            if head < half:
+                own[y, block, x, head:half, :] = add(
+                    own[y, block, x, head:half, :], y_two[block]
+                )
+            return carry
+
+        lax.fori_loop(0, depth, body, 0)
+        start(plans[j][4])
+
+    def stage_four(j):
+        own, z_got = sets[j][0], sets[j][6]
+        for copy in plans[j][4]:
+            copy.wait()
+        total = own[y, z, x].astype(F32)
+        for step in range(1, depth):
+            total = total + z_got[along_z(step)].astype(F32)
+        outs[j][core] = total.astype(outs[j].dtype)
+        start(plans[j][5])
+
+    def stage_five(j):
+        for copy in plans[j][5]:
+            copy.wait()
+        for copy in plans[j][1]:
+            copy.wait_send()
+
+    for j in range(jobs):
+        start(plans[j][0])
+    pl.semaphore_wait(barrier, 2 + depth)
+    for j in range(jobs):
+        start(plans[j][1])
+    stages = (stage_one, stage_two, stage_three, stage_four, stage_five)
+    for tick in range(jobs + len(stages) - 1):
+        for k in reversed(range(len(stages))):
+            if 0 <= tick - k < jobs:
+                stages[k](tick - k)
+
+
+def reduce_all(grads, number):
+    count = grads[0].shape[0]
+    depth = count // 2
+    heads, scratch, outs = [], [], []
+    for g in grads:
+        half, lanes = g.shape[2], g.shape[3] // 2
+        head = first_rows(half, 16 if g.dtype == BF16 else 8)
+        tail = max(half - head, 16 if g.dtype == BF16 else 8)
+        heads.append(head)
+        for shape in (
+            (2, depth, 2, half, lanes),
+            (2, depth, 2, half, lanes),
+            (depth, 2, head, lanes),
+            (2, depth, tail, lanes),
+            (depth, head, lanes),
+            (depth, tail, lanes),
+            (depth, half, lanes),
+        ):
+            scratch.append(pltpu.VMEM(shape, g.dtype))
+        outs.append(jax.ShapeDtypeStruct((2, half, lanes), g.dtype))
+    jobs = len(grads)
+    scratch += [
+        pltpu.SemaphoreType.DMA((jobs, 4)),
+        pltpu.SemaphoreType.DMA((jobs, 9)),
+        pltpu.SemaphoreType.DMA((jobs, 9)),
+        pltpu.SemaphoreType.DMA((jobs, depth)),
+        pltpu.SemaphoreType.DMA((jobs, depth)),
+    ]
+    return pl.pallas_call(
+        functools.partial(reduce_kernel, count, tuple(heads)),
+        out_shape=tuple(outs),
+        in_specs=[pl.BlockSpec(memory_space=pl.ANY)] * jobs,
+        out_specs=[pl.BlockSpec(memory_space=pltpu.VMEM)] * jobs,
+        scratch_shapes=scratch,
+        compiler_params=pltpu.CompilerParams(
+            collective_id=number, has_side_effects=True, vmem_limit_bytes=56 * 1024 * 1024
+        ),
+        name="reduce_all",
+    )(*[g.reshape(depth, 2, *g.shape[1:]) for g in grads])
+
+
 def on_device(
     count,
     shards,
@@ -445,17 +656,17 @@
     d_second = norm_backward(incoming, second_normed, second_recip, gain_two)
     d_outer = d_second.astype(BF16)
     return_grad = jnp.sum(d_outer.astype(F32), axis=0)
-    outer_grad = mul_tn(activated_low, d_outer)
+    outer_grad = mul_tn(d_outer, activated_low)
     d_inner = (mul_nt(d_outer, outer) * gelu_slope).astype(BF16)
     hidden_grad = jnp.sum(d_inner.astype(F32), axis=0)
-    inner_grad = mul_tn(first_low, d_inner)
+    inner_grad = mul_tn(d_inner, first_low)
     d_first = d_second + mul_nt(d_inner, inner)
     scale_grad = jnp.sum(d_first * first_normed, axis=0)
     shift_grad = jnp.sum(d_first, axis=0)
     d_residual = norm_backward(d_first, first_normed, first_recip, gain_one)
     d_branch = d_residual.astype(BF16)
     mixing_grad = jnp.sum(d_branch.astype(F32), axis=0)
-    mixer_grad = mul_nn(attended, d_branch)
+    mixer_grad = mul_tt(d_branch, attended)
     flow = mul_nt(mixer, d_branch).astype(BF16)
     flow_units = exchange(to_units(flow, 1, count, units), 2)
     d_units = attend_back(received, flow_units, unit_starts, unit_docs, wide, lse)
@@ -463,24 +674,10 @@
     bias_sums = jnp.sum(d_joint.astype(F32), axis=1)
     query_grad = bias_sums[0:D]
     values_grad = bias_sums[2 * D :]
-    joint_grad = lax.dot_general(
-        source, d_joint, (((0,), (1,)), ((), ())), preferred_element_type=F32
-    )
+    joint_grad = mul_nn(d_joint, source)
     tokens_grad = d_residual + mul_tt(d_joint, joint)
     tokens_grad = tokens_grad.reshape(MB, 1, rows, D)
 
-    def reduced(grad):
-        over_rows = lax.psum_scatter(
-            grad.astype(BF16), "fsdp", scatter_dimension=0, tiled=True
-        )
-        return lax.psum_scatter(over_rows, "ctx", scatter_dimension=1, tiled=True).astype(F32)
-
-    outer_out_grad = reduced(outer_grad)
-    inner_out = reduced(inner_grad)
-    mixer_out = reduced(mixer_grad)
-    joint_out = reduced(joint_grad)
-
-    world = count * shards
     small = [
         query_grad,
         values_grad,
@@ -492,10 +689,37 @@
         rescale_grad,
         reshift_grad,
     ]
+    world = count * shards
     packed = jnp.concatenate([v.reshape(world, -1) for v in small], axis=1)
-    packed = lax.psum(packed, ("ctx", "fsdp"))
-    index = me * shards + lax.axis_index("fsdp")
-    own = lax.dynamic_slice_in_dim(packed, index, 1, 0)[0]
+    turned = [outer_grad, inner_grad, mixer_grad, joint_grad]
+    if shards == 4 and count % 2 == 0 and D % (32 * count) == 0:
+        core = lax.rem(lax.axis_index("fsdp"), 2)
+        bias_job = packed.reshape(count, 2, 2, -1).transpose(0, 2, 1, 3)
+        spare = -packed.shape[1] % 128
+        bias_job = jnp.pad(bias_job, ((0, 0), (0, 0), (0, 0), (0, spare)))
+        bias_job = jnp.pad(bias_job.reshape(count, 2, 1, -1), ((0, 0), (0, 0), (0, 7), (0, 0)))
+        jobs = [g.astype(BF16).reshape(count, 2, -1, g.shape[1]) for g in turned] + [bias_job]
+        *sums, own = reduce_all(jobs, 4)
+        blocks = []
+        for g in sums:
+            width = g.shape[2] // 2
+            g = g.reshape(-1, 2 * width)
+            blocks.append(lax.dynamic_slice_in_dim(g, core * width, width, 1).T.astype(F32))
+        own = lax.dynamic_index_in_dim(own, core, 0, False)[0, : packed.shape[1]]
+    else:
+
+        def reduced(grad):
+            over_lanes = lax.psum_scatter(
+                grad.astype(BF16), "fsdp", scatter_dimension=1, tiled=True
+            )
+            over_rows = lax.psum_scatter(over_lanes, "ctx", scatter_dimension=0, tiled=True)
+            return over_rows.T.astype(F32)
+
+        blocks = [reduced(g) for g in turned]
+        packed = lax.psum(packed, ("ctx", "fsdp"))
+        index = me * shards + lax.axis_index("fsdp")
+        own = lax.dynamic_slice_in_dim(packed, index, 1, 0)[0]
+    outer_out_grad, inner_out, mixer_out, joint_out = blocks
     sums = []
     begin = 0
     for v in small:

time: 696 us -> 433 us (0.62)
  waiting for transfers between devices: 363 us -> 26.7 us
  Pallas kernels: 164 us -> 274 us
  blocking collectives: 46.4 us -> 6.2 us
    unnamed x16 -> x4, waiting for transfers between devices: 178 us -> 2.58 us
    reduce_scatter x4 -> x0, waiting for transfers between devices: 161 us -> none  [the longest x3 96.1 us: reduced(): lax.psum_scatter(grad.astype(BF16), 'fsdp', scatter_dimension=0, tiled=True)]
    pallas_call x0 -> x1, Pallas kernels: none -> 110 us  [reduce_all(): pl.pallas_call(functools.partial(reduce_kernel, count, tuple(heads)), out...]
    psum x1 -> x0, blocking collectives: 40.2 us -> none  [on_device(): packed = lax.psum(packed, ('ctx', 'fsdp'))]
    unnamed x59 -> x50, local copies, waits for them, and re-layouts: 23.9 us -> 6.99 us
    concatenate x1 -> x10, local copies, waits for them, and re-layouts: 0.1 us -> 12.8 us  [on_device(): packed = jnp.concatenate([v.reshape(world, -1) for v in small], axis=1)]
  transfers between devices with their start and end apart: 12 -> 4, of which waited for: 8 -> 1; matrix products, arithmetic and copies ran while one was open for 12% -> 6% of each run, Pallas kernels for 24% -> 20%
where the time goes in v2:
time: 433 us; the launch traced here: 432 us
  Pallas kernels  274 us (63%)
  matrix products  48.1 us (11%)
  local copies, waits for them, and re-layouts  45.7 us (11%)
  waiting for transfers between devices  26.7 us (6%)
  other arithmetic  16.6 us (4%)
  between operations  14.3 us (3%)
  blocking collectives  6.2 us (1%)
    pallas_call x4, Pallas kernels, exchange(): pl.pallas_call(functools.partial(exchange_kernel, count), out_shape=jax.S...  116 us
    pallas_call x1, Pallas kernels, reduce_all(): pl.pallas_call(functools.partial(reduce_kernel, count, tuple(heads)), out...  110 us
    pallas_call x1, Pallas kernels, attend_back(): pl.pallas_call(functools.partial(attend_back_kernel, width), out_shape=ja...  25.1 us
    all_gather x1, waiting for transfers between devices, on_device(): joint = lax.all_gather(joint_weight, 'fsdp', axis=0, tiled=True)  24 us
    pallas_call x1, Pallas kernels, attend(): pl.pallas_call(functools.partial(attend_kernel, width), out_shape=(jax.Sh...  22.8 us
    dot_general x3, matrix products, mul_nn(): return jnp.dot(a, b, preferred_element_type=F32)  17.1 us
    concatenate x10, local copies, waits for them, and re-layouts, on_device(): packed = jnp.concatenate([v.reshape(world, -1) for v in small], axis=1)  12.8 us
    dot_general x3, matrix products, mul_tt(): lax.dot_general(a, b, (((0,), (1,)), ((), ())), preferred_element_type=F32)  11.9 us
  transfers between devices with their start and end apart: 4, of which 1 were waited for; matrix products, arithmetic and copies ran while one was open for 6% of the time, Pallas kernels for 20%

profile of v2, /device:TPU:0, one launch (start us, length us, event | category | flops | bytes accessed | tf_op | source)
XLA Modules:
  0.0 431.7 jit_solution(11883897294326353181)
XLA Ops:
  7.2 0.7 all-gather.7.cloned.1.call-update
  8.0 0.7 all-gather.9.cloned.1.call-update
  8.8 0.7 all-gather.11.cloned.1.call-update
  10.3 6.2 %all-gather.1 = bf16[4,1,2304]{2,1,0:T(2,128)(2,1)S(1)} all-gather(bf16[1,1,2304]{2,1,0:T(2,128)(2,1)S(1)} %reshape.354), channel_id=2, replica_groups=mesh['ctx'=8,'fsdp'=4] {'fsdp'}, dimensions={0}, use_global_device_ids=true | all-gather | bytes 23040 | tf_op jit(solution)/shard_map/all_gather | solution.py:620
  16.8 0.6 gather_fusion
  17.5 0.6 sub.50.docs_ref
  19.0 24.0 %all-gather.7.cloned.1.call-done = bf16[768,2304]{1,0:T(8,128)(2,1)} async-done(((bf16[192,2304]{1,0:T(8,128)(2,1)}), bf16[768,2304]{1,0:T(8,128)(2,1)}) %all-gather.7.cloned.1.call-update) | async-done | bytes 3538960 | tf_op jit(solution)/shard_map/all_gather | solution.py:606
  43.1 5.5 %fusion.6 = bf16[2304,384]{1,0:T(8,128)(2,1)} fusion(bf16[768,2304]{1,0:T(8,128)(2,1)} %all-gather.7.cloned.1.call-done, bf16[384,768]{1,0:T(8,128)(2,1)S(1)} %bitcast.165, f32[2304]{0:T(1024)S(1)} %pad_maximum_fusion), kind=kOutput, calls=%fused_computation.17 | convolution fusion | flops 1360723968 | bytes 5907456 | tf_op jit(solution)/shard_map/dot_general | solution.py:367
  48.6 4.6 %reshape.315 = bf16[3,12,64,3,128]{4,3,2,1,0:T(4,128)(2,1)S(1)} reshape(bf16[2304,384]{1,0:T(8,128)(2,1)} %fusion.6) | data formatting | bytes 3538944 | tf_op jit(solution)/shard_map/reshape | solution.py:341
  53.9 1.4 copy.130
  55.3 36.8 %exchange_0.1.x_ref = bf16[8,5,192,128]{3,2,1,0:T(8,128)(2,1)} custom-call(bf16[8,5,192,128]{3,2,1,0:T(8,128)(2,1)} %bitcast.132), custom_call_target="tpu_custom_call" | custom-call | tf_op jit(solution)/shard_map/exchange_0/pallas_call | solution.py:96
  92.1 22.8 %attend.1 = (bf16[8,5,64,128]{3,2,1,0:T(8,128)(2,1)}, f32[5,64,1024]{2,1,0:T(8,128)}, f32[5,1,1024]{2,1,0:T(1,128)}) custom-call(s32[5,8]{1,0:T(8,128)} %copy-done.4, bf16[8,5,192,128]{3,2,1,0:T(8,128)(2,1)} %exchange_0.1.x_ref, s32[5,1,1024]{2,1,0:T(1,128)} %sub.50.docs_ref), custom_call_target="tpu_custom_call" | custom-call | tf_op jit(solution)/shard_map/attend/pallas_call | solution.py:280
  114.9 25.5 %exchange_1.1 = bf16[8,5,64,128]{3,2,1,0:T(8,128)(2,1)} custom-call(bf16[8,5,64,128]{3,2,1,0:T(8,128)(2,1)} %get-tuple-element.23.x_ref), custom_call_target="tpu_custom_call" | custom-call | tf_op jit(solution)/shard_map/exchange_1/pallas_call | solution.py:96
  140.3 1.1 copy.84
  142.1 2.4 fusion.39
  144.8 7.0 %multiply_convert_fusion = (bf16[384,3072]{1,0:T(8,128)(2,1)}, f32[384,3072]{1,0:T(8,128)}) fusion(f32[3072]{0:T(1024)S(1)} %reshape.340, bf16[768,3072]{1,0:T(8,128)(2,1)} %all-gather.11.cloned.1.call-done, f32[384,768]{1,0:T(8,128)S(1)} %get-tuple-element.138, f32[768]{0:T(1024)S(1)} %reshape.339, f32[768]{0:T(1024)S(1)} %reshape.338, ...), kind=kOutput, calls=%fused_computation.13 | convolution fusion | flops 1820491776 | bytes 12997632 | tf_op jit(solution)/shard_map/dot_general | solution.py:355
  151.8 5.3 %fusion.40 = (f32[384]{0:T(512)S(1)}, f32[384,768]{1,0:T(8,128)S(1)}) fusion(f32[768]{0:T(1024)S(1)} %reshape.341, bf16[384,3072]{1,0:T(8,128)(2,1)} %get-tuple-element.139, bf16[3072,768]{1,0:T(8,128)(2,1)} %all-gather.13.cloned.1.call-done, f32[768]{0:T(1024)S(1)} %reshape.339, f32[768]{0:T(1024)S(1)} %reshape.338, f32[384]{0:T(512)S(1)} %add_rsqrt_fusion.1, ...), kind=kOutput, calls=%fused_computation.112 | convolution fusion | flops 1814003328 | bytes 9451008 | tf_op jit(solution)/shard_map/dot_general | solution.py:355
  157.4 1.1 fusion.24
  158.5 1.9 convert_reduce_fusion.3
  160.5 4.3 %convolution_convert_fusion.2 = bf16[768,3072]{1,0:T(8,128)(2,1)} fusion(bf16[384,3072]{1,0:T(8,128)(2,1)S(1)} %copy-done.17, f32[384,768]{1,0:T(8,128)S(1)} %get-tuple-element.115), kind=kOutput, calls=%fused_computation.4 | convolution fusion | flops 1814593536 | bytes 8257536 | tf_op jit(solution)/shard_map/dot_general | solution.py:359
  164.8 4.1 convert_reduce_fusion
  168.9 4.6 %convolution_convert_fusion.1 = bf16[3072,768]{1,0:T(8,128)(2,1)} fusion(bf16[384,3072]{1,0:T(8,128)(2,1)S(1)} %get-tuple-element.145, f32[384,768]{1,0:T(8,128)S(1)} %get-tuple-element.138, f32[768]{0:T(1024)S(1)} %reshape.339, f32[768]{0:T(1024)S(1)} %reshape.338, f32[384]{0:T(512)S(1)} %add_rsqrt_fusion.1, f32[384]{0:T(512)S(1)} %broadcast_multiply_fusion.4), kind=kOutput, calls=%fused_computation.3 | convolution fusion | flops 1815773184 | bytes 8266752 | tf_op jit(solution)/shard_map/dot_general | solution.py:359
  173.5 2.9 multiply_reduce_fusion
  176.4 1.0 convert_reduce_fusion.4
  177.7 0.7 fusion.17
  179.1 0.9 copy.131
  180.0 17.5 %exchange_2.1.flow_ref = bf16[8,5,64,128]{3,2,1,0:T(8,128)(2,1)} custom-call(bf16[8,5,64,128]{3,2,1,0:T(8,128)(2,1)} %bitcast.143), custom_call_target="tpu_custom_call" | custom-call | tf_op jit(solution)/shard_map/exchange_2/pallas_call | solution.py:96
  197.6 25.1 %attend_back.1.x_ref = bf16[8,5,192,128]{3,2,1,0:T(8,128)(2,1)} custom-call(s32[5,8]{1,0:T(8,128)} %copy-done.4, bf16[8,5,192,128]{3,2,1,0:T(8,128)(2,1)} %exchange_0.1.x_ref, bf16[8,5,64,128]{3,2,1,0:T(8,128)(2,1)} %exchange_2.1.flow_ref, s32[5,1,1024]{2,1,0:T(1,128)} %sub.50.docs_ref, f32[5,64,1024]{2,1,0:T(8,128)} %get-tuple-element.24.wide_ref, ...), custom_call_target="tpu_custom_call" | custom-call | tf_op jit(solution)/shard_map/attend_back/pallas_call | solution.py:311
  222.6 36.6 %exchange_3.1 = bf16[8,5,192,128]{3,2,1,0:T(8,128)(2,1)} custom-call(bf16[8,5,192,128]{3,2,1,0:T(8,128)(2,1)} %attend_back.1.x_ref), custom_call_target="tpu_custom_call" | custom-call | tf_op jit(solution)/shard_map/exchange_3/pallas_call | solution.py:96
  259.3 1.7 copy.89
  261.1 5.2 %convert_reduce_fusion.1 = f32[3,12,64]{2,1,0:T(8,128)S(1)} fusion(bf16[3,12,3,64,128]{4,3,2,1,0:T(8,128)(2,1)S(1)} %bitcast.128), kind=kLoop, calls=%fused_computation.12 | loop fusion | flops 1767168 | bytes 1778688 | tf_op jit(solution)/shard_map/reduce_sum | solution.py:674
  266.3 1.7 copy.90
  268.0 1.8 convolution_convert_fusion.3
  269.8 0.6 fusion.38
  270.4 1.4 concatenate.30
  271.8 1.4 concatenate.31
  273.2 1.4 concatenate.32
  274.6 1.4 concatenate.33
  275.9 1.4 concatenate.34
  277.3 1.4 concatenate.35
  278.7 1.4 concatenate.36
  280.1 1.4 concatenate.37
  281.5 1.7 concatenate.39
  283.2 0.8 copy.103
  284.0 0.6 pad.18.clone
  284.6 1.5 reshape.329
  286.1 0.8 copy.104
  286.9 0.8 pad.19.clone
  287.7 4.8 %convolution_convert_fusion = bf16[2304,768]{1,0:T(8,128)(2,1)} fusion(bf16[384,768]{1,0:T(8,128)(2,1)} %bitcast.164, bf16[288,8,3,128]{3,2,1,0:T(4,128)(2,1)S(1)} %bitcast.147), kind=kOutput, calls=%fused_computation.2 | convolution fusion | flops 1360723968 | bytes 5898240 | tf_op jit(solution)/shard_map/dot_general | solution.py:355
  292.6 109.7 %reduce_all.1 = (bf16[2,48,1536]{2,1,0:T(8,128)(2,1)}, bf16[2,192,384]{2,1,0:T(8,128)(2,1)}, bf16[2,48,384]{2,1,0:T(8,128)(2,1)}, bf16[2,144,384]{2,1,0:T(8,128)(2,1)}, f32[2,8,384]{2,1,0:T(8,128)}) custom-call(bf16[4,2,2,48,3072]{4,3,2,1,0:T(8,128)(2,1)} %bitcast.136, bf16[4,2,2,192,768]{4,3,2,1,0:T(8,128)(2,1)} %bitcast.137, ...), custom_call_target="tpu_custom_call" | custom-call | tf_op jit(solution)/shard_map/reduce_all/pallas_call | solution.py:568
  402.3 0.7 dynamic-slice_bitcast_fusion
  403.1 0.6 slice_bitcast_fusion
  403.7 0.6 slice_bitcast_fusion.3
  404.2 1.8 constant_dynamic-slice_fusion
  406.0 1.7 copy.102
  407.7 1.6 convert_bitcast_fusion.1
  409.4 1.7 constant_dynamic-slice_fusion.2
  411.1 1.7 copy.100
  412.8 1.6 convert_bitcast_fusion.2
  414.4 1.6 constant_dynamic-slice_fusion.1
  416.0 1.5 copy.101
  417.5 1.4 convert_bitcast_fusion.3
  419.0 1.6 convert_bitcast_fusion
  420.6 4.6 %fusion.11 = f32[384,768]{1,0:T(8,128)} fusion(f32[384,768]{1,0:T(8,128)S(1)} %get-tuple-element.117, bf16[768,2304]{1,0:T(8,128)(2,1)} %all-gather.7.cloned.1.call-done, bf16[288,8,3,128]{3,2,1,0:T(4,128)(2,1)S(1)} %bitcast.148), kind=kOutput, calls=%fused_computation.27 | convolution fusion | flops 1359249408 | bytes 7667712 | tf_op jit(solution)/shard_map/dot_general | solution.py:367
  (92 shorter events, 5.1 us)
Async XLA Ops:
  7.2 35.9 %all-gather.7.cloned.1.call-start = ((), (), s32[]{:S(2)}) async-start(), calls=%async_computation | async-start | bytes 4423680 | tf_op jit(solution)/shard_map/all_gather | solution.py:606
  7.9 134.2 %all-gather.9.cloned.1.call-start = ((), (), s32[]{:S(2)}) async-start(), calls=%async_computation.1 | async-start | bytes 1474560 | tf_op jit(solution)/shard_map/all_gather | solution.py:625
  8.7 1.4 copy-start.5
  8.7 1.4 copy-start.7
  8.7 1.4 copy-start.8
  8.7 1.4 copy-start.9
  8.7 1.4 copy-start.10
  8.7 1.4 copy-start.11
  8.7 1.4 copy-start.12
  8.7 1.4 copy-start.13
  8.7 1.4 copy-start.14
  8.8 8.0 %copy-start.6 = (s32[3,1,8]{2,1,0:T(1,128)S(1)}, s32[3,1,8]{2,1,0:T(1,128)}, u32[]{:S(2)}) copy-start(s32[3,1,8]{2,1,0:T(1,128)} %param.17) | copy-start | bytes 292
  8.8 9.8 %copy-start = (bf16[3,1,128,768]{3,2,1,0:T(8,128)(2,1)S(1)}, bf16[3,1,128,768]{3,2,1,0:T(8,128)(2,1)}, u32[]{:S(2)}) copy-start(bf16[3,1,128,768]{3,2,1,0:T(8,128)(2,1)} %param.31) | copy-start | bytes 1769476
  8.8 136.1 %all-gather.11.cloned.1.call-start = ((), (), s32[]{:S(2)}) async-start(), calls=%async_computation.2 | async-start | bytes 5898240 | tf_op jit(solution)/shard_map/all_gather | solution.py:626
  9.5 33.6 %copy-start.16 = (bf16[3,1,128,768]{3,2,1,0:T(8,128)(2,1)S(1)}, bf16[3,1,128,768]{3,2,1,0:T(8,128)(2,1)}, u32[]{:S(2)}) copy-start(bf16[3,1,128,768]{3,2,1,0:T(8,128)(2,1)} %param.16) | copy-start | bytes 1769476
  9.5 142.3 %all-gather.13.cloned.1.call-start = ((), (), s32[]{:S(2)}) async-start(), calls=%async_computation.3 | async-start | bytes 5898240 | tf_op jit(solution)/shard_map/all_gather | solution.py:627
  17.3 31.2 %copy-start.4 = (s32[5,8]{1,0:T(8,128)}, s32[5,8]{1,0:T(8,128)S(1)}, u32[]{:S(2)}) copy-start(s32[5,8]{1,0:T(8,128)S(1)} %gather_fusion) | copy-start | bytes 484
  142.1 2.5 copy-start.1
  151.8 13.0 %copy-start.18 = (f32[384,3072]{1,0:T(8,128)S(1)}, f32[384,3072]{1,0:T(8,128)}, u32[]{:S(2)}) copy-start(f32[384,3072]{1,0:T(8,128)} %get-tuple-element.140) | copy-start | bytes 14155780
  158.5 1.9 copy-start.17
  160.5 4.4 %copy-start.15 = (bf16[3072,768]{1,0:T(8,128)(2,1)S(1)}, bf16[3072,768]{1,0:T(8,128)(2,1)}, u32[]{:S(2)}) copy-start(bf16[3072,768]{1,0:T(8,128)(2,1)} %all-gather.13.cloned.1.call-done) | copy-start | bytes 14155780
  160.5 13.0 %slice-start = ((s8[4718592]{0:T(1024)(128)(4,1)}), s8[4194304]{0:T(1024)(128)(4,1)S(1)}, s32[]{:S(2)}) async-start(s8[4718592]{0:T(1024)(128)(4,1)} %bitcast.161), calls=%async_computation.4 | async-start | bytes 8388608
  164.8 8.7 %slice-start.1 = ((s8[4718592]{0:T(1024)(128)(4,1)}), s8[524288]{0:T(1024)(128)(4,1)S(1)}, s32[]{:S(2)}) async-start(s8[4718592]{0:T(1024)(128)(4,1)} %bitcast.161), calls=%async_computation.5 | async-start | bytes 1048576
  176.4 1.3 copy-start.3
  266.3 1.7 copy-start.2
Sparse Core Ops, SparseCore 0:
  9.6 33.4 all-gather.6
  44.6 17.4 all-gather.8
  63.7 37.4 all-gather.10
  102.7 37.4 all-gather.12

commit v3 on v2

--- a/solution.py
+++ b/solution.py
@@ -133,67 +133,6 @@
     if chunks == 1:
         return body(0, carry)
     return lax.fori_loop(0, chunks, body, carry)
-
-
-def attend_kernel(
-    width, starts_ref, x_ref, docs_ref, o_ref, wide_ref, lse_ref, key_rows, value_t, key_docs
-):
-    count, _, _, lanes = x_ref.shape
-    length = count * lanes
-    depth = min(length, 1024)
-    unit = pl.program_id(0)
-    for i in range(count):
-        rows = slice(i * lanes, (i + 1) * lanes)
-        key_rows[rows, :] = x_ref[i, 0, HD : 2 * HD, :].T
-        value_t[:, rows] = x_ref[i, 0, 2 * HD : 3 * HD, :]
-    key_documents(starts_ref, unit, length, lanes, key_docs)
-    group = width // lanes
-
-    def block(number, carry):
-        begin = pl.multiple_of(number * width, width)
-        queries = across(x_ref, number * group, slice(0, HD), width, lanes) * SCALE
-        query_docs = docs_ref[0, :, pl.ds(begin, width)]
-
-        def chunk(index, running):
-            peak, total, mixed = running
-            first = pl.multiple_of(index * depth, depth)
-            scores = jnp.dot(
-                key_rows[pl.ds(first, depth), :], queries, preferred_element_type=F32
-            )
-            same = same_document(key_docs, first, depth, query_docs)
-            scores = jnp.where(same, scores, MASKED)
-            new_peak = jnp.maximum(peak, jnp.max(scores, axis=0, keepdims=True))
-            scaling = jnp.exp(peak - new_peak)
-            weights = jnp.exp(scores - new_peak)
-            return (
-                new_peak,
-                total * scaling + jnp.sum(weights, axis=0, keepdims=True),
-                mixed * scaling
-                + jnp.dot(
-                    value_t[:, pl.ds(first, depth)],
-                    weights.astype(BF16),
-                    preferred_element_type=F32,
-                ),
-            )
-
-        peak, total, mixed = over_chunks(
-            length // depth,
-            chunk,
-            (
-                jnp.full((1, width), -jnp.inf, F32),
-                jnp.zeros((1, width), F32),
-                jnp.zeros((HD, width), F32),
-            ),
-        )
-        mixed = mixed / total
-        wide_ref[0, :, pl.ds(begin, width)] = mixed
-        lse_ref[0, :, pl.ds(begin, width)] = peak + jnp.log(total)
-        low = mixed.astype(BF16)
-        for i in range(group):
-            o_ref[number * group + i, 0] = low[:, i * lanes : (i + 1) * lanes]
-        return carry
-
-    lax.fori_loop(0, length // width, block, 0)
 
 
 def attend_back_kernel(
@@ -228,7 +167,7 @@
 
     def block(number, carry):
         begin = pl.multiple_of(number * width, width)
-        queries = across(x_ref, number * group, slice(0, HD), width, lanes) * SCALE
+        queries = across(x_ref, number * group, slice(0, HD), width, lanes)
         flow = across(flow_ref, number * group, slice(0, HD), width, lanes)
         query_rows = queries.T
         flow_rows = flow.T
@@ -271,37 +210,6 @@
 
 def own_block(*dims):
     return pl.BlockSpec(dims, lambda u, starts: (u,) + (0,) * (len(dims) - 1))
-
-
-def attend(x, starts, docs):
-    count, units, _, lanes = x.shape
-    length = count * lanes
-    width = 2 * lanes if count % 2 == 0 else lanes
-    return pl.pallas_call(
-        functools.partial(attend_kernel, width),
-        out_shape=(
-            jax.ShapeDtypeStruct((count, units, HD, lanes), BF16),
-            jax.ShapeDtypeStruct((units, HD, length), F32),
-            jax.ShapeDtypeStruct((units, 1, length), F32),
-        ),
-        grid_spec=pltpu.PrefetchScalarGridSpec(
-            num_scalar_prefetch=1,
-            grid=(units,),
-            in_specs=[unit_block(count, 1, 3 * HD, lanes), own_block(1, 1, length)],
-            out_specs=[
-                unit_block(count, 1, HD, lanes),
-                own_block(1, HD, length),
-                own_block(1, 1, length),
-            ],
-            scratch_shapes=[
-                pltpu.VMEM((length, HD), BF16),
-                pltpu.VMEM((HD, length), BF16),
-                pltpu.VMEM((length, lanes), jnp.int32),
-            ],
-        ),
-        compiler_params=pltpu.CompilerParams(dimension_semantics=("arbitrary",)),
-        name="attend",
-    )(starts, x, docs)
 
 
 def attend_back(x, flow, starts, docs, wide, lse):
@@ -338,7 +246,7 @@
 
 def to_units(columns, parts, count, units):
     rows = columns.shape[1] // MB
-    x = columns.reshape(parts, H, HD, MB, rows).transpose(3, 1, 0, 2, 4)
+    x = columns.reshape(parts, H, HD, MB, rows).transpose(1, 3, 0, 2, 4)
     x = x.reshape(MB * H, parts * HD, rows)
     x = jnp.pad(x, ((0, units * count - MB * H), (0, 0), (0, 0)))
     return x.reshape(units, count, parts * HD, rows).transpose(1, 0, 2, 3)
@@ -347,7 +255,7 @@
 def from_units(x, parts):
     count, units, _, rows = x.shape
     x = x.transpose(1, 0, 2, 3).reshape(units * count, parts * HD, rows)[: MB * H]
-    x = x.reshape(MB, H, parts, HD, rows).transpose(2, 1, 3, 0, 4)
+    x = x.reshape(H, MB, parts, HD, rows).transpose(2, 0, 3, 1, 4)
     return x.reshape(parts * D, MB * rows)
 
 
@@ -365,6 +273,483 @@
 
 def mul_tt(a, b):
     return lax.dot_general(a, b, (((0,), (1,)), ((), ())), preferred_element_type=F32)
+
+
+def forward_kernel(
+    width,
+    starts_ref,
+    tok_ref,
+    docs_ref,
+    joint_ref,
+    vec_ref,
+    mixer_ref,
+    inner_ref,
+    outer_ref,
+    att_ref,
+    got_ref,
+    wide_ref,
+    lse_ref,
+    joint_out,
+    vec_out,
+    mixer_out,
+    inner_out,
+    outer_out,
+    joint_all,
+    bias_rows,
+    put,
+    back_put,
+    back_got,
+    key_rows,
+    value_t,
+    key_docs,
+    mixer_own,
+    inner_own,
+    outer_own,
+    put_sem,
+    got_sem,
+    back_put_sem,
+    back_got_sem,
+    joint_sems,
+    weight_sems,
+    own_sems,
+):
+    count, units, _, lanes = got_ref.shape
+    length = count * lanes
+    depth = min(length, 1024)
+    group = width // lanes
+    pairs = H // 2
+    total_units = MB * H
+    part = joint_ref.shape[0]
+    me, shard = lax.axis_index("ctx"), lax.axis_index("fsdp")
+    y, core = shard // 2, lax.rem(shard, 2)
+    x = lax.rem(me, 2)
+    far = 2 * (1 - y) + core
+    other_core = {"fsdp": 2 * y + 1 - core}
+    other_y = {"fsdp": far}
+    other_x = {"ctx": me + 1 - 2 * x}
+    mine = (total_units - me + count - 1) // count
+
+    barrier = pltpu.get_barrier_semaphore()
+
+    def greet(step, carry):
+        pl.semaphore_signal(barrier, inc=1, device_id={"ctx": lax.rem(me + step, count)})
+        return carry
+
+    lax.fori_loop(1, count, greet, 0)
+    pl.semaphore_signal(barrier, inc=1, device_id=other_core)
+    pl.semaphore_signal(barrier, inc=1, device_id=other_y)
+
+    def remote(src, dst, sems, index, peer):
+        return pltpu.make_async_remote_copy(
+            src_ref=src,
+            dst_ref=dst,
+            send_sem=sems.at[(0, *index)],
+            recv_sem=sems.at[(1, *index)],
+            device_id=peer,
+        )
+
+    def own_joint(pair, third):
+        columns = pl.ds(pl.multiple_of(third * D + pair * 128, 128), 128)
+        return pltpu.make_async_copy(
+            joint_ref.at[:, columns],
+            joint_all.at[pair, shard, :, pl.ds(third * 128, 128)],
+            own_sems.at[0, pair, third],
+        )
+
+    def joint_copy(kind, pair, third, which, peer, source=None):
+        here = joint_all.at[pair, which, :, pl.ds(third * 128, 128)]
+        if source is None:
+            source = here
+        else:
+            source = source.at[:, pl.ds(pl.multiple_of(third * D + pair * 128, 128), 128)]
+        return remote(source, here, joint_sems, (kind, pair, third), peer)
+
+    def joint_y(pair, third):
+        return joint_copy(0, pair, third, shard, other_y, joint_ref)
+
+    def joint_core(pair, third):
+        return joint_copy(1, pair, third, shard, other_core, joint_ref)
+
+    def joint_pass(pair, third):
+        return joint_copy(2, pair, third, far, other_core)
+
+    def joint_store(pair, third):
+        columns = pl.ds(pl.multiple_of(third * D + pair * 128, 128), 128)
+        return pltpu.make_async_copy(
+            joint_all.at[pair, :, :, pl.ds(third * 128, 128)],
+            joint_out.at[:, :, columns],
+            own_sems.at[0, pair, third],
+        )
+
+    def each_third(pair, make, act):
+        for third in range(3):
+            getattr(make(pair, third), act)()
+
+    def every_pair(make, act):
+        def body(pair, carry):
+            each_third(pair, make, act)
+            return carry
+
+        lax.fori_loop(0, pairs, body, 0)
+
+    every_pair(own_joint, "start")
+    wholes = ((mixer_ref, mixer_own, mixer_out), (inner_ref, inner_own, inner_out), (outer_ref, outer_own, outer_out))
+    own_in = [
+        pltpu.make_async_copy(ref, held, own_sems.at[1, i, 0])
+        for i, (ref, held, _) in enumerate(wholes)
+    ]
+    own_out = [
+        pltpu.make_async_copy(held, out.at[shard], own_sems.at[1, i, 1])
+        for i, (_, held, out) in enumerate(wholes)
+    ]
+    for copy in own_in:
+        copy.start()
+    vec_own = pltpu.make_async_copy(vec_ref, vec_out.at[shard], own_sems.at[1, 3, 0])
+    vec_own.start()
+    pl.semaphore_wait(barrier, count + 1)
+
+    vec_y = remote(vec_ref, vec_out.at[shard], weight_sems, (0, 0), other_y)
+    vec_core = remote(vec_ref, vec_out.at[shard], weight_sems, (0, 1), other_core)
+    vec_pass = remote(vec_out.at[far], vec_out.at[far], weight_sems, (0, 2), other_core)
+    mixer_y = remote(mixer_ref, mixer_out.at[shard], weight_sems, (1, 0), other_y)
+    mixer_core = remote(mixer_ref, mixer_out.at[shard], weight_sems, (1, 1), other_core)
+    mixer_pass = remote(mixer_out.at[far], mixer_out.at[far], weight_sems, (1, 2), other_core)
+    halves = []
+    for i, (ref, out) in enumerate(((inner_ref, inner_out), (outer_ref, outer_out))):
+        size = ref.shape[0] // 2
+        rows = pl.ds(pl.multiple_of(x * size, size), size)
+        halves.append(
+            (
+                remote(ref.at[rows, :], out.at[shard, rows, :], weight_sems, (2 + i, 0), other_y),
+                remote(ref, out.at[shard], weight_sems, (2 + i, 1), other_core),
+                remote(
+                    out.at[far, rows, :], out.at[far, rows, :], weight_sems, (2 + i, 3), other_x
+                ),
+                remote(out.at[far], out.at[far], weight_sems, (2 + i, 2), other_core),
+            )
+        )
+    vec_y.start()
+    vec_core.start()
+    every_pair(joint_y, "start")
+    every_pair(joint_core, "start")
+    mixer_y.start()
+    mixer_core.start()
+    for copies in halves:
+        copies[0].start()
+        copies[1].start()
+    for first, second in zip(own_in, own_out):
+        first.wait()
+        second.start()
+
+    vec_own.wait()
+    vec_y.wait_recv()
+    vec_pass.start()
+    vec_core.wait_recv()
+    vec_pass.wait_recv()
+
+    def bias_of(slot):
+        pieces = [
+            vec_out[f, slot : slot + 1, 0:part].astype(F32) for f in range(4)
+        ]
+        return jnp.concatenate(pieces, axis=1)
+
+    query_bias, value_bias = bias_of(0), bias_of(1)
+    for pair in range(pairs):
+        columns = slice(pair * 128, (pair + 1) * 128)
+        bias_rows[pair, :, 0:128] = jnp.broadcast_to(query_bias[:, columns], (8, 128))
+        bias_rows[pair, :, 128:256] = jnp.zeros((8, 128), F32)
+        bias_rows[pair, :, 256:384] = jnp.broadcast_to(value_bias[:, columns], (8, 128))
+
+    def sent_sem(unit):
+        return lax.rem(unit, count), unit // count
+
+    def send_copy(unit):
+        owner, slot = sent_sem(unit)
+        return pltpu.make_async_remote_copy(
+            src_ref=put.at[owner, slot],
+            dst_ref=got_ref.at[me, slot],
+            send_sem=put_sem.at[owner, slot],
+            recv_sem=got_sem.at[me, slot],
+            device_id={"ctx": owner},
+        )
+
+    def keep_copy(unit):
+        owner, slot = sent_sem(unit)
+        return pltpu.make_async_copy(
+            put.at[owner, slot], got_ref.at[me, slot], own_sems.at[2, slot, 0]
+        )
+
+    def project(pair, carry):
+        each_third(pair, own_joint, "wait")
+        each_third(pair, joint_y, "wait_recv")
+        each_third(pair, joint_pass, "start")
+        each_third(pair, joint_core, "wait_recv")
+        each_third(pair, joint_pass, "wait_recv")
+        each_third(pair, joint_store, "start")
+        weight = joint_all[pair].reshape(4 * part, 384)
+        rows = jnp.dot(tok_ref[...], weight, preferred_element_type=F32)
+        rows = (rows + bias_rows[pair, 0:1, :]).astype(BF16)
+        for third in range(3):
+            for batch in range(MB):
+                block = rows[batch * lanes : (batch + 1) * lanes, third * 128 : (third + 1) * 128]
+                turned = block.T
+                if third == 0:
+                    turned = turned * SCALE
+                for j in range(2):
+                    unit = (2 * pair + j) * MB + batch
+                    put[lax.rem(unit, count), unit // count, third * HD : (third + 1) * HD, :] = (
+                        turned[j * HD : (j + 1) * HD]
+                    )
+        for i in range(2 * MB):
+            unit = 2 * pair * MB + i
+
+            @pl.when(lax.rem(unit, count) != me)
+            def _():
+                send_copy(unit).start()
+
+            @pl.when(lax.rem(unit, count) == me)
+            def _():
+                keep_copy(unit).start()
+
+        return carry
+
+    lax.fori_loop(0, pairs, project, 0)
+
+    mixer_y.wait_recv()
+    mixer_pass.start()
+
+    def arrival(sender, slot):
+        return pltpu.make_async_remote_copy(
+            src_ref=put.at[sender, slot],
+            dst_ref=got_ref.at[sender, slot],
+            send_sem=put_sem.at[sender, slot],
+            recv_sem=got_sem.at[sender, slot],
+            device_id={"ctx": sender},
+        )
+
+    def back_copy(peer, slot):
+        return pltpu.make_async_remote_copy(
+            src_ref=back_put.at[peer, slot],
+            dst_ref=back_got.at[me, slot],
+            send_sem=back_put_sem.at[peer, slot],
+            recv_sem=back_got_sem.at[me, slot],
+            device_id={"ctx": peer},
+        )
+
+    def back_keep(slot):
+        return pltpu.make_async_copy(
+            back_put.at[me, slot], back_got.at[me, slot], own_sems.at[2, slot, 1]
+        )
+
+    def relay(i):
+        halves[i][0].wait_recv()
+        halves[i][2].start()
+
+    def hand_on(i):
+        halves[i][2].wait_recv()
+        halves[i][3].start()
+
+    early = total_units // count > 2
+
+    def unit_step(slot, carry):
+        def wait_one(step, inner):
+            arrival(lax.rem(me + step, count), slot).wait_recv()
+            return inner
+
+        lax.fori_loop(1, count, wait_one, 0)
+        keep_copy(slot * count + me).wait()
+        for i in range(count):
+            rows = slice(i * lanes, (i + 1) * lanes)
+            key_rows[rows, :] = got_ref[i, slot, HD : 2 * HD, :].T
+            value_t[:, rows] = got_ref[i, slot, 2 * HD : 3 * HD, :]
+        key_documents(starts_ref, slot, length, lanes, key_docs)
+
+        def block(number, inner):
+            begin = pl.multiple_of(number * width, width)
+            parts = [got_ref[number * group + i, slot, 0:HD, :] for i in range(group)]
+            queries = parts[0] if group == 1 else jnp.concatenate(parts, axis=1)
+            query_docs = docs_ref[slot, :, pl.ds(begin, width)]
+
+            def chunk(index, running):
+                peak, total, mixed = running
+                first = pl.multiple_of(index * depth, depth)
+                scores = jnp.dot(
+                    key_rows[pl.ds(first, depth), :], queries, preferred_element_type=F32
+                )
+                same = same_document(key_docs, first, depth, query_docs)
+                scores = jnp.where(same, scores, MASKED)
+                new_peak = jnp.maximum(peak, jnp.max(scores, axis=0, keepdims=True))
+                scaling = jnp.exp(peak - new_peak)
+                weights = jnp.exp(scores - new_peak)
+                return (
+                    new_peak,
+                    total * scaling + jnp.sum(weights, axis=0, keepdims=True),
+                    mixed * scaling
+                    + jnp.dot(
+                        value_t[:, pl.ds(first, depth)],
+                        weights.astype(BF16),
+                        preferred_element_type=F32,
+                    ),
+                )
+
+            peak, total, mixed = over_chunks(
+                length // depth,
+                chunk,
+                (
+                    jnp.full((1, width), -jnp.inf, F32),
+                    jnp.zeros((1, width), F32),
+                    jnp.zeros((HD, width), F32),
+                ),
+            )
+            mixed = mixed / total
+            wide_ref[slot, :, pl.ds(begin, width)] = mixed
+            lse_ref[slot, :, pl.ds(begin, width)] = peak + jnp.log(total)
+            low = mixed.astype(BF16)
+            for i in range(group):
+                back_put[number * group + i, slot] = low[:, i * lanes : (i + 1) * lanes]
+            return inner
+
+        lax.fori_loop(0, length // width, block, 0)
+
+        def send_one(step, inner):
+            back_copy(lax.rem(me + step, count), slot).start()
+            return inner
+
+        lax.fori_loop(1, count, send_one, 0)
+        back_keep(slot).start()
+        if early:
+
+            @pl.when(slot == 2)
+            def _():
+                relay(0)
+
+        return carry
+
+    lax.fori_loop(0, mine, unit_step, 0)
+
+    if not early:
+        relay(0)
+    relay(1)
+    hand_on(0)
+
+    def home(unit, carry):
+        owner, slot = lax.rem(unit, count), unit // count
+
+        @pl.when(owner != me)
+        def _():
+            pltpu.make_async_remote_copy(
+                src_ref=back_put.at[owner, slot],
+                dst_ref=back_got.at[owner, slot],
+                send_sem=back_put_sem.at[owner, slot],
+                recv_sem=back_got_sem.at[owner, slot],
+                device_id={"ctx": owner},
+            ).wait_recv()
+
+        @pl.when(owner == me)
+        def _():
+            back_keep(slot).wait()
+
+        return carry
+
+    lax.fori_loop(0, total_units, home, 0)
+    for pair in range(pairs):
+        for batch in range(MB):
+            tops = []
+            for j in range(2):
+                unit = (2 * pair + j) * MB + batch
+                tops.append(back_got[unit % count, unit // count])
+            block = jnp.concatenate(tops, axis=0).T
+            att_ref[batch * lanes : (batch + 1) * lanes, pair * 128 : (pair + 1) * 128] = block
+
+    hand_on(1)
+    for copies in halves:
+        copies[0].wait_send()
+        copies[1].wait()
+        copies[2].wait_send()
+        copies[3].wait()
+    vec_y.wait_send()
+    vec_core.wait_send()
+    vec_pass.wait_send()
+    mixer_y.wait_send()
+    mixer_core.wait()
+    mixer_pass.wait()
+    every_pair(joint_y, "wait_send")
+    every_pair(joint_core, "wait_send")
+    every_pair(joint_pass, "wait_send")
+    for copy in own_out:
+        copy.wait()
+
+    def sent(unit, carry):
+        @pl.when(lax.rem(unit, count) != me)
+        def _():
+            send_copy(unit).wait_send()
+
+        return carry
+
+    lax.fori_loop(0, total_units, sent, 0)
+
+    def returned(slot, carry):
+        def one(step, inner):
+            back_copy(lax.rem(me + step, count), slot).wait_send()
+            return inner
+
+        lax.fori_loop(1, count, one, 0)
+        return carry
+
+    lax.fori_loop(0, mine, returned, 0)
+    every_pair(joint_store, "wait")
+
+
+def forward(count, starts, tokens, docs, joint, vectors, mixer, inner, outer, number):
+    units = starts.shape[0]
+    lanes = tokens.shape[0] // MB
+    length = count * lanes
+    width = 2 * lanes
+    part = joint.shape[0]
+    pairs = H // 2
+    vm = pl.BlockSpec(memory_space=pltpu.VMEM)
+    hbm = pl.BlockSpec(memory_space=pl.ANY)
+    dma = pltpu.SemaphoreType.DMA
+    return pl.pallas_call(
+        functools.partial(forward_kernel, width),
+        out_shape=(
+            jax.ShapeDtypeStruct(tokens.shape, BF16),
+            jax.ShapeDtypeStruct((count, units, 3 * HD, lanes), BF16),
+            jax.ShapeDtypeStruct((units, HD, length), F32),
+            jax.ShapeDtypeStruct((units, 1, length), F32),
+            jax.ShapeDtypeStruct((4, *joint.shape), BF16),
+            jax.ShapeDtypeStruct((4, *vectors.shape), BF16),
+            jax.ShapeDtypeStruct((4, *mixer.shape), BF16),
+            jax.ShapeDtypeStruct((4, *inner.shape), BF16),
+            jax.ShapeDtypeStruct((4, *outer.shape), BF16),
+        ),
+        in_specs=[pl.BlockSpec(memory_space=pltpu.SMEM), vm, vm, hbm, vm, hbm, hbm, hbm],
+        out_specs=(vm, vm, vm, vm, hbm, vm, hbm, hbm, hbm),
+        scratch_shapes=[
+            pltpu.VMEM((pairs, 4, part, 384), BF16),
+            pltpu.VMEM((pairs, 8, 384), F32),
+            pltpu.VMEM((count, units, 3 * HD, lanes), BF16),
+            pltpu.VMEM((count, units, HD, lanes), BF16),
+            pltpu.VMEM((count, units, HD, lanes), BF16),
+            pltpu.VMEM((length, HD), BF16),
+            pltpu.VMEM((HD, length), BF16),
+            pltpu.VMEM((length, lanes), jnp.int32),
+            pltpu.VMEM(mixer.shape, BF16),
+            pltpu.VMEM(inner.shape, BF16),
+            pltpu.VMEM(outer.shape, BF16),
+            dma((count, units)),
+            dma((count, units)),
+            dma((count, units)),
+            dma((count, units)),
+            dma((2, 3, pairs, 3)),
+            dma((2, 4, 4)),
+            dma((3, max(pairs, units, 4), 3)),
+        ],
+        compiler_params=pltpu.CompilerParams(
+            collective_id=number, has_side_effects=True, vmem_limit_bytes=56 * 1024 * 1024
+        ),
+        name="forward",
+    )(starts, tokens, docs, joint, vectors, mixer, inner, outer)
 
 
 def first_rows(half, tile):
@@ -603,8 +988,8 @@
     units = -(-MB * H // count)
     me = lax.axis_index("ctx")
 
-    joint = lax.all_gather(joint_weight, "fsdp", axis=0, tiled=True)
-    vectors = jnp.concatenate(
+    part = D // shards
+    vectors = jnp.stack(
         [
             query_bias,
             value_bias,
@@ -614,31 +999,38 @@
             outer_bias,
             second_gain,
             second_shift,
-            inner_bias,
         ]
     )
-    vectors = lax.all_gather(vectors, "fsdp", axis=0)
-    part = D // shards
-    names = [vectors[:, i * part : (i + 1) * part].reshape(D).astype(F32) for i in range(8)]
-    qbias, vbias, mbias, gain_one, shift_one, obias, gain_two, shift_two = names
-    ibias = vectors[:, 8 * part :].reshape(FF).astype(F32)
-    mixer = lax.all_gather(mixer_weight, "fsdp", axis=0, tiled=True)
-    inner = lax.all_gather(inner_weight, "fsdp", axis=0, tiled=True)
-    outer = lax.all_gather(outer_weight, "fsdp", axis=0, tiled=True)
-
+    vectors = jnp.pad(vectors, ((0, 8), (0, D - part)))
+    vectors = vectors.at[8].set(inner_bias)
     source = tokens.reshape(MB * rows, D)
     unit_ids = jnp.arange(units, dtype=jnp.int32) * count + me
-    unit_starts = doc_starts[:, 0][jnp.minimum(unit_ids // H, MB - 1)]
+    unit_starts = doc_starts[:, 0][lax.rem(unit_ids, MB)]
     positions = jnp.arange(length, dtype=jnp.int32)
     unit_docs = jax.vmap(lambda s: doc_index(positions, s))(unit_starts)[:, None, :]
 
-    joint_bias = jnp.concatenate([qbias, jnp.zeros((D,), F32), vbias])
-    projected = (mul_tt(joint, source) + joint_bias[:, None]).astype(BF16)
-    received = exchange(to_units(projected, 3, count, units), 0)
-    mixed, wide, lse = attend(received, unit_starts, unit_docs)
-    attended = from_units(exchange(mixed, 1), 1)
-
-    branch = mul_tn(attended, mixer) + mbias
+    attended, received, wide, lse, joint, vectors, mixer, inner, outer = forward(
+        count,
+        unit_starts,
+        source,
+        unit_docs,
+        joint_weight,
+        vectors,
+        mixer_weight,
+        inner_weight,
+        outer_weight,
+        0,
+    )
+    joint = joint.reshape(D, 3 * D)
+    mixer, inner, outer = mixer.reshape(D, D), inner.reshape(D, FF), outer.reshape(FF, D)
+    heads_of = [
+        vectors[:, i, :part].reshape(D).astype(F32)
+        for i in range(8)
+    ]
+    _, _, mbias, gain_one, shift_one, obias, gain_two, shift_two = heads_of
+    ibias = vectors[:, 8].reshape(FF).astype(F32)
+
+    branch = mul_nn(attended, mixer) + mbias
     first, first_normed, first_recip = norm_forward(
         source.astype(F32) + branch, gain_one, shift_one
     )
@@ -666,7 +1058,7 @@
     d_residual = norm_backward(d_first, first_normed, first_recip, gain_one)
     d_branch = d_residual.astype(BF16)
     mixing_grad = jnp.sum(d_branch.astype(F32), axis=0)
-    mixer_grad = mul_tt(d_branch, attended)
+    mixer_grad = mul_tn(d_branch, attended)
     flow = mul_nt(mixer, d_branch).astype(BF16)
     flow_units = exchange(to_units(flow, 1, count, units), 2)
     d_units = attend_back(received, flow_units, unit_starts, unit_docs, wide, lse)

time: 433 us -> 401 us (0.926)
  waiting for transfers between devices: 26.7 us -> 0 us
  between operations: 14.3 us -> 0.98 us
  Pallas kernels: 274 us -> 286 us
  blocking collectives: 6.2 us -> 0 us
  other arithmetic: 16.6 us -> 21.5 us
    pallas_call x1, Pallas kernels: 22.8 us -> 98 us  [forward(): pl.pallas_call(functools.partial(forward_kernel, width), out_shape=(jax.S...]
    pallas_call x4 -> x2, Pallas kernels: 116 us -> 53.3 us  [exchange(): pl.pallas_call(functools.partial(exchange_kernel, count), out_shape=jax.S...]
    all_gather x4 -> x0, waiting for transfers between devices: 24.1 us -> none  [the longest x1 24 us: on_device(): joint = lax.all_gather(joint_weight, 'fsdp', axis=0, tiled=True)]
    dot_general x3 -> x1, matrix products: 11.9 us -> 4.6 us  [mul_tt(): lax.dot_general(a, b, (((0,), (1,)), ((), ())), preferred_element_type=F32)]
    all_gather x1 -> x0, blocking collectives: 6.2 us -> none  [on_device(): vectors = lax.all_gather(vectors, 'fsdp', axis=0)]
    another operation x0 -> x10, local copies, waits for them, and re-layouts: none -> 5.98 us  [the longest x9 5.29 us: on_device(): jnp.stack([query_bias, value_bias, mixer_bias, first_gain, first_shift, o...]
    reshape x4 -> x2, local copies, waits for them, and re-layouts: 7.01 us -> 1.89 us  [the longest x1 1.68 us: from_units(): x = x.reshape(H, MB, parts, HD, rows).transpose(2, 0, 3, 1, 4)]
    dot_general x3 -> x4, matrix products: 17.1 us -> 18 us  [mul_nn(): return jnp.dot(a, b, preferred_element_type=F32)]
  transfers between devices with their start and end apart: 4 -> 0, of which waited for: 1 -> 0; matrix products, arithmetic and copies ran while one was open for 6% -> 0% of each run, Pallas kernels for 20% -> 0%
where the time goes in v3:
time: 401 us; the launch traced here: 400 us
  Pallas kernels  286 us (71%)
  matrix products  46.4 us (12%)
  local copies, waits for them, and re-layouts  44.7 us (11%)
  other arithmetic  21.5 us (5%)
    pallas_call x1, Pallas kernels, reduce_all(): pl.pallas_call(functools.partial(reduce_kernel, count, tuple(heads)), out...  110 us
    pallas_call x1, Pallas kernels, forward(): pl.pallas_call(functools.partial(forward_kernel, width), out_shape=(jax.S...  98 us
    pallas_call x2, Pallas kernels, exchange(): pl.pallas_call(functools.partial(exchange_kernel, count), out_shape=jax.S...  53.3 us
    pallas_call x1, Pallas kernels, attend_back(): pl.pallas_call(functools.partial(attend_back_kernel, width), out_shape=ja...  25.3 us
    dot_general x4, matrix products, mul_nn(): return jnp.dot(a, b, preferred_element_type=F32)  18 us
    dot_general x3, matrix products, mul_tn(): lax.dot_general(a, b, (((0,), (0,)), ((), ())), preferred_element_type=F32)  13.3 us
    concatenate x10, local copies, waits for them, and re-layouts, on_device(): packed = jnp.concatenate([v.reshape(world, -1) for v in small], axis=1)  12.1 us
    dot_general x3, matrix products, mul_nt(): lax.dot_general(a, b, (((1,), (1,)), ((), ())), preferred_element_type=F32)  10.4 us

profile of v3, /device:TPU:0, one launch (start us, length us, event | category | flops | bytes accessed | tf_op | source)
XLA Modules:
  0.0 399.8 jit_solution(9827072475594929076)
XLA Ops:
  0.7 0.7 copy.86
  2.7 0.7 stack.27
  3.4 0.7 stack.28
  4.0 0.7 stack.29
  4.7 0.7 stack.30
  5.3 0.7 stack.31
  6.0 0.7 stack.32
  6.6 0.7 stack.33
  7.3 0.7 stack.34
  8.0 0.7 reshape.298
  9.4 98.0 %forward.1 = (bf16[384,768]{1,0:T(8,128)(2,1)}, bf16[8,5,192,128]{3,2,1,0:T(8,128)(2,1)}, f32[5,64,1024]{2,1,0:T(8,128)}, f32[5,1,1024]{2,1,0:T(1,128)}, bf16[4,...) custom-call(s32[5,8]{1,0:T(8,128)} %copy-done.10, ...), custom_call_target="tpu_custom_call" | custom-call | tf_op jit(solution)/shard_map/forward/pallas_call | solution.py:713
  107.4 1.7 convert_reduce_fusion.7
  109.2 2.2 fusion.33
  111.8 0.8 slice_convert_fusion
  112.6 6.9 %multiply_convert_fusion = (bf16[384,3072]{1,0:T(8,128)(2,1)}, f32[384,3072]{1,0:T(8,128)}) fusion(f32[3072]{0:T(1024)S(1)} %bitcast.136, bf16[768,3072]{1,0:T(8,128)(2,1)} %bitcast.137, f32[384,768]{1,0:T(8,128)S(1)} %get-tuple-element.145, f32[768]{0:T(1024)S(1)} %reshape.319, f32[768]{0:T(1024)S(1)} %reshape.318, f32[384]{0:T(512)S(1)} %add_rsqrt_fusion.1, ...), kind=kOutput, calls=%fused_computation.13 | convolution fusion | flops 1820491776 | bytes 12997632 | tf_op jit(solution)/shard_map/dot_general | solution.py:263
  119.6 5.2 %fusion.34 = (f32[384]{0:T(512)S(1)}, f32[384,768]{1,0:T(8,128)S(1)}) fusion(f32[768]{0:T(1024)S(1)} %reshape.321, bf16[384,3072]{1,0:T(8,128)(2,1)} %get-tuple-element.146, bf16[3072,768]{1,0:T(8,128)(2,1)} %bitcast.141, f32[768]{0:T(1024)S(1)} %reshape.319, f32[768]{0:T(1024)S(1)} %reshape.318, f32[384]{0:T(512)S(1)} %add_rsqrt_fusion.1, ...), kind=kOutput, calls=%fused_computation.99 | convolution fusion | flops 1814003328 | bytes 9451008 | tf_op jit(solution)/shard_map/dot_general | solution.py:263
  125.0 0.8 reshape.322
  125.8 1.1 fusion.22
  127.5 0.8 convert_reduce_fusion.2
  128.8 1.4 reshape.323
  130.2 2.8 convert_reduce_fusion.3
  132.9 6.7 %convert_reduce_fusion = (f32[3072]{0:T(1024)}, bf16[384,3072]{1,0:T(8,128)(2,1)S(1)}) fusion(f32[384,3072]{1,0:T(8,128)} %get-tuple-element.147, bf16[3072,768]{1,0:T(8,128)(2,1)} %bitcast.142, f32[384,768]{1,0:T(8,128)S(1)} %get-tuple-element.130), kind=kOutput, calls=%fused_computation.11 | convolution fusion | flops 1826386944 | bytes 12988416 | tf_op jit(solution)/shard_map/dot_general | solution.py:271
  139.7 2.9 multiply_reduce_fusion
  142.6 1.0 convert_reduce_fusion.4
  143.9 0.8 convolution_convert_fusion.4
  145.1 0.9 copy.85
  146.0 15.4 %exchange_2.1.flow_ref = bf16[8,5,64,128]{3,2,1,0:T(8,128)(2,1)} custom-call(bf16[8,5,64,128]{3,2,1,0:T(8,128)(2,1)} %bitcast.119), custom_call_target="tpu_custom_call" | custom-call | tf_op jit(solution)/shard_map/exchange_2/pallas_call | solution.py:96
  161.5 25.3 %attend_back.1.x_ref = bf16[8,5,192,128]{3,2,1,0:T(8,128)(2,1)} custom-call(s32[5,8]{1,0:T(8,128)} %copy-done.10, bf16[8,5,192,128]{3,2,1,0:T(8,128)(2,1)} %get-tuple-element.46.x_ref, bf16[8,5,64,128]{3,2,1,0:T(8,128)(2,1)} %exchange_2.1.flow_ref, s32[5,1,1024]{2,1,0:T(1,128)} %sub.45.docs_ref, f32[5,64,1024]{2,1,0:T(8,128)} %get-tuple-element.47.wide_ref, ...), custom_call_target="tpu_custom_call" | custom-call | tf_op jit(solution)/shard_map/attend_back/pallas_call | solution.py:219
  186.8 37.8 %exchange_3.1 = bf16[8,5,192,128]{3,2,1,0:T(8,128)(2,1)} custom-call(bf16[8,5,192,128]{3,2,1,0:T(8,128)(2,1)} %attend_back.1.x_ref), custom_call_target="tpu_custom_call" | custom-call | tf_op jit(solution)/shard_map/exchange_3/pallas_call | solution.py:96
  224.6 1.7 copy.58
  226.4 5.1 %convert_reduce_fusion.1 = f32[3,12,64]{2,1,0:T(8,128)S(1)} fusion(bf16[12,3,3,64,128]{4,3,2,1,0:T(8,128)(2,1)S(1)} %bitcast.109), kind=kLoop, calls=%fused_computation.12 | loop fusion | flops 1767168 | bytes 1778688 | tf_op jit(solution)/shard_map/reduce_sum | solution.py:1066
  231.6 0.7 concatenate.24
  232.3 0.7 concatenate.25
  233.0 0.8 concatenate.26
  233.8 1.4 concatenate.27
  235.1 1.4 concatenate.28
  236.5 1.4 concatenate.29
  237.9 1.4 concatenate.30
  239.2 1.4 concatenate.31
  240.6 1.4 concatenate.32
  242.0 1.7 concatenate.33
  243.7 0.8 copy.71
  244.5 0.6 pad.20.clone
  245.2 1.5 reshape.311
  246.6 0.8 copy.72
  247.5 0.8 pad.21.clone
  248.3 7.1 %convolution_convert_fusion.1 = bf16[3072,768]{1,0:T(8,128)(2,1)} fusion(bf16[384,3072]{1,0:T(8,128)(2,1)} %copy-done.18, f32[384,768]{1,0:T(8,128)} %copy-done.1, f32[768]{0:T(1024)} %copy-done.16, f32[768]{0:T(1024)} %copy-done.12, f32[384]{0:T(512)} %copy-done.14, f32[384]{0:T(512)} %copy-done.11), kind=kOutput, calls=%fused_computation.3 | convolution fusion | flops 1815773184 | bytes 8266752 | tf_op jit(solution)/shard_map/dot_general | solution.py:267
  255.4 4.4 %convolution_convert_fusion.2 = bf16[768,3072]{1,0:T(8,128)(2,1)} fusion(bf16[384,3072]{1,0:T(8,128)(2,1)S(1)} %copy-done.17, f32[384,768]{1,0:T(8,128)S(1)} %copy-done.5), kind=kOutput, calls=%fused_computation.4 | convolution fusion | flops 1814593536 | bytes 8257536 | tf_op jit(solution)/shard_map/dot_general | solution.py:267
  259.8 1.8 convolution_convert_fusion.3
  261.6 1.7 copy.59
  263.3 3.8 convolution_convert_fusion
  267.1 109.6 %reduce_all.1 = (bf16[2,48,1536]{2,1,0:T(8,128)(2,1)}, bf16[2,192,384]{2,1,0:T(8,128)(2,1)}, bf16[2,48,384]{2,1,0:T(8,128)(2,1)}, bf16[2,144,384]{2,1,0:T(8,128)(2,1)}, f32[2,8,384]{2,1,0:T(8,128)}) custom-call(bf16[4,2,2,48,3072]{4,3,2,1,0:T(8,128)(2,1)} %bitcast.114, bf16[4,2,2,192,768]{4,3,2,1,0:T(8,128)(2,1)} %bitcast.113, ...), custom_call_target="tpu_custom_call" | custom-call | tf_op jit(solution)/shard_map/reduce_all/pallas_call | solution.py:953
  376.7 1.8 constant_dynamic-slice_fusion
  378.5 1.9 copy.70
  380.4 1.6 convert_bitcast_fusion.1
  382.0 1.7 constant_dynamic-slice_fusion.2
  383.7 1.7 copy.68
  385.4 1.6 convert_bitcast_fusion.2
  387.1 1.6 convert_bitcast_fusion
  388.7 1.6 constant_dynamic-slice_fusion.1
  390.3 1.5 copy.69
  391.8 1.4 convert_bitcast_fusion.3
  393.3 0.7 dynamic-slice_bitcast_fusion
  395.2 4.6 %fusion.10 = f32[384,768]{1,0:T(8,128)} fusion(f32[384,768]{1,0:T(8,128)S(1)} %get-tuple-element.132, bf16[768,2304]{1,0:T(8,128)(2,1)} %bitcast.143, bf16[288,8,3,128]{3,2,1,0:T(4,128)(2,1)S(1)} %bitcast.121), kind=kOutput, calls=%fused_computation.24 | convolution fusion | flops 1359249408 | bytes 7667712 | tf_op jit(solution)/shard_map/dot_general | solution.py:275
  (72 shorter events, 6.1 us)
Async XLA Ops:
  1.9 6.8 %copy-start.10 = (s32[5,8]{1,0:T(8,128)}, s32[5,8]{1,0:T(8,128)S(1)}, u32[]{:S(2)}) copy-start(s32[5,8]{1,0:T(8,128)S(1)} %gather_fusion) | copy-start | bytes 484
  8.7 0.6 copy-start.9
  9.3 99.8 %copy-start.7 = (bf16[3,1,128,768]{3,2,1,0:T(8,128)(2,1)S(1)}, bf16[3,1,128,768]{3,2,1,0:T(8,128)(2,1)}, u32[]{:S(2)}) copy-start(bf16[3,1,128,768]{3,2,1,0:T(8,128)(2,1)} %param.18) | copy-start | bytes 1769476
  111.3 31.3 %copy-start.1 = (f32[384,768]{1,0:T(8,128)}, f32[384,768]{1,0:T(8,128)S(1)}, u32[]{:S(2)}) copy-start(f32[384,768]{1,0:T(8,128)S(1)} %get-tuple-element.145) | copy-start | bytes 3538948
  111.3 31.3 %copy-start.11 = (f32[384]{0:T(512)}, f32[384]{0:T(512)S(1)}, u32[]{:S(2)}) copy-start(f32[384]{0:T(512)S(1)} %broadcast_multiply_fusion.4) | copy-start | bytes 4612
  111.6 8.0 %copy-start.14 = (f32[384]{0:T(512)}, f32[384]{0:T(512)S(1)}, u32[]{:S(2)}) copy-start(f32[384]{0:T(512)S(1)} %add_rsqrt_fusion.1) | copy-start | bytes 4612
  111.7 7.9 %copy-start.12 = (f32[768]{0:T(1024)}, f32[768]{0:T(1024)S(1)}, u32[]{:S(2)}) copy-start(f32[768]{0:T(1024)S(1)} %reshape.318) | copy-start | bytes 9220
  111.8 7.8 %copy-start.16 = (f32[768]{0:T(1024)}, f32[768]{0:T(1024)S(1)}, u32[]{:S(2)}) copy-start(f32[768]{0:T(1024)S(1)} %reshape.319) | copy-start | bytes 9220
  124.7 1.1 copy-start
  130.2 9.5 %slice-start = ((s8[4718592]{0:T(1024)(128)(4,1)}), s8[4194304]{0:T(1024)(128)(4,1)S(1)}, s32[]{:S(2)}) async-start(s8[4718592]{0:T(1024)(128)(4,1)} %bitcast.138), calls=%async_computation | async-start | bytes 8388608
  132.9 6.7 %copy-start.4 = (f32[384,768]{1,0:T(8,128)}, f32[384,768]{1,0:T(8,128)S(1)}, u32[]{:S(2)}) copy-start(f32[384,768]{1,0:T(8,128)S(1)} %get-tuple-element.130) | copy-start | bytes 3538948
  132.9 6.7 %copy-start.13 = (f32[768]{0:T(1024)S(1)}, f32[768]{0:T(1024)}, u32[]{:S(2)}) copy-start(f32[768]{0:T(1024)} %copy-done.12) | copy-start | bytes 9220
  132.9 6.7 %copy-start.15 = (f32[384]{0:T(512)S(1)}, f32[384]{0:T(512)}, u32[]{:S(2)}) copy-start(f32[384]{0:T(512)} %copy-done.14) | copy-start | bytes 4612
  132.9 6.7 %slice-start.1 = ((s8[4718592]{0:T(1024)(128)(4,1)}), s8[524288]{0:T(1024)(128)(4,1)S(1)}, s32[]{:S(2)}) async-start(s8[4718592]{0:T(1024)(128)(4,1)} %bitcast.138), calls=%async_computation.1 | async-start | bytes 1048576
  139.6 3.0 copy-start.18
  142.6 1.3 copy-start.6
  248.3 7.1 %copy-start.5 = (f32[384,768]{1,0:T(8,128)S(1)}, f32[384,768]{1,0:T(8,128)}, u32[]{:S(2)}) copy-start(f32[384,768]{1,0:T(8,128)} %copy-done.4) | copy-start | bytes 3538948
  248.3 7.1 %copy-start.17 = (bf16[384,3072]{1,0:T(8,128)(2,1)S(1)}, bf16[384,3072]{1,0:T(8,128)(2,1)}, u32[]{:S(2)}) copy-start(bf16[384,3072]{1,0:T(8,128)(2,1)} %get-tuple-element.146) | copy-start | bytes 7077892
  255.4 4.4 %copy-start.8 = (bf16[384,768]{1,0:T(8,128)(2,1)S(1)}, bf16[384,768]{1,0:T(8,128)(2,1)}, u32[]{:S(2)}) copy-start(bf16[384,768]{1,0:T(8,128)(2,1)} %get-tuple-element.41) | copy-start | bytes 1769476
  263.3 3.8 copy-start.2
  378.5 16.6 %copy-start.3 = (bf16[12,3,3,64,128]{4,1,3,0,2:T(4,128)(2,1)S(1)}, bf16[12,3,3,64,128]{4,1,3,0,2:T(4,128)(2,1)}, u32[]{:S(2)}) copy-start(bf16[12,3,3,64,128]{4,1,3,0,2:T(4,128)(2,1)} %copy-done.2) | copy-start | bytes 5308420

commit v4 on v3

--- a/solution.py
+++ b/solution.py
@@ -373,12 +373,9 @@
     def joint_pass(pair, third):
         return joint_copy(2, pair, third, far, other_core)
 
-    def joint_store(pair, third):
-        columns = pl.ds(pl.multiple_of(third * D + pair * 128, 128), 128)
+    def joint_store(pair):
         return pltpu.make_async_copy(
-            joint_all.at[pair, :, :, pl.ds(third * 128, 128)],
-            joint_out.at[:, :, columns],
-            own_sems.at[0, pair, third],
+            joint_all.at[pair], joint_out.at[pair], own_sems.at[0, pair, 0]
         )
 
     def each_third(pair, make, act):
@@ -485,7 +482,7 @@
         each_third(pair, joint_pass, "start")
         each_third(pair, joint_core, "wait_recv")
         each_third(pair, joint_pass, "wait_recv")
-        each_third(pair, joint_store, "start")
+        joint_store(pair).start()
         weight = joint_all[pair].reshape(4 * part, 384)
         rows = jnp.dot(tok_ref[...], weight, preferred_element_type=F32)
         rows = (rows + bias_rows[pair, 0:1, :]).astype(BF16)
@@ -697,7 +694,8 @@
         return carry
 
     lax.fori_loop(0, mine, returned, 0)
-    every_pair(joint_store, "wait")
+    for pair in range(pairs):
+        joint_store(pair).wait()
 
 
 def forward(count, starts, tokens, docs, joint, vectors, mixer, inner, outer, number):
@@ -717,7 +715,7 @@
             jax.ShapeDtypeStruct((count, units, 3 * HD, lanes), BF16),
             jax.ShapeDtypeStruct((units, HD, length), F32),
             jax.ShapeDtypeStruct((units, 1, length), F32),
-            jax.ShapeDtypeStruct((4, *joint.shape), BF16),
+            jax.ShapeDtypeStruct((pairs, 4, part, 384), BF16),
             jax.ShapeDtypeStruct((4, *vectors.shape), BF16),
             jax.ShapeDtypeStruct((4, *mixer.shape), BF16),
             jax.ShapeDtypeStruct((4, *inner.shape), BF16),
@@ -752,215 +750,606 @@
     )(starts, tokens, docs, joint, vectors, mixer, inner, outer)
 
 
+JOINT_JOB = 3
+BIAS_ROWS = 16
+
+
 def first_rows(half, tile):
     return half if half <= tile else (half // tile + 1) // 2 * tile
 
 
-def reduce_kernel(count, heads, *refs):
-    jobs = len(heads)
-    grads, outs, scratch = refs[:jobs], refs[jobs : 2 * jobs], refs[2 * jobs :]
-    sets = [scratch[7 * j : 7 * j + 7] for j in range(jobs)]
-    load_sem, send_sem, recv_sem, z_send, z_recv = scratch[7 * jobs :]
-    me, shard = lax.axis_index("ctx"), lax.axis_index("fsdp")
-    depth = count // 2
-    y, core = shard // 2, lax.rem(shard, 2)
-    z, x = me // 2, lax.rem(me, 2)
-    other_core = {"fsdp": 2 * y + 1 - core}
-    other_y = {"fsdp": 2 * (1 - y) + core}
-    other_x = {"ctx": 2 * z + 1 - x}
-
-    def along_z(step):
-        return lax.rem(z + step, depth)
-
-    barrier = pltpu.get_barrier_semaphore()
-    for peer in (other_core, other_y, other_x):
-        pl.semaphore_signal(barrier, inc=1, device_id=peer)
-    for step in range(1, depth):
-        pl.semaphore_signal(barrier, inc=1, device_id={"ctx": 2 * along_z(step) + x})
-
-    def remote(src, dst, j, slot, peer):
-        return pltpu.make_async_remote_copy(
-            src_ref=src,
-            dst_ref=dst,
-            send_sem=send_sem.at[j, slot],
-            recv_sem=recv_sem.at[j, slot],
-            device_id=peer,
-        )
-
-    def plan(j):
-        own, got, y_one, x_one, x_two, y_two, z_got = sets[j]
+class Place:
+    def __init__(self, count):
+        self.count = count
+        self.depth = count // 2
+        self.me, self.shard = lax.axis_index("ctx"), lax.axis_index("fsdp")
+        self.y, self.core = self.shard // 2, lax.rem(self.shard, 2)
+        self.z, self.x = self.me // 2, lax.rem(self.me, 2)
+        self.other_core = {"fsdp": 2 * self.y + 1 - self.core}
+        self.other_y = {"fsdp": 2 * (1 - self.y) + self.core}
+        self.other_x = {"ctx": 2 * self.z + 1 - self.x}
+
+    def along_z(self, step):
+        return lax.rem(self.z + step, self.depth)
+
+    def peer_z(self, step):
+        return {"ctx": 2 * self.along_z(step) + self.x}
+
+
+def start(copies):
+    for copy in copies:
+        copy.start()
+
+
+def added(a, b):
+    return (a.astype(F32) + b.astype(F32)).astype(a.dtype)
+
+
+class Reduction:
+    def __init__(self, place, j, grad, out, head, buffers, load_sem, sems, z_sems):
+        own, got, y_one, x_one, x_two, y_two, z_got = buffers
+        self.place, self.out, self.head, self.own, self.buffers = place, out, head, own, buffers
         half, lanes = own.shape[3], own.shape[4]
-        head = heads[j]
-        tail = head < half
-        loads, firsts = [], []
+        self.half = half
+        p = place
+
+        def remote(src, dst, slot, peer):
+            return pltpu.make_async_remote_copy(
+                src_ref=src,
+                dst_ref=dst,
+                send_sem=sems.at[0, j, slot],
+                recv_sem=sems.at[1, j, slot],
+                device_id=peer,
+            )
+
+        self.loads, self.firsts = [], []
         for side in range(2):
             columns = pl.ds(side * lanes, lanes)
             for low in range(2):
-                loads.append(
+                slot = 2 * side + low
+                self.loads.append(
                     pltpu.make_async_copy(
-                        grads[j].at[:, low, core, :, columns],
+                        grad.at[:, low, p.core, :, columns],
                         own.at[side, :, low],
-                        load_sem.at[j, 2 * side + low],
+                        load_sem.at[j, slot],
                     )
                 )
-            for low in range(2):
-                firsts.append(
+                self.firsts.append(
                     remote(
-                        grads[j].at[:, low, 1 - core, :, columns],
+                        grad.at[:, low, 1 - p.core, :, columns],
                         got.at[side, :, low],
-                        j,
-                        2 * side + low,
-                        other_core,
+                        slot,
+                        p.other_core,
                     )
                 )
-        second = [remote(own.at[1 - y, :, :, 0:head, :], y_one, j, 4, other_y)]
-        third = [remote(own.at[y, :, 1 - x, 0:head, :], x_two, j, 5, other_x)]
-        if tail:
-            second.append(remote(own.at[:, :, 1 - x, head:half, :], x_one, j, 6, other_x))
-            third.append(remote(own.at[1 - y, :, x, head:half, :], y_two, j, 7, other_y))
-        fourth = [
+        self.second = [remote(own.at[1 - p.y, :, :, 0:head, :], y_one, 4, p.other_y)]
+        self.third = [remote(own.at[p.y, :, 1 - p.x, 0:head, :], x_two, 5, p.other_x)]
+        if head < half:
+            self.second.append(remote(own.at[:, :, 1 - p.x, head:half, :], x_one, 6, p.other_x))
+            self.third.append(remote(own.at[1 - p.y, :, p.x, head:half, :], y_two, 7, p.other_y))
+        self.fourth = [
             pltpu.make_async_remote_copy(
-                src_ref=own.at[y, along_z(step), x],
-                dst_ref=z_got.at[z],
-                send_sem=z_send.at[j, step],
-                recv_sem=z_recv.at[j, step],
-                device_id={"ctx": 2 * along_z(step) + x},
+                src_ref=own.at[p.y, p.along_z(step), p.x],
+                dst_ref=z_got.at[p.z],
+                send_sem=z_sems.at[0, j, step],
+                recv_sem=z_sems.at[1, j, step],
+                device_id=p.peer_z(step),
             )
-            for step in range(1, depth)
+            for step in range(1, p.depth)
         ]
-        last = [remote(outs[j].at[core], outs[j].at[core], j, 8, other_core)]
-        return (loads, firsts, second, third, fourth, last)
-
-    plans = [plan(j) for j in range(jobs)]
-
-    def add(a, b):
-        return (a.astype(F32) + b.astype(F32)).astype(a.dtype)
-
-    def start(copies):
-        for copy in copies:
-            copy.start()
-
-    def stage_one(j):
-        own, got = sets[j][0], sets[j][1]
-        for copy in plans[j][0]:
+        self.last = [remote(out.at[p.core], out.at[p.core], 8, p.other_core)]
+
+    def stage_zero(self):
+        start(self.loads)
+        start(self.firsts)
+
+    def stage_one(self):
+        own, got = self.own, self.buffers[1]
+        for copy in self.loads:
             copy.wait()
-        for copy in plans[j][1]:
+        for copy in self.firsts:
             copy.wait_recv()
 
         def body(block, carry):
             for side in range(2):
                 for low in range(2):
-                    own[side, block, low] = add(own[side, block, low], got[side, block, low])
+                    own[side, block, low] = added(own[side, block, low], got[side, block, low])
             return carry
 
-        lax.fori_loop(0, depth, body, 0)
-        start(plans[j][2])
-
-    def stage_two(j):
-        own, _, y_one, x_one, _, _, _ = sets[j]
-        half, head = own.shape[3], heads[j]
-        for copy in plans[j][2]:
+        lax.fori_loop(0, self.place.depth, body, 0)
+        start(self.second)
+
+    def stage_two(self):
+        p, own, head, half = self.place, self.own, self.head, self.half
+        y_one, x_one = self.buffers[2], self.buffers[3]
+        for copy in self.second:
             copy.wait()
 
         def body(block, carry):
             for low in range(2):
-                own[y, block, low, 0:head, :] = add(
-                    own[y, block, low, 0:head, :], y_one[block, low]
+                own[p.y, block, low, 0:head, :] = added(
+                    own[p.y, block, low, 0:head, :], y_one[block, low]
                 )
             if head < half:
                 for side in range(2):
-                    own[side, block, x, head:half, :] = add(
-                        own[side, block, x, head:half, :], x_one[side, block]
+                    own[side, block, p.x, head:half, :] = added(
+                        own[side, block, p.x, head:half, :], x_one[side, block]
                     )
             return carry
 
-        lax.fori_loop(0, depth, body, 0)
-        start(plans[j][3])
-
-    def stage_three(j):
-        own, _, _, _, x_two, y_two, _ = sets[j]
-        half, head = own.shape[3], heads[j]
-        for copy in plans[j][3]:
+        lax.fori_loop(0, p.depth, body, 0)
+        start(self.third)
+
+    def stage_three(self):
+        p, own, head, half = self.place, self.own, self.head, self.half
+        x_two, y_two = self.buffers[4], self.buffers[5]
+        for copy in self.third:
             copy.wait()
 
         def body(block, carry):
-            own[y, block, x, 0:head, :] = add(own[y, block, x, 0:head, :], x_two[block])
+            own[p.y, block, p.x, 0:head, :] = added(
+                own[p.y, block, p.x, 0:head, :], x_two[block]
+            )
             if head < half:
-                own[y, block, x, head:half, :] = add(
-                    own[y, block, x, head:half, :], y_two[block]
+                own[p.y, block, p.x, head:half, :] = added(
+                    own[p.y, block, p.x, head:half, :], y_two[block]
                 )
             return carry
 
-        lax.fori_loop(0, depth, body, 0)
-        start(plans[j][4])
-
-    def stage_four(j):
-        own, z_got = sets[j][0], sets[j][6]
-        for copy in plans[j][4]:
+        lax.fori_loop(0, p.depth, body, 0)
+        start(self.fourth)
+
+    def stage_four(self):
+        p, z_got = self.place, self.buffers[6]
+        for copy in self.fourth:
             copy.wait()
-        total = own[y, z, x].astype(F32)
-        for step in range(1, depth):
-            total = total + z_got[along_z(step)].astype(F32)
-        outs[j][core] = total.astype(outs[j].dtype)
-        start(plans[j][5])
-
-    def stage_five(j):
-        for copy in plans[j][5]:
+        total = self.own[p.y, p.z, p.x].astype(F32)
+        for step in range(1, p.depth):
+            total = total + z_got[p.along_z(step)].astype(F32)
+        self.out[p.core] = total.astype(self.out.dtype)
+        start(self.last)
+
+    def stage_five(self):
+        for copy in self.last:
             copy.wait()
-        for copy in plans[j][1]:
+        for copy in self.firsts:
             copy.wait_send()
 
-    for j in range(jobs):
-        start(plans[j][0])
-    pl.semaphore_wait(barrier, 2 + depth)
-    for j in range(jobs):
-        start(plans[j][1])
-    stages = (stage_one, stage_two, stage_three, stage_four, stage_five)
-    for tick in range(jobs + len(stages) - 1):
-        for k in reversed(range(len(stages))):
-            if 0 <= tick - k < jobs:
-                stages[k](tick - k)
-
-
-def reduce_all(grads, number):
-    count = grads[0].shape[0]
+
+def reduction_buffers(count, half, lanes, dtype):
     depth = count // 2
-    heads, scratch, outs = [], [], []
-    for g in grads:
-        half, lanes = g.shape[2], g.shape[3] // 2
-        head = first_rows(half, 16 if g.dtype == BF16 else 8)
-        tail = max(half - head, 16 if g.dtype == BF16 else 8)
+    head = first_rows(half, 16)
+    tail = max(half - head, 16)
+    shapes = (
+        (2, depth, 2, half, lanes),
+        (2, depth, 2, half, lanes),
+        (depth, 2, head, lanes),
+        (2, depth, tail, lanes),
+        (depth, head, lanes),
+        (depth, tail, lanes),
+        (depth, half, lanes),
+        (2, half, lanes),
+    )
+    return head, [pltpu.VMEM(shape, dtype) for shape in shapes]
+
+
+def backward_kernel(width, heads, *refs):
+    (
+        starts_ref,
+        flow_ref,
+        docs_ref,
+        got_ref,
+        wide_ref,
+        lse_ref,
+        tok_ref,
+        residual_ref,
+        bias_ref,
+        joint_ref,
+        outer_grad,
+        inner_grad,
+        mixer_grad,
+        tokens_out,
+        outer_out,
+        inner_out,
+        mixer_out,
+        joint_out,
+        bias_out,
+        flow_put,
+        flow_got,
+        put,
+        home_got,
+        key_rows,
+        value_rows,
+        key_t,
+        key_docs,
+        d_key,
+        d_value,
+        joint_all,
+        joint_grad,
+        d_turned,
+        bias_sum,
+        bias_got,
+        bias_z,
+        flow_sems,
+        home_sems,
+        own_sems,
+        load_sem,
+        sems,
+        z_sems,
+        bias_sems,
+        *buffers,
+    ) = refs
+    count, units, _, lanes = got_ref.shape
+    length = count * lanes
+    depth = min(length, 1024)
+    group = width // lanes
+    pairs = H // 2
+    total_units = MB * H
+    p = Place(count)
+    me = p.me
+    mine = (total_units - me + count - 1) // count
+
+    barrier = pltpu.get_barrier_semaphore()
+
+    def greet(step, carry):
+        pl.semaphore_signal(barrier, inc=1, device_id={"ctx": lax.rem(me + step, count)})
+        return carry
+
+    lax.fori_loop(1, count, greet, 0)
+    pl.semaphore_signal(barrier, inc=1, device_id=p.other_core)
+    pl.semaphore_signal(barrier, inc=1, device_id=p.other_y)
+    joint_load = pltpu.make_async_copy(joint_ref, joint_all, own_sems.at[2, 0])
+    joint_load.start()
+
+    grads = (outer_grad, inner_grad, mixer_grad, joint_grad)
+    outs = (outer_out, inner_out, mixer_out, joint_out)
+    jobs = [
+        Reduction(
+            p,
+            j,
+            grads[j],
+            buffers[8 * j + 7],
+            heads[j],
+            buffers[8 * j : 8 * j + 7],
+            load_sem,
+            sems,
+            z_sems,
+        )
+        for j in range(4)
+    ]
+    outer_job, inner_job, mixer_job, joint_job = jobs
+
+    pl.semaphore_wait(barrier, count + 1)
+    for job in (outer_job, inner_job, mixer_job):
+        job.stage_zero()
+
+    def unit_copy(source, target, sem, owner, slot):
+        return pltpu.make_async_remote_copy(
+            src_ref=source.at[owner, slot],
+            dst_ref=target.at[me, slot],
+            send_sem=sem.at[0, owner, slot],
+            recv_sem=sem.at[1, me, slot],
+            device_id={"ctx": owner},
+        )
+
+    def unit_arrival(source, target, sem, sender, slot):
+        return pltpu.make_async_remote_copy(
+            src_ref=source.at[sender, slot],
+            dst_ref=target.at[sender, slot],
+            send_sem=sem.at[0, sender, slot],
+            recv_sem=sem.at[1, sender, slot],
+            device_id={"ctx": sender},
+        )
+
+    def unit_keep(source, target, kind, slot):
+        return pltpu.make_async_copy(
+            source.at[me, slot], target.at[me, slot], own_sems.at[kind, slot]
+        )
+
+    for pair in range(pairs):
+        for batch in range(MB):
+            block = flow_ref[
+                batch * lanes : (batch + 1) * lanes, pair * 128 : (pair + 1) * 128
+            ].T
+            for j in range(2):
+                unit = (2 * pair + j) * MB + batch
+                flow_put[unit % count, unit // count] = block[j * HD : (j + 1) * HD]
+
+    def send_flow(unit, carry):
+        owner, slot = lax.rem(unit, count), unit // count
+
+        @pl.when(owner != me)
+        def _():
+            unit_copy(flow_put, flow_got, flow_sems, owner, slot).start()
+
+        @pl.when(owner == me)
+        def _():
+            unit_keep(flow_put, flow_got, 0, slot).start()
+
+        return carry
+
+    lax.fori_loop(0, total_units, send_flow, 0)
+    outer_job.stage_one()
+    inner_job.stage_one()
+    mixer_job.stage_one()
+
+    def unit_step(slot, carry):
+        def wait_one(step, inner):
+            unit_arrival(flow_put, flow_got, flow_sems, lax.rem(me + step, count), slot).wait_recv()
+            return inner
+
+        lax.fori_loop(1, count, wait_one, 0)
+        unit_keep(flow_put, flow_got, 0, slot).wait()
+        for i in range(count):
+            rows = slice(i * lanes, (i + 1) * lanes)
+            key_rows[rows, :] = got_ref[i, slot, HD : 2 * HD, :].T
+            value_rows[rows, :] = got_ref[i, slot, 2 * HD : 3 * HD, :].T
+            key_t[:, rows] = got_ref[i, slot, HD : 2 * HD, :]
+        key_documents(starts_ref, slot, length, lanes, key_docs)
+        d_key[...] = jnp.zeros_like(d_key)
+        d_value[...] = jnp.zeros_like(d_value)
+
+        def block(number, inner):
+            begin = pl.multiple_of(number * width, width)
+
+            def beside(ref):
+                parts = [ref[number * group + i, slot, 0:HD, :] for i in range(group)]
+                return parts[0] if group == 1 else jnp.concatenate(parts, axis=1)
+
+            queries, flow = beside(got_ref), beside(flow_got)
+            query_rows, flow_rows = queries.T, flow.T
+            query_docs = docs_ref[slot, :, pl.ds(begin, width)]
+            log_total = lse_ref[slot, :, pl.ds(begin, width)]
+            spread = jnp.sum(
+                flow.astype(F32) * wide_ref[slot, :, pl.ds(begin, width)], axis=0, keepdims=True
+            )
+
+            def chunk(index, d_query):
+                first = pl.multiple_of(index * depth, depth)
+                rows = pl.ds(first, depth)
+                scores = jnp.dot(key_rows[rows, :], queries, preferred_element_type=F32)
+                same = same_document(key_docs, first, depth, query_docs)
+                probs = jnp.exp(jnp.where(same, scores, MASKED) - log_total)
+                pressure = jnp.dot(value_rows[rows, :], flow, preferred_element_type=F32)
+                d_scores = (probs * (pressure - spread)).astype(BF16)
+                d_value[rows, :] += jnp.dot(
+                    probs.astype(BF16), flow_rows, preferred_element_type=F32
+                )
+                d_key[rows, :] += jnp.dot(d_scores, query_rows, preferred_element_type=F32)
+                return d_query + jnp.dot(key_t[:, rows], d_scores, preferred_element_type=F32)
+
+            d_query = over_chunks(length // depth, chunk, jnp.zeros((HD, width), F32))
+            low = (d_query * SCALE).astype(BF16)
+            for i in range(group):
+                put[number * group + i, slot, 0:HD, :] = low[:, i * lanes : (i + 1) * lanes]
+            return inner
+
+        lax.fori_loop(0, length // width, block, 0)
+        for i in range(count):
+            rows = slice(i * lanes, (i + 1) * lanes)
+            put[i, slot, HD : 2 * HD, :] = d_key[rows, :].T.astype(BF16)
+            put[i, slot, 2 * HD : 3 * HD, :] = d_value[rows, :].T.astype(BF16)
+
+        def send_one(step, inner):
+            unit_copy(put, home_got, home_sems, lax.rem(me + step, count), slot).start()
+            return inner
+
+        lax.fori_loop(1, count, send_one, 0)
+        unit_keep(put, home_got, 1, slot).start()
+
+        @pl.when(slot == 1)
+        def _():
+            outer_job.stage_two()
+
+        @pl.when(slot == 3)
+        def _():
+            inner_job.stage_two()
+
+        return carry
+
+    lax.fori_loop(0, mine, unit_step, 0)
+    mixer_job.stage_two()
+    outer_job.stage_three()
+
+    bias_sum[0] = bias_ref[...]
+    ones = jnp.ones((8, MB * lanes), BF16)
+    for pair in range(pairs):
+        columns = []
+        for batch in range(MB):
+            blocks = []
+            for j in range(2):
+                unit = (2 * pair + j) * MB + batch
+                owner, slot = unit % count, unit // count
+
+                @pl.when(owner != me)
+                def _():
+                    unit_arrival(put, home_got, home_sems, owner, slot).wait_recv()
+
+                @pl.when(owner == me)
+                def _():
+                    unit_keep(put, home_got, 1, slot).wait()
+
+                blocks.append(home_got[owner, slot])
+            rows = [b[third * HD : (third + 1) * HD] for third in range(3) for b in blocks]
+            columns.append(jnp.concatenate(rows, axis=0))
+        d_pair = jnp.concatenate(columns, axis=1)
+        d_turned[pair] = d_pair.T
+        grad = jnp.dot(d_pair, tok_ref[...], preferred_element_type=F32).astype(BF16)
+        half = joint_grad.shape[3]
+        for third in range(3):
+            row, end = third * D + pair * 128, third * D + (pair + 1) * 128
+            while row < end:
+                block, inside = row // half, row % half
+                size = min(end - row, half - inside)
+                taken = row - third * D - pair * 128 + third * 128
+                joint_grad[block // 4, block // 2 % 2, block % 2, inside : inside + size, :] = (
+                    grad[taken : taken + size]
+                )
+                row += size
+        sums = lax.dot_general(
+            ones, d_pair, (((1,), (1,)), ((), ())), preferred_element_type=F32
+        )
+        bias_sum[0, 0:1, pair * 128 : (pair + 1) * 128] = sums[0:1, 0:128]
+        bias_sum[0, 1:2, pair * 128 : (pair + 1) * 128] = sums[0:1, 256:384]
+
+    joint_job.stage_zero()
+
+    def bias_copy(level, peer):
+        return pltpu.make_async_remote_copy(
+            src_ref=bias_sum.at[level],
+            dst_ref=bias_got.at[level],
+            send_sem=bias_sems.at[0, level],
+            recv_sem=bias_sems.at[1, level],
+            device_id=peer,
+        )
+
+    bias_steps = [
+        bias_copy(0, p.other_core),
+        bias_copy(1, p.other_y),
+        bias_copy(2, p.other_x),
+    ]
+    bias_last = [
+        pltpu.make_async_remote_copy(
+            src_ref=bias_sum.at[3],
+            dst_ref=bias_z.at[p.z],
+            send_sem=bias_sems.at[0, 3 + step],
+            recv_sem=bias_sems.at[1, 3 + step],
+            device_id=p.peer_z(step),
+        )
+        for step in range(1, p.depth)
+    ]
+
+    def bias_level(level):
+        bias_steps[level].wait()
+        bias_sum[level + 1] = bias_sum[level] + bias_got[level]
+
+    bias_steps[0].start()
+    inner_job.stage_three()
+    mixer_job.stage_three()
+    joint_job.stage_one()
+    bias_level(0)
+    bias_steps[1].start()
+
+    joint_load.wait()
+    total = residual_ref[...]
+    for pair in range(pairs):
+        total = total + lax.dot_general(
+            d_turned[pair],
+            joint_all[pair],
+            (((1,), (1,)), ((), ())),
+            preferred_element_type=F32,
+        )
+    tokens_out[...] = total
+
+    bias_level(1)
+    bias_steps[2].start()
+    joint_job.stage_two()
+    bias_level(2)
+    start(bias_last)
+    outer_job.stage_four()
+    inner_job.stage_four()
+    joint_job.stage_three()
+    mixer_job.stage_four()
+
+    def finish(j):
+        jobs[j].stage_five()
+        whole = buffers[8 * j + 7]
+        lanes_half = whole.shape[2] // 2
+        rows = jnp.concatenate([whole[0], whole[1]], axis=0).astype(F32)
+        rows = jnp.where(p.core == 0, rows[:, :lanes_half], rows[:, lanes_half:])
+        outs[j][...] = rows.T
+
+    finish(0)
+    finish(1)
+    finish(2)
+    for copy in bias_last:
+        copy.wait()
+    bias_total = bias_sum[3]
+    for step in range(1, p.depth):
+        bias_total = bias_total + bias_z[p.along_z(step)]
+    bias_out[...] = bias_total
+
+    def sent(unit, carry):
+        @pl.when(lax.rem(unit, count) != me)
+        def _():
+            unit_copy(flow_put, flow_got, flow_sems, lax.rem(unit, count), unit // count).wait_send()
+
+        return carry
+
+    lax.fori_loop(0, total_units, sent, 0)
+
+    def returned(slot, carry):
+        def one(step, inner):
+            unit_copy(put, home_got, home_sems, lax.rem(me + step, count), slot).wait_send()
+            return inner
+
+        lax.fori_loop(1, count, one, 0)
+        return carry
+
+    lax.fori_loop(0, mine, returned, 0)
+    joint_job.stage_four()
+    finish(3)
+
+
+def backward(
+    starts, flow, docs, got, wide, lse, source, residual, biases, joint, outer, inner, mixer, number
+):
+    count, units, _, lanes = got.shape
+    length = count * lanes
+    width = 2 * lanes
+    pairs = H // 2
+    vm = pl.BlockSpec(memory_space=pltpu.VMEM)
+    hbm = pl.BlockSpec(memory_space=pl.ANY)
+    dma = pltpu.SemaphoreType.DMA
+    half_joint = 3 * D // (2 * count)
+    grads = [g.reshape(count // 2, 2, 2, -1, g.shape[1]) for g in (outer, inner, mixer)]
+    shapes = [(g.shape[3], g.shape[4] // 2) for g in grads] + [(half_joint, D // 2)]
+    heads, buffers = [], []
+    for half, width_half in shapes:
+        head, some = reduction_buffers(count, half, width_half, BF16)
         heads.append(head)
-        for shape in (
-            (2, depth, 2, half, lanes),
-            (2, depth, 2, half, lanes),
-            (depth, 2, head, lanes),
-            (2, depth, tail, lanes),
-            (depth, head, lanes),
-            (depth, tail, lanes),
-            (depth, half, lanes),
-        ):
-            scratch.append(pltpu.VMEM(shape, g.dtype))
-        outs.append(jax.ShapeDtypeStruct((2, half, lanes), g.dtype))
-    jobs = len(grads)
-    scratch += [
-        pltpu.SemaphoreType.DMA((jobs, 4)),
-        pltpu.SemaphoreType.DMA((jobs, 9)),
-        pltpu.SemaphoreType.DMA((jobs, 9)),
-        pltpu.SemaphoreType.DMA((jobs, depth)),
-        pltpu.SemaphoreType.DMA((jobs, depth)),
-    ]
+        buffers += some
+    outs = [jax.ShapeDtypeStruct((w // 2, 2 * half), F32) for half, w in shapes]
     return pl.pallas_call(
-        functools.partial(reduce_kernel, count, tuple(heads)),
-        out_shape=tuple(outs),
-        in_specs=[pl.BlockSpec(memory_space=pl.ANY)] * jobs,
-        out_specs=[pl.BlockSpec(memory_space=pltpu.VMEM)] * jobs,
-        scratch_shapes=scratch,
+        functools.partial(backward_kernel, width, tuple(heads)),
+        out_shape=(
+            jax.ShapeDtypeStruct(residual.shape, F32),
+            *outs,
+            jax.ShapeDtypeStruct((BIAS_ROWS, D), F32),
+        ),
+        in_specs=[pl.BlockSpec(memory_space=pltpu.SMEM)] + [vm] * 8 + [hbm] * 4,
+        out_specs=(vm,) * 6,
+        scratch_shapes=[
+            pltpu.VMEM((count, units, HD, lanes), BF16),
+            pltpu.VMEM((count, units, HD, lanes), BF16),
+            pltpu.VMEM((count, units, 3 * HD, lanes), BF16),
+            pltpu.VMEM((count, units, 3 * HD, lanes), BF16),
+            pltpu.VMEM((length, HD), BF16),
+            pltpu.VMEM((length, HD), BF16),
+            pltpu.VMEM((HD, length), BF16),
+            pltpu.VMEM((length, lanes), jnp.int32),
+            pltpu.VMEM((length, HD), F32),
+            pltpu.VMEM((length, HD), F32),
+            pltpu.VMEM((pairs, D, 384), BF16),
+            pltpu.VMEM((count // 2, 2, 2, half_joint, D), BF16),
+            pltpu.VMEM((pairs, MB * lanes, 384), BF16),
+            pltpu.VMEM((4, BIAS_ROWS, D), F32),
+            pltpu.VMEM((3, BIAS_ROWS, D), F32),
+            pltpu.VMEM((count // 2, BIAS_ROWS, D), F32),
+            dma((2, count, units)),
+            dma((2, count, units)),
+            dma((3, units)),
+            dma((4, 4)),
+            dma((2, 4, 9)),
+            dma((2, 4, count // 2)),
+            dma((2, 3 + count // 2)),
+            *buffers,
+        ],
         compiler_params=pltpu.CompilerParams(
-            collective_id=number, has_side_effects=True, vmem_limit_bytes=56 * 1024 * 1024
+            collective_id=number, has_side_effects=True, vmem_limit_bytes=62 * 1024 * 1024
         ),
-        name="reduce_all",
-    )(*[g.reshape(depth, 2, *g.shape[1:]) for g in grads])
+        name="backward",
+    )(starts, flow, docs, got, wide, lse, source, residual, biases, joint, *grads)
 
 
 def on_device(
@@ -1021,7 +1410,7 @@
         outer_weight,
         0,
     )
-    joint = joint.reshape(D, 3 * D)
+    joint = joint.reshape(H // 2, D, 384)
     mixer, inner, outer = mixer.reshape(D, D), inner.reshape(D, FF), outer.reshape(FF, D)
     heads_of = [
         vectors[:, i, :part].reshape(D).astype(F32)
@@ -1059,46 +1448,44 @@
     d_branch = d_residual.astype(BF16)
     mixing_grad = jnp.sum(d_branch.astype(F32), axis=0)
     mixer_grad = mul_tn(d_branch, attended)
-    flow = mul_nt(mixer, d_branch).astype(BF16)
-    flow_units = exchange(to_units(flow, 1, count, units), 2)
-    d_units = attend_back(received, flow_units, unit_starts, unit_docs, wide, lse)
-    d_joint = from_units(exchange(d_units, 3), 3)
-    bias_sums = jnp.sum(d_joint.astype(F32), axis=1)
-    query_grad = bias_sums[0:D]
-    values_grad = bias_sums[2 * D :]
-    joint_grad = mul_nn(d_joint, source)
-    tokens_grad = d_residual + mul_tt(d_joint, joint)
-    tokens_grad = tokens_grad.reshape(MB, 1, rows, D)
-
-    small = [
-        query_grad,
-        values_grad,
+    world = count * shards
+    index = me * shards + lax.axis_index("fsdp")
+    sums = [
         mixing_grad,
         scale_grad,
         shift_grad,
-        hidden_grad,
         return_grad,
         rescale_grad,
         reshift_grad,
+        *hidden_grad.reshape(FF // D, D),
     ]
-    world = count * shards
-    packed = jnp.concatenate([v.reshape(world, -1) for v in small], axis=1)
-    turned = [outer_grad, inner_grad, mixer_grad, joint_grad]
+    turned = [outer_grad, inner_grad, mixer_grad]
     if shards == 4 and count % 2 == 0 and D % (32 * count) == 0:
-        core = lax.rem(lax.axis_index("fsdp"), 2)
-        bias_job = packed.reshape(count, 2, 2, -1).transpose(0, 2, 1, 3)
-        spare = -packed.shape[1] % 128
-        bias_job = jnp.pad(bias_job, ((0, 0), (0, 0), (0, 0), (0, spare)))
-        bias_job = jnp.pad(bias_job.reshape(count, 2, 1, -1), ((0, 0), (0, 0), (0, 7), (0, 0)))
-        jobs = [g.astype(BF16).reshape(count, 2, -1, g.shape[1]) for g in turned] + [bias_job]
-        *sums, own = reduce_all(jobs, 4)
-        blocks = []
-        for g in sums:
-            width = g.shape[2] // 2
-            g = g.reshape(-1, 2 * width)
-            blocks.append(lax.dynamic_slice_in_dim(g, core * width, width, 1).T.astype(F32))
-        own = lax.dynamic_index_in_dim(own, core, 0, False)[0, : packed.shape[1]]
+        flow = mul_nt(d_branch, mixer).astype(BF16)
+        biases = jnp.pad(jnp.stack(sums), ((2, BIAS_ROWS - 2 - len(sums)), (0, 0)))
+        tokens_grad, *blocks, biases = backward(
+            unit_starts,
+            flow,
+            unit_docs,
+            received,
+            wide,
+            lse,
+            source,
+            d_residual,
+            biases,
+            joint,
+            *[g.astype(BF16) for g in turned],
+            1,
+        )
     else:
+        natural = joint.reshape(H // 2, D, 3, 128).transpose(1, 2, 0, 3).reshape(D, 3 * D)
+        flow = mul_nt(mixer, d_branch).astype(BF16)
+        flow_units = exchange(to_units(flow, 1, count, units), 2)
+        d_units = attend_back(received, flow_units, unit_starts, unit_docs, wide, lse)
+        d_joint = from_units(exchange(d_units, 3), 3)
+        bias_sums = jnp.sum(d_joint.astype(F32), axis=1)
+        turned.append(mul_nn(d_joint, source))
+        tokens_grad = d_residual + mul_tt(d_joint, natural)
 
         def reduced(grad):
             over_lanes = lax.psum_scatter(
@@ -1108,16 +1495,14 @@
             return over_rows.T.astype(F32)
 
         blocks = [reduced(g) for g in turned]
-        packed = lax.psum(packed, ("ctx", "fsdp"))
-        index = me * shards + lax.axis_index("fsdp")
-        own = lax.dynamic_slice_in_dim(packed, index, 1, 0)[0]
+        biases = jnp.stack([bias_sums[:D], bias_sums[2 * D :], *sums])
+        biases = lax.psum(biases, ("ctx", "fsdp"))
+    tokens_grad = tokens_grad.reshape(MB, 1, rows, D)
     outer_out_grad, inner_out, mixer_out, joint_out = blocks
-    sums = []
-    begin = 0
-    for v in small:
-        size = v.shape[0] // world
-        sums.append(own[begin : begin + size])
-        begin += size
+    own = lax.dynamic_slice_in_dim(biases[:8], index * (D // world), D // world, 1)
+    hidden_rows = biases[8 : 8 + FF // D].reshape(FF)
+    own_hidden = lax.dynamic_slice_in_dim(hidden_rows, index * (FF // world), FF // world, 0)
+    sums = [*own[:5], own_hidden, *own[5:]]
     return (result, tokens_grad, joint_out, mixer_out, inner_out, outer_out_grad, *sums)
 
 

time: 401 us -> 264 us (0.66)
  Pallas kernels: 286 us -> 209 us
  local copies, waits for them, and re-layouts: 44.7 us -> 19.3 us
  matrix products: 46.4 us -> 27.5 us
  other arithmetic: 21.5 us -> 5.11 us
    pallas_call x4 -> x1, Pallas kernels: 188 us -> 111 us  [backward(): pl.pallas_call(functools.partial(backward_kernel, width, tuple(heads)), o...]
    concatenate x10 -> x0, local copies, waits for them, and re-layouts: 12.1 us -> none  [on_device(): packed = jnp.concatenate([v.reshape(world, -1) for v in small], axis=1)]
    dot_general x4 -> x3, matrix products: 18 us -> 7.15 us  [mul_nn(): return jnp.dot(a, b, preferred_element_type=F32)]
    convert_element_type x4 -> x0, other arithmetic: 6.37 us -> none  [on_device(): lax.dynamic_slice_in_dim(g, core * width, width, 1).T.astype(F32)]
    reduce_sum x1 -> x0, other arithmetic: 5.12 us -> none  [on_device(): bias_sums = jnp.sum(d_joint.astype(F32), axis=1)]
    dot_general x1 -> x0, matrix products: 4.6 us -> none  [mul_tt(): lax.dot_general(a, b, (((0,), (1,)), ((), ())), preferred_element_type=F32)]
    dynamic_slice x3 -> x2, local copies, waits for them, and re-layouts: 5.06 us -> 0.66 us  [the longest x1 0.58 us: on_device(): lax.dynamic_slice_in_dim(hidden_rows, index * (FF // world), FF // world, 0)]
    reshape x4 -> x1, local copies, waits for them, and re-layouts: 4.22 us -> 0.01 us  [on_device(): hidden_rows = biases[8:8 + FF // D].reshape(FF)]
where the time goes in v4:
time: 264 us; the launch traced here: 262 us
  Pallas kernels  209 us (79%)
  matrix products  27.5 us (10%)
  local copies, waits for them, and re-layouts  19.3 us (7%)
  other arithmetic  5.11 us (2%)
    pallas_call x1, Pallas kernels, backward(): pl.pallas_call(functools.partial(backward_kernel, width, tuple(heads)), o...  111 us
    pallas_call x1, Pallas kernels, forward(): pl.pallas_call(functools.partial(forward_kernel, width), out_shape=(jax.S...  97.8 us
    dot_general x3, matrix products, mul_tn(): lax.dot_general(a, b, (((0,), (0,)), ((), ())), preferred_element_type=F32)  13 us
    unnamed x46, local copies, waits for them, and re-layouts  8.21 us
    dot_general x3, matrix products, mul_nt(): lax.dot_general(a, b, (((1,), (1,)), ((), ())), preferred_element_type=F32)  7.34 us
    dot_general x3, matrix products, mul_nn(): return jnp.dot(a, b, preferred_element_type=F32)  7.15 us
    another operation x9, local copies, waits for them, and re-layouts, on_device(): jnp.stack([query_bias, value_bias, mixer_bias, first_gain, first_shift, o...  5.3 us

profile of v4, /device:TPU:0, one launch (start us, length us, event | category | flops | bytes accessed | tf_op | source)
XLA Modules:
  0.0 261.9 jit_solution(16203922285787420993)
XLA Ops:
  0.7 0.7 stack.48
  1.3 0.7 stack.49
  2.0 0.7 stack.50
  2.6 0.7 stack.51
  3.3 0.7 stack.52
  4.0 0.7 stack.53
  4.6 0.7 stack.54
  5.3 0.7 stack.55
  6.0 0.7 copy.39
  6.6 0.7 reshape.233
  7.3 0.6 gather_fusion
  7.9 0.0 copy-start.13
  7.9 0.1 scatter.4.vec_ref
  8.0 0.0 copy-start.11
  8.0 0.1 convert_reduce_fusion.4
  8.1 0.6 sub.45.docs_ref.refs_2_
  8.8 97.8 %forward.1 = (bf16[384,768]{1,0:T(8,128)(2,1)}, bf16[8,5,192,128]{3,2,1,0:T(8,128)(2,1)}, f32[5,64,1024]{2,1,0:T(8,128)}, f32[5,1,1024]{2,1,0:T(1,128)}, bf16[6,...) custom-call(s32[5,8]{1,0:T(8,128)} %copy-done.13, ...), custom_call_target="tpu_custom_call" | custom-call | tf_op jit(solution)/shard_map/forward/pallas_call | solution.py:711
  106.5 0.8 slice_convert_fusion
  107.3 1.0 convert_reduce_fusion.6
  108.4 0.1 reshape.249
  108.5 0.1 reshape.245
  108.5 0.1 reshape.246
  108.6 0.1 reshape.250
  108.7 0.1 reshape.248
  108.8 0.1 reshape.244
  108.8 0.3 convert_reduce_fusion.1
  109.1 0.0 copy-done.4
  109.2 0.0 copy-start.14
  109.2 2.3 fusion.25
  111.5 0.0 slice-start
  111.5 0.3 multiply_reduce_fusion.3
  111.8 0.2 copy-done.14
  112.0 2.7 %multiply_convert_fusion = (bf16[384,3072]{1,0:T(8,128)(2,1)S(1)}, f32[384,3072]{1,0:T(8,128)S(1)}) fusion(f32[3072]{0:T(1024)S(1)} %bitcast.78, bf16[768,3072]{1,0:T(8,128)(2,1)S(1)} %bitcast.79, f32[384,768]{1,0:T(8,128)S(1)} %get-tuple-element.119, f32[768]{0:T(1024)S(1)} %reshape.246, f32[768]{0:T(1024)S(1)} %reshape.245, f32[384]{0:T(512)S(1)} %add_rsqrt_fusion.1, ...), kind=kOutput, calls=%fused_computation.11 | convolution fusion | flops 1820491776 | bytes 12997632 | tf_op jit(solution)/shard_map/dot_general | solution.py:263
  114.7 2.2 fusion.26
  116.9 0.3 multiply_reduce_fusion.2
  117.2 0.6 fusion.14
  117.8 1.3 convert_reduce_fusion.2
  119.1 3.4 %convert_reduce_fusion = (f32[3072]{0:T(1024)S(1)}, bf16[384,3072]{1,0:T(8,128)(2,1)S(1)}) fusion(f32[384,3072]{1,0:T(8,128)S(1)} %get-tuple-element.121, bf16[3072,768]{1,0:T(8,128)(2,1)S(1)} %bitcast.84, f32[384,768]{1,0:T(8,128)S(1)} %get-tuple-element.102), kind=kOutput, calls=%fused_computation.10 | convolution fusion | flops 1826386944 | bytes 12988416 | tf_op jit(solution)/shard_map/dot_general | solution.py:271
  122.6 0.0 copy-start.17
  122.6 0.0 copy-done.6
  122.6 2.4 multiply_reduce_fusion
  125.0 0.0 copy-done.17
  125.1 0.4 convert_reduce_fusion.3
  125.5 0.0 copy-start
  125.5 0.8 copy-done.5
  126.4 1.5 convolution_convert_fusion.3.refs_1_
  127.9 0.1 stack.63
  128.0 0.6 pad.11.refs_8_
  128.6 0.0 copy-done
  128.6 1.8 convolution_convert_fusion.2
  130.4 6.7 %convolution_convert_fusion = bf16[3072,768]{1,0:T(8,128)(2,1)} fusion(bf16[384,3072]{1,0:T(8,128)(2,1)} %copy-done.17, f32[384,768]{1,0:T(8,128)S(1)} %copy-done.3, f32[768]{0:T(1024)S(1)} %reshape.246, f32[768]{0:T(1024)S(1)} %reshape.245, f32[384]{0:T(512)S(1)} %add_rsqrt_fusion.1, f32[384]{0:T(512)S(1)} %broadcast_multiply_fusion.4), kind=kOutput, calls=%fused_computation.2 | convolution fusion | flops 1815773184 | bytes 8266752 | tf_op jit(solution)/shard_map/dot_general | solution.py:267
  137.2 0.0 copy-done.16
  137.2 4.4 %convolution_convert_fusion.1 = bf16[768,3072]{1,0:T(8,128)(2,1)} fusion(bf16[384,3072]{1,0:T(8,128)(2,1)S(1)} %copy-done.16, f32[384,768]{1,0:T(8,128)S(1)} %copy-done.7), kind=kOutput, calls=%fused_computation.3 | convolution fusion | flops 1814593536 | bytes 8257536 | tf_op jit(solution)/shard_map/dot_general | solution.py:267
  141.6 111.2 %backward.1 = (f32[384,768]{1,0:T(8,128)}, f32[768,96]{1,0:T(8,128)}, f32[192,384]{1,0:T(8,128)}, f32[192,96]{1,0:T(8,128)}, f32[192,288]{1,0:T(8,128)}, /*index=5*/f32[16,768]{1,0:T(8,128)}) custom-call(s32[5,8]{1,0:T(8,128)} %copy-done.13, bf16[384,768]{1,0:T(8,128)(2,1)} %convolution_convert_fusion.3.refs_1_, s32[5,1,1024]{2,1,0:T(1,128)} %sub.45.docs_ref.refs_2_, ...), custom_call_target="tpu_custom_call" | custom-call | tf_op jit(solution)/shard_map/backward/pallas_call | solution.py:1313
  252.8 0.7 slice.64
  253.6 0.7 slice.63
  254.3 0.1 constant_dynamic-slice_fusion
  254.4 0.6 dynamic_slice.7
  255.0 0.5 slice_bitcast_fusion
  255.5 1.9 copy.36
  257.4 2.4 copy.45
  259.8 0.7 copy.46
  260.6 0.6 copy.47
  261.2 0.7 copy.48
  (52 shorter events, 0.2 us)
Async XLA Ops:
  7.9 0.9 copy-start.13
  8.0 0.8 copy-start.11
  8.8 100.1 %copy-start.1 = (bf16[3,1,128,768]{3,2,1,0:T(8,128)(2,1)S(1)}, bf16[3,1,128,768]{3,2,1,0:T(8,128)(2,1)}, u32[]{:S(2)}) copy-start(bf16[3,1,128,768]{3,2,1,0:T(8,128)(2,1)} %param.33) | copy-start | bytes 1769476
  8.8 100.4 %copy-start.4 = (bf16[3,1,128,768]{3,2,1,0:T(8,128)(2,1)S(1)}, bf16[3,1,128,768]{3,2,1,0:T(8,128)(2,1)}, u32[]{:S(2)}) copy-start(bf16[3,1,128,768]{3,2,1,0:T(8,128)(2,1)} %param.18) | copy-start | bytes 1769476
  109.2 2.9 %copy-start.14 = (bf16[4,192,3072]{2,1,0:T(8,128)(2,1)S(1)}, bf16[4,192,3072]{2,1,0:T(8,128)(2,1)}, u32[]{:S(2)}) copy-start(bf16[4,192,3072]{2,1,0:T(8,128)(2,1)} %get-tuple-element.45) | copy-start | bytes 14155780
  111.5 13.6 %copy-start.2 = (f32[384,768]{1,0:T(8,128)}, f32[384,768]{1,0:T(8,128)S(1)}, u32[]{:S(2)}) copy-start(f32[384,768]{1,0:T(8,128)S(1)} %get-tuple-element.119) | copy-start | bytes 3538948
  111.5 3.2 %slice-start = ((s8[4718592]{0:T(1024)(128)(4,1)}), s8[4194304]{0:T(1024)(128)(4,1)S(1)}, s32[]{:S(2)}) async-start(s8[4718592]{0:T(1024)(128)(4,1)} %bitcast.81), calls=%async_computation | async-start | bytes 8388608
  112.0 2.7 %slice-start.1 = ((s8[4718592]{0:T(1024)(128)(4,1)}), s8[524288]{0:T(1024)(128)(4,1)S(1)}, s32[]{:S(2)}) async-start(s8[4718592]{0:T(1024)(128)(4,1)} %bitcast.81), calls=%async_computation.1 | async-start | bytes 1048576
  114.7 2.2 copy-start.15
  119.1 3.5 %copy-start.6 = (f32[384,768]{1,0:T(8,128)}, f32[384,768]{1,0:T(8,128)S(1)}, u32[]{:S(2)}) copy-start(f32[384,768]{1,0:T(8,128)S(1)} %get-tuple-element.102) | copy-start | bytes 3538948
  122.6 2.4 copy-start.17
  125.1 1.3 copy-start.5
  125.5 3.1 %copy-start = (f32[384,768]{1,0:T(8,128)}, f32[384,768]{1,0:T(8,128)S(1)}, u32[]{:S(2)}) copy-start(f32[384,768]{1,0:T(8,128)S(1)} %get-tuple-element.104.refs_7_) | copy-start | bytes 3538948
  126.4 2.2 copy-start.8
  128.6 1.8 copy-start.3
  130.4 6.7 %copy-start.7 = (f32[384,768]{1,0:T(8,128)S(1)}, f32[384,768]{1,0:T(8,128)}, u32[]{:S(2)}) copy-start(f32[384,768]{1,0:T(8,128)} %copy-done.6) | copy-start | bytes 3538948
  130.4 6.7 %copy-start.16 = (bf16[384,3072]{1,0:T(8,128)(2,1)S(1)}, bf16[384,3072]{1,0:T(8,128)(2,1)}, u32[]{:S(2)}) copy-start(bf16[384,3072]{1,0:T(8,128)(2,1)} %copy-done.15) | copy-start | bytes 7077892
  257.4 2.4 copy-start.10
  257.4 3.1 %copy-start.12 = (f32[192,96]{1,0:T(8,128)S(1)}, f32[192,96]{1,0:T(8,128)}, u32[]{:S(2)}) copy-start(f32[192,96]{1,0:T(8,128)} %get-tuple-element.147) | copy-start | bytes 221188
  257.4 3.8 %copy-start.9 = (f32[192,384]{1,0:T(8,128)S(1)}, f32[192,384]{1,0:T(8,128)}, u32[]{:S(2)}) copy-start(f32[192,384]{1,0:T(8,128)} %get-tuple-element.148) | copy-start | bytes 884740

commit v5 on v4

--- a/solution.py
+++ b/solution.py
@@ -22,10 +22,6 @@
 
 F32 = jnp.float32
 BF16 = jnp.bfloat16
-
-
-def doc_index(positions, starts_row):
-    return jnp.sum((starts_row[None, :] <= positions[:, None]).astype(jnp.int32), axis=1) - 1
 
 
 def norm_forward(hidden, gain, shift):
@@ -48,6 +44,50 @@
 def gelu_parts(inner):
     cumulative = 0.5 * (1.0 + lax.erf(inner * ROOT_HALF))
     return (inner * cumulative, cumulative + inner * jnp.exp(-0.5 * inner * inner) * GAUSS_PEAK)
+
+
+UNITS = MB * H
+BIAS_ROWS = 16
+RELAY_PIECES = 3
+
+
+def spare_owner(count, j):
+    stride = count // (UNITS % count)
+    return j * stride + (j % 2 if stride > 1 else 0)
+
+
+def owner_of(count, unit):
+    full, rest = UNITS // count, UNITS % count
+    if rest == 0:
+        return unit % count
+    if full == 0:
+        return spare_owner(count, unit)
+    late = unit // (full * count)
+    return (1 - late) * (unit % count) + late * spare_owner(count, unit - full * count)
+
+
+def spare_index(count, device):
+    return device // (count // (UNITS % count))
+
+
+def owned(count, device):
+    full, rest = UNITS // count, UNITS % count
+    if rest == 0:
+        return full
+    j = spare_index(count, device)
+    extra = (spare_owner(count, j) == device) & (j < rest)
+    return full + extra.astype(jnp.int32)
+
+
+def batch_of(count, device, slot):
+    full, rest = UNITS // count, UNITS % count
+    if rest == 0:
+        return (slot * count + device) % MB
+    if full == 0:
+        return jnp.minimum(spare_index(count, device), UNITS - 1) % MB
+    late = slot // full
+    unit = slot * count + (1 - late) * device + late * spare_index(count, device)
+    return unit % MB
 
 
 def exchange_kernel(count, x_ref, y_ref, held, send_sem, recv_sem, own_sem):
@@ -114,12 +154,23 @@
     return parts[0] if len(parts) == 1 else jnp.concatenate(parts, axis=1)
 
 
-def key_documents(starts_ref, unit, length, lanes, key_docs):
-    position = lax.broadcasted_iota(jnp.int32, (length, lanes), 0)
-    docs = jnp.zeros((length, lanes), jnp.int32) - 1
+def document(starts_ref, batch, position):
+    docs = jnp.zeros(position.shape, jnp.int32) - 1
     for j in range(starts_ref.shape[1]):
-        docs = docs + jnp.where(position >= starts_ref[unit, j], 1, 0)
-    key_docs[...] = docs
+        docs = docs + jnp.where(position >= starts_ref[batch, j], 1, 0)
+    return docs
+
+
+def key_documents(starts_ref, batch, key_docs):
+    key_docs[...] = document(
+        starts_ref, batch, lax.broadcasted_iota(jnp.int32, key_docs.shape, 0)
+    )
+
+
+def query_documents(starts_ref, batch, begin, width):
+    return document(
+        starts_ref, batch, lax.broadcasted_iota(jnp.int32, (1, width), 1) + begin
+    )
 
 
 def same_document(key_docs, first, width, query_docs):
@@ -140,7 +191,6 @@
     starts_ref,
     x_ref,
     flow_ref,
-    docs_ref,
     wide_ref,
     lse_ref,
     d_ref,
@@ -160,7 +210,8 @@
         key_rows[rows, :] = x_ref[i, 0, HD : 2 * HD, :].T
         value_rows[rows, :] = x_ref[i, 0, 2 * HD : 3 * HD, :].T
         key_t[:, rows] = x_ref[i, 0, HD : 2 * HD, :]
-    key_documents(starts_ref, unit, length, lanes, key_docs)
+    batch = batch_of(count, lax.axis_index("ctx"), unit)
+    key_documents(starts_ref, batch, key_docs)
     d_key[...] = jnp.zeros_like(d_key)
     d_value[...] = jnp.zeros_like(d_value)
     group = width // lanes
@@ -171,7 +222,7 @@
         flow = across(flow_ref, number * group, slice(0, HD), width, lanes)
         query_rows = queries.T
         flow_rows = flow.T
-        query_docs = docs_ref[0, :, pl.ds(begin, width)]
+        query_docs = query_documents(starts_ref, batch, begin, width)
         log_total = lse_ref[0, :, pl.ds(begin, width)]
         spread = jnp.sum(
             flow.astype(F32) * wide_ref[0, :, pl.ds(begin, width)], axis=0, keepdims=True
@@ -212,7 +263,7 @@
     return pl.BlockSpec(dims, lambda u, starts: (u,) + (0,) * (len(dims) - 1))
 
 
-def attend_back(x, flow, starts, docs, wide, lse):
+def attend_back(x, flow, starts, wide, lse):
     count, units, _, lanes = x.shape
     length = count * lanes
     width = 2 * lanes if count % 2 == 0 else lanes
@@ -225,7 +276,6 @@
             in_specs=[
                 unit_block(count, 1, 3 * HD, lanes),
                 unit_block(count, 1, HD, lanes),
-                own_block(1, 1, length),
                 own_block(1, HD, length),
                 own_block(1, 1, length),
             ],
@@ -241,20 +291,22 @@
         ),
         compiler_params=pltpu.CompilerParams(dimension_semantics=("arbitrary",)),
         name="attend_back",
-    )(starts, x, flow, docs, wide, lse)
+    )(starts, x, flow, wide, lse)
 
 
 def to_units(columns, parts, count, units):
     rows = columns.shape[1] // MB
     x = columns.reshape(parts, H, HD, MB, rows).transpose(1, 3, 0, 2, 4)
-    x = x.reshape(MB * H, parts * HD, rows)
-    x = jnp.pad(x, ((0, units * count - MB * H), (0, 0), (0, 0)))
-    return x.reshape(units, count, parts * HD, rows).transpose(1, 0, 2, 3)
+    x = x.reshape(UNITS, parts * HD, rows)
+    places = [owner_of(count, u) * units + u // count for u in range(UNITS)]
+    y = jnp.zeros((count * units, parts * HD, rows), columns.dtype)
+    return y.at[jnp.array(places)].set(x).reshape(count, units, parts * HD, rows)
 
 
 def from_units(x, parts):
     count, units, _, rows = x.shape
-    x = x.transpose(1, 0, 2, 3).reshape(units * count, parts * HD, rows)[: MB * H]
+    places = [owner_of(count, u) * units + u // count for u in range(UNITS)]
+    x = x.reshape(count * units, parts * HD, rows)[jnp.array(places)]
     x = x.reshape(H, MB, parts, HD, rows).transpose(2, 0, 3, 1, 4)
     return x.reshape(parts * D, MB * rows)
 
@@ -279,12 +331,14 @@
     width,
     starts_ref,
     tok_ref,
-    docs_ref,
     joint_ref,
-    vec_ref,
     mixer_ref,
     inner_ref,
     outer_ref,
+    *refs,
+):
+    vec_refs = refs[:9]
+    (
     att_ref,
     got_ref,
     wide_ref,
@@ -295,6 +349,7 @@
     inner_out,
     outer_out,
     joint_all,
+    vec_put,
     bias_rows,
     put,
     back_put,
@@ -311,8 +366,9 @@
     back_got_sem,
     joint_sems,
     weight_sems,
+    relay_sems,
     own_sems,
-):
+    ) = refs[9:]
     count, units, _, lanes = got_ref.shape
     length = count * lanes
     depth = min(length, 1024)
@@ -327,7 +383,7 @@
     other_core = {"fsdp": 2 * y + 1 - core}
     other_y = {"fsdp": far}
     other_x = {"ctx": me + 1 - 2 * x}
-    mine = (total_units - me + count - 1) // count
+    mine = owned(count, me)
 
     barrier = pltpu.get_barrier_semaphore()
 
@@ -401,44 +457,77 @@
     ]
     for copy in own_in:
         copy.start()
-    vec_own = pltpu.make_async_copy(vec_ref, vec_out.at[shard], own_sems.at[1, 3, 0])
-    vec_own.start()
+    for i, ref in enumerate(vec_refs):
+        vec_put[i : i + 1, 0 : ref.shape[0]] = ref[...].astype(F32).reshape(1, ref.shape[0])
+    vec_out[shard] = vec_put[...]
     pl.semaphore_wait(barrier, count + 1)
 
-    vec_y = remote(vec_ref, vec_out.at[shard], weight_sems, (0, 0), other_y)
-    vec_core = remote(vec_ref, vec_out.at[shard], weight_sems, (0, 1), other_core)
+    vec_y = remote(vec_put, vec_out.at[shard], weight_sems, (0, 0), other_y)
+    vec_core = remote(vec_put, vec_out.at[shard], weight_sems, (0, 1), other_core)
     vec_pass = remote(vec_out.at[far], vec_out.at[far], weight_sems, (0, 2), other_core)
     mixer_y = remote(mixer_ref, mixer_out.at[shard], weight_sems, (1, 0), other_y)
     mixer_core = remote(mixer_ref, mixer_out.at[shard], weight_sems, (1, 1), other_core)
     mixer_pass = remote(mixer_out.at[far], mixer_out.at[far], weight_sems, (1, 2), other_core)
-    halves = []
-    for i, (ref, out) in enumerate(((inner_ref, inner_out), (outer_ref, outer_out))):
-        size = ref.shape[0] // 2
-        rows = pl.ds(pl.multiple_of(x * size, size), size)
-        halves.append(
-            (
-                remote(ref.at[rows, :], out.at[shard, rows, :], weight_sems, (2 + i, 0), other_y),
-                remote(ref, out.at[shard], weight_sems, (2 + i, 1), other_core),
-                remote(
-                    out.at[far, rows, :], out.at[far, rows, :], weight_sems, (2 + i, 3), other_x
-                ),
-                remote(out.at[far], out.at[far], weight_sems, (2 + i, 2), other_core),
-            )
-        )
+    class Relayed:
+        def __init__(self, ref, out, index):
+            size = ref.shape[0] // 2
+            piece = size // RELAY_PIECES
+            self.over_y, self.over_x = [], []
+            for k in range(RELAY_PIECES):
+                rows = pl.ds(pl.multiple_of(x * size + k * piece, piece), piece)
+                self.over_y.append(
+                    remote(
+                        ref.at[rows, :],
+                        out.at[shard, rows, :],
+                        relay_sems,
+                        (index, 0, k),
+                        other_y,
+                    )
+                )
+                passed = out.at[far, rows, :]
+                self.over_x.append(remote(passed, passed, relay_sems, (index, 1, k), other_x))
+            self.core = remote(ref, out.at[shard], weight_sems, (2 + index, 0), other_core)
+            self.all = remote(out.at[far], out.at[far], weight_sems, (2 + index, 1), other_core)
+
+        def begin(self):
+            for copy in self.over_y:
+                copy.start()
+            self.core.start()
+
+        def relay(self, k):
+            self.over_y[k].wait_recv()
+            self.over_x[k].start()
+
+        def hand_on(self):
+            for copy in self.over_x:
+                copy.wait_recv()
+            self.all.start()
+
+        def end(self):
+            for copy in self.over_y + self.over_x:
+                copy.wait_send()
+            self.core.wait()
+            self.all.wait()
+
+    outer_way = Relayed(outer_ref, outer_out, 0)
+    inner_way = Relayed(inner_ref, inner_out, 1)
     vec_y.start()
     vec_core.start()
-    every_pair(joint_y, "start")
-    every_pair(joint_core, "start")
+
+    def send_joint(pair, carry):
+        each_third(pair, joint_y, "start")
+        each_third(pair, joint_core, "start")
+        return carry
+
+    lax.fori_loop(0, pairs, send_joint, 0)
+    outer_way.begin()
+    inner_way.begin()
     mixer_y.start()
     mixer_core.start()
-    for copies in halves:
-        copies[0].start()
-        copies[1].start()
     for first, second in zip(own_in, own_out):
         first.wait()
         second.start()
 
-    vec_own.wait()
     vec_y.wait_recv()
     vec_pass.start()
     vec_core.wait_recv()
@@ -446,7 +535,7 @@
 
     def bias_of(slot):
         pieces = [
-            vec_out[f, slot : slot + 1, 0:part].astype(F32) for f in range(4)
+            vec_out[f, slot : slot + 1, 0:part] for f in range(4)
         ]
         return jnp.concatenate(pieces, axis=1)
 
@@ -458,7 +547,7 @@
         bias_rows[pair, :, 256:384] = jnp.broadcast_to(value_bias[:, columns], (8, 128))
 
     def sent_sem(unit):
-        return lax.rem(unit, count), unit // count
+        return owner_of(count, unit), unit // count
 
     def send_copy(unit):
         owner, slot = sent_sem(unit)
@@ -470,10 +559,9 @@
             device_id={"ctx": owner},
         )
 
-    def keep_copy(unit):
-        owner, slot = sent_sem(unit)
+    def keep_copy(slot):
         return pltpu.make_async_copy(
-            put.at[owner, slot], got_ref.at[me, slot], own_sems.at[2, slot, 0]
+            put.at[me, slot], got_ref.at[me, slot], own_sems.at[2, slot, 0]
         )
 
     def project(pair, carry):
@@ -494,26 +582,24 @@
                     turned = turned * SCALE
                 for j in range(2):
                     unit = (2 * pair + j) * MB + batch
-                    put[lax.rem(unit, count), unit // count, third * HD : (third + 1) * HD, :] = (
+                    put[owner_of(count, unit), unit // count, third * HD : (third + 1) * HD, :] = (
                         turned[j * HD : (j + 1) * HD]
                     )
         for i in range(2 * MB):
-            unit = 2 * pair * MB + i
-
-            @pl.when(lax.rem(unit, count) != me)
+            unit = 2 * pair * MB + lax.rem(i + me, 2 * MB)
+            owner, slot = owner_of(count, unit), unit // count
+
+            @pl.when(owner != me)
             def _():
                 send_copy(unit).start()
 
-            @pl.when(lax.rem(unit, count) == me)
+            @pl.when(owner == me)
             def _():
-                keep_copy(unit).start()
+                keep_copy(slot).start()
 
         return carry
 
     lax.fori_loop(0, pairs, project, 0)
-
-    mixer_y.wait_recv()
-    mixer_pass.start()
 
     def arrival(sender, slot):
         return pltpu.make_async_remote_copy(
@@ -538,14 +624,6 @@
             back_put.at[me, slot], back_got.at[me, slot], own_sems.at[2, slot, 1]
         )
 
-    def relay(i):
-        halves[i][0].wait_recv()
-        halves[i][2].start()
-
-    def hand_on(i):
-        halves[i][2].wait_recv()
-        halves[i][3].start()
-
     early = total_units // count > 2
 
     def unit_step(slot, carry):
@@ -554,18 +632,19 @@
             return inner
 
         lax.fori_loop(1, count, wait_one, 0)
-        keep_copy(slot * count + me).wait()
+        keep_copy(slot).wait()
         for i in range(count):
             rows = slice(i * lanes, (i + 1) * lanes)
             key_rows[rows, :] = got_ref[i, slot, HD : 2 * HD, :].T
             value_t[:, rows] = got_ref[i, slot, 2 * HD : 3 * HD, :]
-        key_documents(starts_ref, slot, length, lanes, key_docs)
+        batch = batch_of(count, me, slot)
+        key_documents(starts_ref, batch, key_docs)
 
         def block(number, inner):
             begin = pl.multiple_of(number * width, width)
             parts = [got_ref[number * group + i, slot, 0:HD, :] for i in range(group)]
             queries = parts[0] if group == 1 else jnp.concatenate(parts, axis=1)
-            query_docs = docs_ref[slot, :, pl.ds(begin, width)]
+            query_docs = query_documents(starts_ref, batch, begin, width)
 
             def chunk(index, running):
                 peak, total, mixed = running
@@ -616,21 +695,37 @@
         back_keep(slot).start()
         if early:
 
+            @pl.when(slot == 0)
+            def _():
+                outer_way.relay(0)
+                outer_way.relay(1)
+
+            @pl.when(slot == 1)
+            def _():
+                outer_way.relay(2)
+                inner_way.relay(0)
+
             @pl.when(slot == 2)
             def _():
-                relay(0)
+                inner_way.relay(1)
+                inner_way.relay(2)
 
         return carry
 
     lax.fori_loop(0, mine, unit_step, 0)
 
     if not early:
-        relay(0)
-    relay(1)
-    hand_on(0)
+        for k in range(RELAY_PIECES):
+            outer_way.relay(k)
+        for k in range(RELAY_PIECES):
+            inner_way.relay(k)
+    mixer_y.wait_recv()
+    mixer_pass.start()
+    outer_way.hand_on()
+    inner_way.hand_on()
 
     def home(unit, carry):
-        owner, slot = lax.rem(unit, count), unit // count
+        owner, slot = owner_of(count, unit), unit // count
 
         @pl.when(owner != me)
         def _():
@@ -654,16 +749,12 @@
             tops = []
             for j in range(2):
                 unit = (2 * pair + j) * MB + batch
-                tops.append(back_got[unit % count, unit // count])
+                tops.append(back_got[owner_of(count, unit), unit // count])
             block = jnp.concatenate(tops, axis=0).T
             att_ref[batch * lanes : (batch + 1) * lanes, pair * 128 : (pair + 1) * 128] = block
 
-    hand_on(1)
-    for copies in halves:
-        copies[0].wait_send()
-        copies[1].wait()
-        copies[2].wait_send()
-        copies[3].wait()
+    outer_way.end()
+    inner_way.end()
     vec_y.wait_send()
     vec_core.wait_send()
     vec_pass.wait_send()
@@ -677,7 +768,7 @@
         copy.wait()
 
     def sent(unit, carry):
-        @pl.when(lax.rem(unit, count) != me)
+        @pl.when(owner_of(count, unit) != me)
         def _():
             send_copy(unit).wait_send()
 
@@ -698,8 +789,8 @@
         joint_store(pair).wait()
 
 
-def forward(count, starts, tokens, docs, joint, vectors, mixer, inner, outer, number):
-    units = starts.shape[0]
+def forward(count, starts, tokens, joint, mixer, inner, outer, vectors, number):
+    units = -(-UNITS // count)
     lanes = tokens.shape[0] // MB
     length = count * lanes
     width = 2 * lanes
@@ -716,15 +807,16 @@
             jax.ShapeDtypeStruct((units, HD, length), F32),
             jax.ShapeDtypeStruct((units, 1, length), F32),
             jax.ShapeDtypeStruct((pairs, 4, part, 384), BF16),
-            jax.ShapeDtypeStruct((4, *vectors.shape), BF16),
+            jax.ShapeDtypeStruct((4, BIAS_ROWS, D), F32),
             jax.ShapeDtypeStruct((4, *mixer.shape), BF16),
             jax.ShapeDtypeStruct((4, *inner.shape), BF16),
             jax.ShapeDtypeStruct((4, *outer.shape), BF16),
         ),
-        in_specs=[pl.BlockSpec(memory_space=pltpu.SMEM), vm, vm, hbm, vm, hbm, hbm, hbm],
+        in_specs=[pl.BlockSpec(memory_space=pltpu.SMEM), vm] + [hbm] * 4 + [vm] * 9,
         out_specs=(vm, vm, vm, vm, hbm, vm, hbm, hbm, hbm),
         scratch_shapes=[
             pltpu.VMEM((pairs, 4, part, 384), BF16),
+            pltpu.VMEM((BIAS_ROWS, D), F32),
             pltpu.VMEM((pairs, 8, 384), F32),
             pltpu.VMEM((count, units, 3 * HD, lanes), BF16),
             pltpu.VMEM((count, units, HD, lanes), BF16),
@@ -741,17 +833,14 @@
             dma((count, units)),
             dma((2, 3, pairs, 3)),
             dma((2, 4, 4)),
+            dma((2, 2, 2, RELAY_PIECES)),
             dma((3, max(pairs, units, 4), 3)),
         ],
         compiler_params=pltpu.CompilerParams(
             collective_id=number, has_side_effects=True, vmem_limit_bytes=56 * 1024 * 1024
         ),
         name="forward",
-    )(starts, tokens, docs, joint, vectors, mixer, inner, outer)
-
-
-JOINT_JOB = 3
-BIAS_ROWS = 16
+    )(starts, tokens, joint, mixer, inner, outer, *vectors)
 
 
 def first_rows(half, tile):
@@ -769,6 +858,8 @@
         self.other_y = {"fsdp": 2 * (1 - self.y) + self.core}
         self.other_x = {"ctx": 2 * self.z + 1 - self.x}
 
+        self.hi, self.lo = self.z // 2, lax.rem(self.z, 2)
+
     def along_z(self, step):
         return lax.rem(self.z + step, self.depth)
 
@@ -786,12 +877,13 @@
 
 
 class Reduction:
-    def __init__(self, place, j, grad, out, head, buffers, load_sem, sems, z_sems):
-        own, got, y_one, x_one, x_two, y_two, z_got = buffers
-        self.place, self.out, self.head, self.own, self.buffers = place, out, head, own, buffers
-        half, lanes = own.shape[3], own.shape[4]
-        self.half = half
+    def __init__(self, place, j, grad, out, head, paired, buffers, sems, z_sems):
+        got, y_one, x_one, x_two, y_two, z_got = buffers
+        self.place, self.grad, self.out, self.head, self.buffers = place, grad, out, head, buffers
+        half, lanes = grad.shape[4], grad.shape[5] // 2
+        self.half, self.lanes, self.paired = half, lanes, paired
         p = place
+        here, there = self.side(p.y), self.side(1 - p.y)
 
         def remote(src, dst, slot, peer):
             return pltpu.make_async_remote_copy(
@@ -802,142 +894,153 @@
                 device_id=peer,
             )
 
-        self.loads, self.firsts = [], []
-        for side in range(2):
-            columns = pl.ds(side * lanes, lanes)
-            for low in range(2):
-                slot = 2 * side + low
-                self.loads.append(
-                    pltpu.make_async_copy(
-                        grad.at[:, low, p.core, :, columns],
-                        own.at[side, :, low],
-                        load_sem.at[j, slot],
-                    )
-                )
-                self.firsts.append(
-                    remote(
-                        grad.at[:, low, 1 - p.core, :, columns],
-                        got.at[side, :, low],
-                        slot,
-                        p.other_core,
-                    )
-                )
-        self.second = [remote(own.at[1 - p.y, :, :, 0:head, :], y_one, 4, p.other_y)]
-        self.third = [remote(own.at[p.y, :, 1 - p.x, 0:head, :], x_two, 5, p.other_x)]
-        if head < half:
-            self.second.append(remote(own.at[:, :, 1 - p.x, head:half, :], x_one, 6, p.other_x))
-            self.third.append(remote(own.at[1 - p.y, :, p.x, head:half, :], y_two, 7, p.other_y))
-        self.fourth = [
-            pltpu.make_async_remote_copy(
-                src_ref=own.at[p.y, p.along_z(step), p.x],
-                dst_ref=z_got.at[p.z],
+        def z_copy(z, target, step):
+            return pltpu.make_async_remote_copy(
+                src_ref=grad.at[z // 2, lax.rem(z, 2), p.x, p.core, :, here],
+                dst_ref=z_got.at[target],
                 send_sem=z_sems.at[0, j, step],
                 recv_sem=z_sems.at[1, j, step],
-                device_id=p.peer_z(step),
+                device_id={"ctx": 2 * z + p.x},
             )
-            for step in range(1, p.depth)
+
+        self.first = [remote(grad.at[:, :, :, 1 - p.core], got, 0, p.other_core)]
+        self.second = [remote(grad.at[:, :, :, p.core, 0:head, there], y_one, 1, p.other_y)]
+        self.third = [
+            remote(grad.at[:, :, 1 - p.x, p.core, 0:head, here], x_two, 2, p.other_x)
         ]
-        self.last = [remote(out.at[p.core], out.at[p.core], 8, p.other_core)]
+        if head < half:
+            self.second.append(
+                remote(grad.at[:, :, 1 - p.x, p.core, head:half, :], x_one, 3, p.other_x)
+            )
+            self.third.append(
+                remote(grad.at[:, :, p.x, p.core, head:half, there], y_two, 4, p.other_y)
+            )
+        if paired:
+            near = {"ctx": 2 * (2 * p.hi + 1 - p.lo) + p.x}
+            self.fourth = [
+                remote(
+                    grad.at[:, 1 - p.lo, p.x, p.core, :, here], z_got.at[pl.ds(0, 2)], 6, near
+                )
+            ]
+            self.fifth = [z_copy(2 * (1 - p.hi) + p.lo, 2, 1)]
+        else:
+            self.fourth = []
+            self.fifth = [z_copy(lax.rem(p.z + step, 4), p.z, step) for step in range(1, 4)]
+        self.last = [remote(out.at[p.core], out.at[p.core], 5, p.other_core)]
+
+    def side(self, y):
+        return pl.ds(pl.multiple_of(y * self.lanes, 128), self.lanes)
+
+    def each(self, body):
+        def step(block, carry):
+            body(block // 2, lax.rem(block, 2))
+            return carry
+
+        lax.fori_loop(0, 4, step, 0)
 
     def stage_zero(self):
-        start(self.loads)
-        start(self.firsts)
+        start(self.first)
 
     def stage_one(self):
-        own, got = self.own, self.buffers[1]
-        for copy in self.loads:
-            copy.wait()
-        for copy in self.firsts:
+        p, grad, got = self.place, self.grad, self.buffers[0]
+        for copy in self.first:
             copy.wait_recv()
 
-        def body(block, carry):
-            for side in range(2):
-                for low in range(2):
-                    own[side, block, low] = added(own[side, block, low], got[side, block, low])
-            return carry
-
-        lax.fori_loop(0, self.place.depth, body, 0)
+        def body(hi, lo):
+            for x in range(2):
+                grad[hi, lo, x, p.core] = added(grad[hi, lo, x, p.core], got[hi, lo, x])
+
+        self.each(body)
         start(self.second)
 
     def stage_two(self):
-        p, own, head, half = self.place, self.own, self.head, self.half
-        y_one, x_one = self.buffers[2], self.buffers[3]
+        p, grad, head, half = self.place, self.grad, self.head, self.half
+        y_one, x_one = self.buffers[1], self.buffers[2]
+        here = self.side(p.y)
         for copy in self.second:
             copy.wait()
 
-        def body(block, carry):
-            for low in range(2):
-                own[p.y, block, low, 0:head, :] = added(
-                    own[p.y, block, low, 0:head, :], y_one[block, low]
+        def body(hi, lo):
+            for x in range(2):
+                grad[hi, lo, x, p.core, 0:head, here] = added(
+                    grad[hi, lo, x, p.core, 0:head, here], y_one[hi, lo, x]
                 )
             if head < half:
-                for side in range(2):
-                    own[side, block, p.x, head:half, :] = added(
-                        own[side, block, p.x, head:half, :], x_one[side, block]
-                    )
-            return carry
-
-        lax.fori_loop(0, p.depth, body, 0)
+                grad[hi, lo, p.x, p.core, head:half, :] = added(
+                    grad[hi, lo, p.x, p.core, head:half, :], x_one[hi, lo]
+                )
+
+        self.each(body)
         start(self.third)
 
     def stage_three(self):
-        p, own, head, half = self.place, self.own, self.head, self.half
-        x_two, y_two = self.buffers[4], self.buffers[5]
+        p, grad, head, half = self.place, self.grad, self.head, self.half
+        x_two, y_two = self.buffers[3], self.buffers[4]
+        here = self.side(p.y)
         for copy in self.third:
             copy.wait()
 
-        def body(block, carry):
-            own[p.y, block, p.x, 0:head, :] = added(
-                own[p.y, block, p.x, 0:head, :], x_two[block]
+        def body(hi, lo):
+            grad[hi, lo, p.x, p.core, 0:head, here] = added(
+                grad[hi, lo, p.x, p.core, 0:head, here], x_two[hi, lo]
             )
             if head < half:
-                own[p.y, block, p.x, head:half, :] = added(
-                    own[p.y, block, p.x, head:half, :], y_two[block]
+                grad[hi, lo, p.x, p.core, head:half, here] = added(
+                    grad[hi, lo, p.x, p.core, head:half, here], y_two[hi, lo]
                 )
-            return carry
-
-        lax.fori_loop(0, p.depth, body, 0)
-        start(self.fourth)
+
+        self.each(body)
+        start(self.fourth if self.paired else self.fifth)
 
     def stage_four(self):
-        p, z_got = self.place, self.buffers[6]
+        p, grad, z_got = self.place, self.grad, self.buffers[5]
+        here = self.side(p.y)
         for copy in self.fourth:
             copy.wait()
-        total = self.own[p.y, p.z, p.x].astype(F32)
-        for step in range(1, p.depth):
-            total = total + z_got[p.along_z(step)].astype(F32)
+        for hi in range(2):
+            grad[hi, p.lo, p.x, p.core, :, here] = added(
+                grad[hi, p.lo, p.x, p.core, :, here], z_got[hi]
+            )
+        start(self.fifth)
+
+    def stage_five(self):
+        p, z_got = self.place, self.buffers[5]
+        for copy in self.fifth:
+            copy.wait()
+        total = self.grad[p.hi, p.lo, p.x, p.core, :, self.side(p.y)].astype(F32)
+        if self.paired:
+            total = total + z_got[2].astype(F32)
+        else:
+            for step in range(1, 4):
+                total = total + z_got[lax.rem(p.z + step, 4)].astype(F32)
         self.out[p.core] = total.astype(self.out.dtype)
         start(self.last)
 
-    def stage_five(self):
+    def stage_six(self):
         for copy in self.last:
             copy.wait()
-        for copy in self.firsts:
+        for copy in self.first:
             copy.wait_send()
 
 
-def reduction_buffers(count, half, lanes, dtype):
-    depth = count // 2
-    head = first_rows(half, 16)
+def reduction_buffers(half, lanes, head, dtype):
     tail = max(half - head, 16)
     shapes = (
-        (2, depth, 2, half, lanes),
-        (2, depth, 2, half, lanes),
-        (depth, 2, head, lanes),
-        (2, depth, tail, lanes),
-        (depth, head, lanes),
-        (depth, tail, lanes),
-        (depth, half, lanes),
+        (2, 2, 2, half, 2 * lanes),
+        (2, 2, 2, head, lanes),
+        (2, 2, tail, 2 * lanes),
+        (2, 2, head, lanes),
+        (2, 2, tail, lanes),
+        (4, half, lanes),
         (2, half, lanes),
     )
-    return head, [pltpu.VMEM(shape, dtype) for shape in shapes]
-
-
-def backward_kernel(width, heads, *refs):
+    return [pltpu.VMEM(shape, dtype) for shape in shapes]
+
+
+def backward_kernel(width, plan, *refs):
     (
         starts_ref,
         flow_ref,
-        docs_ref,
         got_ref,
         wide_ref,
         lse_ref,
@@ -945,9 +1048,12 @@
         residual_ref,
         bias_ref,
         joint_ref,
-        outer_grad,
-        inner_grad,
-        mixer_grad,
+        d_outer_ref,
+        act_ref,
+        d_inner_ref,
+        first_ref,
+        d_branch_ref,
+        att_ref,
         tokens_out,
         outer_out,
         inner_out,
@@ -965,15 +1071,19 @@
         d_key,
         d_value,
         joint_all,
-        joint_grad,
+        outer_one,
+        outer_two,
+        inner_one,
+        inner_two,
+        mixer_grad,
+        joint_one,
+        joint_two,
         d_turned,
         bias_sum,
         bias_got,
-        bias_z,
         flow_sems,
         home_sems,
         own_sems,
-        load_sem,
         sems,
         z_sems,
         bias_sems,
@@ -987,7 +1097,7 @@
     total_units = MB * H
     p = Place(count)
     me = p.me
-    mine = (total_units - me + count - 1) // count
+    mine = owned(count, me)
 
     barrier = pltpu.get_barrier_semaphore()
 
@@ -998,30 +1108,67 @@
     lax.fori_loop(1, count, greet, 0)
     pl.semaphore_signal(barrier, inc=1, device_id=p.other_core)
     pl.semaphore_signal(barrier, inc=1, device_id=p.other_y)
+    pl.semaphore_signal(barrier, inc=1, device_id={**p.other_y, **p.other_x})
     joint_load = pltpu.make_async_copy(joint_ref, joint_all, own_sems.at[2, 0])
     joint_load.start()
 
-    grads = (outer_grad, inner_grad, mixer_grad, joint_grad)
-    outs = (outer_out, inner_out, mixer_out, joint_out)
+    grads = (outer_one, outer_two, inner_one, inner_two, mixer_grad, joint_one, joint_two)
     jobs = [
         Reduction(
             p,
             j,
             grads[j],
-            buffers[8 * j + 7],
-            heads[j],
-            buffers[8 * j : 8 * j + 7],
-            load_sem,
+            buffers[7 * j + 6],
+            plan[j][2],
+            plan[j][3],
+            buffers[7 * j : 7 * j + 6],
             sems,
             z_sems,
         )
-        for j in range(4)
+        for j in range(len(grads))
     ]
-    outer_job, inner_job, mixer_job, joint_job = jobs
-
-    pl.semaphore_wait(barrier, count + 1)
-    for job in (outer_job, inner_job, mixer_job):
-        job.stage_zero()
+    o_one, o_two, i_one, i_two, m_one, j_one, j_two = jobs
+
+    def store_rows(targets, row, values, columns):
+        half = sum(t.shape[4] for t in targets)
+        done = 0
+        while done < values.shape[0]:
+            block, inside = (row + done) // half, (row + done) % half
+            k = 0
+            while inside >= targets[k].shape[4]:
+                inside -= targets[k].shape[4]
+                k += 1
+            size = min(values.shape[0] - done, targets[k].shape[4] - inside)
+            targets[k][
+                block // 8,
+                block // 4 % 2,
+                block // 2 % 2,
+                block % 2,
+                inside : inside + size,
+                columns,
+            ] = values[done : done + size]
+            done += size
+
+    d_outer_turned = d_outer_ref[...].T
+
+    def outer_gradient(which):
+        for side in range(2):
+            begin = (2 * side + which) * D
+            values = jnp.dot(
+                d_outer_turned, act_ref[:, begin : begin + D], preferred_element_type=F32
+            )
+            columns = slice(side * D, (side + 1) * D)
+            store_rows(((outer_one, outer_two)[which],), 0, values.astype(BF16), columns)
+
+    def inner_gradient():
+        for k in range(FF // D):
+            turned = d_inner_ref[:, k * D : (k + 1) * D].T
+            values = jnp.dot(turned, first_ref[...], preferred_element_type=F32)
+            store_rows((inner_one, inner_two), k * D, values.astype(BF16), slice(0, D))
+
+    def mixer_gradient():
+        values = jnp.dot(d_branch_ref[...].T, att_ref[...], preferred_element_type=F32)
+        store_rows((mixer_grad,), 0, values.astype(BF16), slice(0, D))
 
     def unit_copy(source, target, sem, owner, slot):
         return pltpu.make_async_remote_copy(
@@ -1053,25 +1200,35 @@
             ].T
             for j in range(2):
                 unit = (2 * pair + j) * MB + batch
-                flow_put[unit % count, unit // count] = block[j * HD : (j + 1) * HD]
-
-    def send_flow(unit, carry):
-        owner, slot = lax.rem(unit, count), unit // count
-
-        @pl.when(owner != me)
+                flow_put[owner_of(count, unit), unit // count] = block[j * HD : (j + 1) * HD]
+
+    pl.semaphore_wait(barrier, count + 2)
+
+    def send_flow(turn, carry):
+        slot, owner = turn // count, lax.rem(me + turn, count)
+
+        @pl.when((owner != me) & (slot < owned(count, owner)))
         def _():
             unit_copy(flow_put, flow_got, flow_sems, owner, slot).start()
 
-        @pl.when(owner == me)
+        @pl.when((owner == me) & (slot < mine))
         def _():
             unit_keep(flow_put, flow_got, 0, slot).start()
 
         return carry
 
-    lax.fori_loop(0, total_units, send_flow, 0)
-    outer_job.stage_one()
-    inner_job.stage_one()
-    mixer_job.stage_one()
+    lax.fori_loop(0, units * count, send_flow, 0)
+    bias_sum[0] = bias_ref[...]
+    outer_gradient(0)
+    o_one.stage_zero()
+    outer_gradient(1)
+    o_two.stage_zero()
+    o_one.stage_one()
+    inner_gradient()
+    i_one.stage_zero()
+    i_two.stage_zero()
+    mixer_gradient()
+    m_one.stage_zero()
 
     def unit_step(slot, carry):
         def wait_one(step, inner):
@@ -1085,7 +1242,8 @@
             key_rows[rows, :] = got_ref[i, slot, HD : 2 * HD, :].T
             value_rows[rows, :] = got_ref[i, slot, 2 * HD : 3 * HD, :].T
             key_t[:, rows] = got_ref[i, slot, HD : 2 * HD, :]
-        key_documents(starts_ref, slot, length, lanes, key_docs)
+        batch = batch_of(count, me, slot)
+        key_documents(starts_ref, batch, key_docs)
         d_key[...] = jnp.zeros_like(d_key)
         d_value[...] = jnp.zeros_like(d_value)
 
@@ -1098,7 +1256,7 @@
 
             queries, flow = beside(got_ref), beside(flow_got)
             query_rows, flow_rows = queries.T, flow.T
-            query_docs = docs_ref[slot, :, pl.ds(begin, width)]
+            query_docs = query_documents(starts_ref, batch, begin, width)
             log_total = lse_ref[slot, :, pl.ds(begin, width)]
             spread = jnp.sum(
                 flow.astype(F32) * wide_ref[slot, :, pl.ds(begin, width)], axis=0, keepdims=True
@@ -1137,21 +1295,24 @@
         lax.fori_loop(1, count, send_one, 0)
         unit_keep(put, home_got, 1, slot).start()
 
-        @pl.when(slot == 1)
+        @pl.when(slot == 0)
         def _():
-            outer_job.stage_two()
-
-        @pl.when(slot == 3)
+            o_two.stage_one()
+
+        @pl.when(slot == 2)
         def _():
-            inner_job.stage_two()
+            o_one.stage_two()
+            i_one.stage_one()
 
         return carry
 
     lax.fori_loop(0, mine, unit_step, 0)
-    mixer_job.stage_two()
-    outer_job.stage_three()
-
-    bias_sum[0] = bias_ref[...]
+    o_two.stage_two()
+    i_two.stage_one()
+    o_one.stage_three()
+    i_one.stage_two()
+    m_one.stage_one()
+
     ones = jnp.ones((8, MB * lanes), BF16)
     for pair in range(pairs):
         columns = []
@@ -1159,7 +1320,7 @@
             blocks = []
             for j in range(2):
                 unit = (2 * pair + j) * MB + batch
-                owner, slot = unit % count, unit // count
+                owner, slot = owner_of(count, unit), unit // count
 
                 @pl.when(owner != me)
                 def _():
@@ -1175,104 +1336,113 @@
         d_pair = jnp.concatenate(columns, axis=1)
         d_turned[pair] = d_pair.T
         grad = jnp.dot(d_pair, tok_ref[...], preferred_element_type=F32).astype(BF16)
-        half = joint_grad.shape[3]
         for third in range(3):
-            row, end = third * D + pair * 128, third * D + (pair + 1) * 128
-            while row < end:
-                block, inside = row // half, row % half
-                size = min(end - row, half - inside)
-                taken = row - third * D - pair * 128 + third * 128
-                joint_grad[block // 4, block // 2 % 2, block % 2, inside : inside + size, :] = (
-                    grad[taken : taken + size]
-                )
-                row += size
+            store_rows(
+                (joint_one, joint_two),
+                third * D + pair * 128,
+                grad[third * 128 : (third + 1) * 128],
+                slice(0, D),
+            )
         sums = lax.dot_general(
             ones, d_pair, (((1,), (1,)), ((), ())), preferred_element_type=F32
         )
         bias_sum[0, 0:1, pair * 128 : (pair + 1) * 128] = sums[0:1, 0:128]
         bias_sum[0, 1:2, pair * 128 : (pair + 1) * 128] = sums[0:1, 256:384]
-
-    joint_job.stage_zero()
-
-    def bias_copy(level, peer):
+        if pair == 2:
+            o_two.stage_three()
+            o_one.stage_four()
+            i_two.stage_two()
+            i_one.stage_three()
+
+    m_one.stage_two()
+    o_two.stage_four()
+
+    plane = (p.other_y, p.other_x, {**p.other_y, **p.other_x})
+
+    def bias_copy(level, number, slot, peer):
         return pltpu.make_async_remote_copy(
             src_ref=bias_sum.at[level],
-            dst_ref=bias_got.at[level],
-            send_sem=bias_sems.at[0, level],
-            recv_sem=bias_sems.at[1, level],
+            dst_ref=bias_got.at[slot],
+            send_sem=bias_sems.at[0, number],
+            recv_sem=bias_sems.at[1, number],
             device_id=peer,
         )
 
-    bias_steps = [
-        bias_copy(0, p.other_core),
-        bias_copy(1, p.other_y),
-        bias_copy(2, p.other_x),
+    bias_core = bias_copy(0, 0, 0, p.other_core)
+    bias_plane = [bias_copy(1, 1 + i, 1 + i, peer) for i, peer in enumerate(plane)]
+    bias_z = [
+        bias_copy(2, 3 + step, 3 + step, {"ctx": 2 * lax.rem(p.z + step, 4) + p.x})
+        for step in range(1, 4)
     ]
-    bias_last = [
-        pltpu.make_async_remote_copy(
-            src_ref=bias_sum.at[3],
-            dst_ref=bias_z.at[p.z],
-            send_sem=bias_sems.at[0, 3 + step],
-            recv_sem=bias_sems.at[1, 3 + step],
-            device_id=p.peer_z(step),
-        )
-        for step in range(1, p.depth)
-    ]
-
-    def bias_level(level):
-        bias_steps[level].wait()
-        bias_sum[level + 1] = bias_sum[level] + bias_got[level]
-
-    bias_steps[0].start()
-    inner_job.stage_three()
-    mixer_job.stage_three()
-    joint_job.stage_one()
-    bias_level(0)
-    bias_steps[1].start()
+    bias_core.start()
+    j_one.stage_zero()
+    j_two.stage_zero()
 
     joint_load.wait()
-    total = residual_ref[...]
-    for pair in range(pairs):
-        total = total + lax.dot_general(
-            d_turned[pair],
-            joint_all[pair],
-            (((1,), (1,)), ((), ())),
-            preferred_element_type=F32,
-        )
-    tokens_out[...] = total
-
-    bias_level(1)
-    bias_steps[2].start()
-    joint_job.stage_two()
-    bias_level(2)
-    start(bias_last)
-    outer_job.stage_four()
-    inner_job.stage_four()
-    joint_job.stage_three()
-    mixer_job.stage_four()
-
-    def finish(j):
-        jobs[j].stage_five()
-        whole = buffers[8 * j + 7]
-        lanes_half = whole.shape[2] // 2
-        rows = jnp.concatenate([whole[0], whole[1]], axis=0).astype(F32)
-        rows = jnp.where(p.core == 0, rows[:, :lanes_half], rows[:, lanes_half:])
-        outs[j][...] = rows.T
-
-    finish(0)
-    finish(1)
-    finish(2)
-    for copy in bias_last:
+
+    def token_terms(first, last, total):
+        for pair in range(first, last):
+            total = total + lax.dot_general(
+                d_turned[pair],
+                joint_all[pair],
+                (((1,), (1,)), ((), ())),
+                preferred_element_type=F32,
+            )
+        tokens_out[...] = total
+
+    token_terms(0, pairs // 2, residual_ref[...])
+    bias_core.wait()
+    bias_sum[1] = bias_sum[0] + bias_got[0]
+    start(bias_plane)
+    j_one.stage_one()
+    j_two.stage_one()
+    i_two.stage_three()
+    i_one.stage_four()
+    token_terms(pairs // 2, pairs, tokens_out[...])
+    m_one.stage_three()
+    for copy in bias_plane:
         copy.wait()
-    bias_total = bias_sum[3]
-    for step in range(1, p.depth):
-        bias_total = bias_total + bias_z[p.along_z(step)]
-    bias_out[...] = bias_total
+    bias_sum[2] = bias_sum[1] + bias_got[1] + bias_got[2] + bias_got[3]
+    start(bias_z)
+    j_one.stage_two()
+    i_two.stage_four()
+    j_two.stage_two()
+    m_one.stage_four()
+    j_one.stage_three()
+    j_two.stage_three()
+    o_one.stage_five()
+    o_two.stage_five()
+    i_one.stage_five()
+
+    def parts_of(j):
+        jobs[j].stage_six()
+        whole = buffers[7 * j + 6]
+        return [whole[low].astype(F32) for low in range(2)]
+
+    def own_lanes(rows):
+        width_own = rows.shape[1] // 2
+        return jnp.where(p.core == 0, rows[:, :width_own], rows[:, width_own:])
+
+    def put_out(out, pieces):
+        out[...] = jnp.concatenate(pieces, axis=0).T
+
+    one, two = parts_of(0), parts_of(1)
+    put_out(outer_out, [jnp.where(p.core == 0, a, b) for a, b in zip(one, two)])
+    i_two.stage_five()
+    m_one.stage_five()
+    one, two = parts_of(2), parts_of(3)
+    put_out(inner_out, [own_lanes(r) for r in (one[0], two[0], one[1], two[1])])
+    put_out(mixer_out, [own_lanes(r) for r in parts_of(4)])
+    for copy in bias_z:
+        copy.wait()
+    bias_out[...] = bias_sum[2] + bias_got[4] + bias_got[5] + bias_got[6]
 
     def sent(unit, carry):
-        @pl.when(lax.rem(unit, count) != me)
+        owner, slot = owner_of(count, unit), unit // count
+
+        @pl.when(owner != me)
         def _():
-            unit_copy(flow_put, flow_got, flow_sems, lax.rem(unit, count), unit // count).wait_send()
+            unit_copy(flow_put, flow_got, flow_sems, owner, slot).wait_send()
 
         return carry
 
@@ -1287,12 +1457,14 @@
         return carry
 
     lax.fori_loop(0, mine, returned, 0)
-    joint_job.stage_four()
-    finish(3)
+    j_one.stage_five()
+    j_two.stage_five()
+    one, two = parts_of(5), parts_of(6)
+    put_out(joint_out, [own_lanes(r) for r in (one[0], two[0], one[1], two[1])])
 
 
 def backward(
-    starts, flow, docs, got, wide, lse, source, residual, biases, joint, outer, inner, mixer, number
+    starts, flow, got, wide, lse, source, residual, biases, joint, activations, number
 ):
     count, units, _, lanes = got.shape
     length = count * lanes
@@ -1301,23 +1473,35 @@
     vm = pl.BlockSpec(memory_space=pltpu.VMEM)
     hbm = pl.BlockSpec(memory_space=pl.ANY)
     dma = pltpu.SemaphoreType.DMA
+    small = D // (2 * count)
     half_joint = 3 * D // (2 * count)
-    grads = [g.reshape(count // 2, 2, 2, -1, g.shape[1]) for g in (outer, inner, mixer)]
-    shapes = [(g.shape[3], g.shape[4] // 2) for g in grads] + [(half_joint, D // 2)]
-    heads, buffers = [], []
-    for half, width_half in shapes:
-        head, some = reduction_buffers(count, half, width_half, BF16)
-        heads.append(head)
-        buffers += some
-    outs = [jax.ShapeDtypeStruct((w // 2, 2 * half), F32) for half, w in shapes]
+    early = first_rows(half_joint, 16)
+    plan = (
+        (small, FF // 2, small, True),
+        (small, FF // 2, small, True),
+        (2 * small, D, 4 * small // 3, True),
+        (2 * small, D, 4 * small // 3, True),
+        (small, D, small, True),
+        (early, D, first_rows(early, 16), False),
+        (half_joint - early, D, first_rows(half_joint - early, 16), False),
+    )
+    buffers = []
+    for half, full, head, _ in plan:
+        buffers += reduction_buffers(half, full // 2, head, BF16)
+    outs = [
+        jax.ShapeDtypeStruct((FF // 4, 2 * small), F32),
+        jax.ShapeDtypeStruct((D // 4, FF // count), F32),
+        jax.ShapeDtypeStruct((D // 4, 2 * small), F32),
+        jax.ShapeDtypeStruct((D // 4, 2 * half_joint), F32),
+    ]
     return pl.pallas_call(
-        functools.partial(backward_kernel, width, tuple(heads)),
+        functools.partial(backward_kernel, width, plan),
         out_shape=(
             jax.ShapeDtypeStruct(residual.shape, F32),
             *outs,
             jax.ShapeDtypeStruct((BIAS_ROWS, D), F32),
         ),
-        in_specs=[pl.BlockSpec(memory_space=pltpu.SMEM)] + [vm] * 8 + [hbm] * 4,
+        in_specs=[pl.BlockSpec(memory_space=pltpu.SMEM)] + [vm] * 7 + [hbm] + [vm] * 6,
         out_specs=(vm,) * 6,
         scratch_shapes=[
             pltpu.VMEM((count, units, HD, lanes), BF16),
@@ -1331,25 +1515,23 @@
             pltpu.VMEM((length, HD), F32),
             pltpu.VMEM((length, HD), F32),
             pltpu.VMEM((pairs, D, 384), BF16),
-            pltpu.VMEM((count // 2, 2, 2, half_joint, D), BF16),
+            *[pltpu.VMEM((2, 2, 2, 2, half, full), BF16) for half, full, _, _ in plan],
             pltpu.VMEM((pairs, MB * lanes, 384), BF16),
-            pltpu.VMEM((4, BIAS_ROWS, D), F32),
             pltpu.VMEM((3, BIAS_ROWS, D), F32),
-            pltpu.VMEM((count // 2, BIAS_ROWS, D), F32),
+            pltpu.VMEM((7, BIAS_ROWS, D), F32),
             dma((2, count, units)),
             dma((2, count, units)),
             dma((3, units)),
-            dma((4, 4)),
-            dma((2, 4, 9)),
-            dma((2, 4, count // 2)),
-            dma((2, 3 + count // 2)),
+            dma((2, len(plan), 7)),
+            dma((2, len(plan), 4)),
+            dma((2, 7)),
             *buffers,
         ],
         compiler_params=pltpu.CompilerParams(
-            collective_id=number, has_side_effects=True, vmem_limit_bytes=62 * 1024 * 1024
+            collective_id=number, has_side_effects=True, vmem_limit_bytes=67043328
         ),
         name="backward",
-    )(starts, flow, docs, got, wide, lse, source, residual, biases, joint, *grads)
+    )(starts, flow, got, wide, lse, source, residual, biases, joint, *activations)
 
 
 def on_device(
@@ -1378,46 +1560,39 @@
     me = lax.axis_index("ctx")
 
     part = D // shards
-    vectors = jnp.stack(
-        [
-            query_bias,
-            value_bias,
-            mixer_bias,
-            first_gain,
-            first_shift,
-            outer_bias,
-            second_gain,
-            second_shift,
-        ]
-    )
-    vectors = jnp.pad(vectors, ((0, 8), (0, D - part)))
-    vectors = vectors.at[8].set(inner_bias)
+    vectors = [
+        query_bias,
+        value_bias,
+        mixer_bias,
+        first_gain,
+        first_shift,
+        outer_bias,
+        second_gain,
+        second_shift,
+        inner_bias,
+    ]
     source = tokens.reshape(MB * rows, D)
-    unit_ids = jnp.arange(units, dtype=jnp.int32) * count + me
-    unit_starts = doc_starts[:, 0][lax.rem(unit_ids, MB)]
-    positions = jnp.arange(length, dtype=jnp.int32)
-    unit_docs = jax.vmap(lambda s: doc_index(positions, s))(unit_starts)[:, None, :]
+    batch_starts = doc_starts[:, 0]
 
     attended, received, wide, lse, joint, vectors, mixer, inner, outer = forward(
         count,
-        unit_starts,
+        batch_starts,
         source,
-        unit_docs,
         joint_weight,
-        vectors,
         mixer_weight,
         inner_weight,
         outer_weight,
+        vectors,
         0,
     )
     joint = joint.reshape(H // 2, D, 384)
     mixer, inner, outer = mixer.reshape(D, D), inner.reshape(D, FF), outer.reshape(FF, D)
     heads_of = [
-        vectors[:, i, :part].reshape(D).astype(F32)
+        vectors[:, i, :part].reshape(D)
         for i in range(8)
     ]
     _, _, mbias, gain_one, shift_one, obias, gain_two, shift_two = heads_of
-    ibias = vectors[:, 8].reshape(FF).astype(F32)
+    ibias = vectors[:, 8].reshape(FF)
 
     branch = mul_nn(attended, mixer) + mbias
     first, first_normed, first_recip = norm_forward(
@@ -1437,17 +1612,14 @@
     d_second = norm_backward(incoming, second_normed, second_recip, gain_two)
     d_outer = d_second.astype(BF16)
     return_grad = jnp.sum(d_outer.astype(F32), axis=0)
-    outer_grad = mul_tn(d_outer, activated_low)
     d_inner = (mul_nt(d_outer, outer) * gelu_slope).astype(BF16)
     hidden_grad = jnp.sum(d_inner.astype(F32), axis=0)
-    inner_grad = mul_tn(d_inner, first_low)
     d_first = d_second + mul_nt(d_inner, inner)
     scale_grad = jnp.sum(d_first * first_normed, axis=0)
     shift_grad = jnp.sum(d_first, axis=0)
     d_residual = norm_backward(d_first, first_normed, first_recip, gain_one)
     d_branch = d_residual.astype(BF16)
     mixing_grad = jnp.sum(d_branch.astype(F32), axis=0)
-    mixer_grad = mul_tn(d_branch, attended)
     world = count * shards
     index = me * shards + lax.axis_index("fsdp")
     sums = [
@@ -1459,14 +1631,12 @@
         reshift_grad,
         *hidden_grad.reshape(FF // D, D),
     ]
-    turned = [outer_grad, inner_grad, mixer_grad]
-    if shards == 4 and count % 2 == 0 and D % (32 * count) == 0:
+    if shards == 4 and count == 8:
         flow = mul_nt(d_branch, mixer).astype(BF16)
         biases = jnp.pad(jnp.stack(sums), ((2, BIAS_ROWS - 2 - len(sums)), (0, 0)))
         tokens_grad, *blocks, biases = backward(
-            unit_starts,
+            batch_starts,
             flow,
-            unit_docs,
             received,
             wide,
             lse,
@@ -1474,17 +1644,22 @@
             d_residual,
             biases,
             joint,
-            *[g.astype(BF16) for g in turned],
+            [d_outer, activated_low, d_inner, first_low, d_branch, attended],
             1,
         )
     else:
         natural = joint.reshape(H // 2, D, 3, 128).transpose(1, 2, 0, 3).reshape(D, 3 * D)
         flow = mul_nt(mixer, d_branch).astype(BF16)
         flow_units = exchange(to_units(flow, 1, count, units), 2)
-        d_units = attend_back(received, flow_units, unit_starts, unit_docs, wide, lse)
+        d_units = attend_back(received, flow_units, batch_starts, wide, lse)
         d_joint = from_units(exchange(d_units, 3), 3)
         bias_sums = jnp.sum(d_joint.astype(F32), axis=1)
-        turned.append(mul_nn(d_joint, source))
+        turned = [
+            mul_tn(d_outer, activated_low),
+            mul_tn(d_inner, first_low),
+            mul_tn(d_branch, attended),
+            mul_nn(d_joint, source),
+        ]
         tokens_grad = d_residual + mul_tt(d_joint, natural)
 
         def reduced(grad):

time: 264 us -> 228 us (0.86)
  Pallas kernels: 209 us -> 194 us
  matrix products: 27.5 us -> 14.9 us
  local copies, waits for them, and re-layouts: 19.3 us -> 13.6 us
    pallas_call x1, Pallas kernels: 97.8 us -> 83.6 us  [forward(): pl.pallas_call(functools.partial(forward_kernel, width), out_shape=(jax.S...]
    dot_general x3 -> x0, matrix products: 13 us -> none  [mul_tn(): lax.dot_general(a, b, (((0,), (0,)), ((), ())), preferred_element_type=F32)]
    another operation x10 -> x0, local copies, waits for them, and re-layouts: 5.98 us -> none  [the longest x9 5.3 us: on_device(): jnp.stack([query_bias, value_bias, mixer_bias, first_gain, first_shift, o...]
    unnamed x46 -> x34, local copies, waits for them, and re-layouts: 8.21 us -> 7.68 us
where the time goes in v5:
time: 228 us
  Pallas kernels  194 us (85%)
  matrix products  14.9 us (7%)
  local copies, waits for them, and re-layouts  13.6 us (6%)
  other arithmetic  4.46 us (2%)
    pallas_call x1, Pallas kernels, backward(): pl.pallas_call(functools.partial(backward_kernel, width, plan), out_shape...  110 us
    pallas_call x1, Pallas kernels, forward(): pl.pallas_call(functools.partial(forward_kernel, width), out_shape=(jax.S...  83.6 us
    unnamed x34, local copies, waits for them, and re-layouts  7.68 us
    dot_general x3, matrix products, mul_nt(): lax.dot_general(a, b, (((1,), (1,)), ((), ())), preferred_element_type=F32)  7.44 us
    dot_general x3, matrix products, mul_nn(): return jnp.dot(a, b, preferred_element_type=F32)  7.44 us

profile of v5, /device:TPU:0, one launch (start us, length us, event | category | flops | bytes accessed | tf_op | source)
XLA Modules:
  0.0 228.0 jit_solution(15361147348093212878)
XLA Ops:
  0.7 1.3 copy.36
  1.9 0.0 copy-start
  1.9 0.0 copy-start.5
  1.9 83.6 %forward.1 = (bf16[384,768]{1,0:T(8,128)(2,1)}, bf16[8,5,192,128]{3,2,1,0:T(8,128)(2,1)}, f32[5,64,1024]{2,1,0:T(8,128)}, f32[5,1,1024]{2,1,0:T(1,128)}, bf16[6,...) custom-call(s32[3,8]{1,0:T(4,128)} %bitcast.67, ...), custom_call_target="tpu_custom_call" | custom-call | tf_op jit(solution)/shard_map/forward/pallas_call | solution.py:802
  85.6 0.9 slice.44
  86.5 1.2 slice_reduce_fusion.1
  87.6 0.1 mul.158
  87.7 0.1 mul.147
  87.8 0.1 add.100
  87.9 0.1 add.113
  87.9 0.1 add.108
  88.0 0.1 add.95
  88.1 0.0 copy-done
  88.1 0.3 convert_reduce_fusion.1
  88.4 0.0 copy-done.5
  88.4 0.0 copy-start.10
  88.4 2.3 %fusion.18 = (f32[384]{0:T(512)S(1)}, f32[384,768]{1,0:T(8,128)S(1)}) fusion(f32[768]{0:T(1024)S(1)} %add.95, bf16[384,768]{1,0:T(8,128)(2,1)} %get-tuple-element.30.refs_14_, bf16[768,768]{1,0:T(8,128)(2,1)} %bitcast.76, bf16[384,768]{1,0:T(8,128)(2,1)S(1)} %bitcast.64), kind=kOutput, calls=%fused_computation.66 | convolution fusion | flops 454164096 | bytes 3543552 | tf_op jit(solution)/shard_map/dot_general | solution.py:315
  90.7 0.3 multiply_reduce_fusion.3
  91.0 0.0 slice-start
  91.0 0.3 fusion.15.refs_12_
  91.3 0.0 copy-done.10
  91.3 0.0 copy-start.4
  91.3 0.0 slice-start.1
  91.3 3.0 %multiply_convert_fusion = (bf16[384,3072]{1,0:T(8,128)(2,1)S(1)}, f32[384,3072]{1,0:T(8,128)S(1)}) fusion(f32[3072]{0:T(1024)S(1)} %bitcast.69, bf16[384,768]{1,0:T(8,128)(2,1)S(1)} %fusion.15.refs_12_, bf16[768,3072]{1,0:T(8,128)(2,1)S(1)} %bitcast.70), kind=kOutput, calls=%fused_computation.8 | convolution fusion | flops 1819017216 | bytes 12398592 | tf_op jit(solution)/shard_map/dot_general | solution.py:315
  94.3 0.0 copy-done.4
  94.3 0.0 copy-start.1
  94.3 0.0 slice-done
  94.3 0.0 slice-done.1
  94.4 2.1 fusion.19
  96.5 0.0 copy-done.1
  96.5 0.3 multiply_reduce_fusion.2
  96.8 0.6 fusion.14
  97.4 1.4 convert_reduce_fusion.2
  98.7 0.0 copy-start.3
  98.7 3.6 %convert_reduce_fusion = (f32[3072]{0:T(1024)S(1)}, bf16[384,3072]{1,0:T(8,128)(2,1)S(1)}) fusion(f32[384,3072]{1,0:T(8,128)S(1)} %get-tuple-element.96, bf16[384,768]{1,0:T(8,128)(2,1)S(1)} %get-tuple-element.75.refs_9_, bf16[3072,768]{1,0:T(8,128)(2,1)S(1)} %bitcast.75), kind=kOutput, calls=%fused_computation.7 | convolution fusion | flops 1826092032 | bytes 12398592 | tf_op jit(solution)/shard_map/dot_general | solution.py:323
  102.3 0.0 copy-done.3
  102.3 0.0 copy-start.2
  102.3 2.4 %multiply_reduce_fusion = (f32[768]{0:T(1024)S(1)}, f32[384]{0:T(512)S(1)}, f32[384]{0:T(512)S(1)}, f32[768]{0:T(1024)S(1)}, f32[384,768]{1,0:T(8,128)S(1)}) fusion(f32[384,768]{1,0:T(8,128)S(1)} %get-tuple-element.94, f32[384]{0:T(512)S(1)} %add_rsqrt_fusion.1, f32[384]{0:T(512)S(1)} %broadcast_multiply_fusion.4, f32[768]{0:T(1024)S(1)} %mul.147, ...), kind=kOutput, calls=%fused_computation.29 | convolution fusion | flops 1814886144 | bytes 10632192 | tf_op jit(solution)/shard_map/dot_general | solution.py:323
  104.7 0.0 copy-done.2
  104.8 0.0 copy-start.11
  104.8 1.4 convert_reduce_fusion.3
  106.3 0.0 copy-start.6
  106.3 0.0 copy-done.11
  106.3 1.5 convolution_convert_fusion.refs_1_
  107.8 0.0 copy-done.6
  107.8 0.1 stack.27
  107.9 0.6 pad.4.refs_7_
  108.5 110.4 %backward.1 = (f32[384,768]{1,0:T(8,128)}, f32[768,96]{1,0:T(8,128)}, f32[192,384]{1,0:T(8,128)}, f32[192,96]{1,0:T(8,128)}, f32[192,288]{1,0:T(8,128)}, /*index=5*/f32[16,768]{1,0:T(8,128)}) custom-call(s32[3,8]{1,0:T(4,128)} %bitcast.68, bf16[384,768]{1,0:T(8,128)(2,1)} %convolution_convert_fusion.refs_1_, ...), custom_call_target="tpu_custom_call" | custom-call | tf_op jit(solution)/shard_map/backward/pallas_call | solution.py:1497
  218.9 0.7 slice.49
  219.7 0.7 slice.48
  220.4 0.1 constant_dynamic-slice_fusion
  220.5 0.6 dynamic_slice.7
  221.1 0.5 slice_bitcast_fusion
  221.6 1.9 copy.33
  223.5 0.0 copy-start.8
  223.5 0.0 copy-start.9
  223.5 0.0 copy-start.7
  223.5 2.4 %copy.41 = f32[3,1,128,768]{3,2,1,0:T(8,128)} copy(f32[3,1,128,768]{3,2,1,0:T(8,128)} %bitcast.65) | data formatting | bytes 2359296
  225.9 0.0 copy-done.8
  225.9 0.7 copy.42
  226.6 0.0 copy-done.9
  226.6 0.6 copy.43
  227.3 0.0 copy-done.7
  227.3 0.7 copy.44
  (20 shorter events, 0.1 us)
Async XLA Ops:
  1.9 86.2 %copy-start = (bf16[3,1,128,768]{3,2,1,0:T(8,128)(2,1)S(1)}, bf16[3,1,128,768]{3,2,1,0:T(8,128)(2,1)}, u32[]{:S(2)}) copy-start(bf16[3,1,128,768]{3,2,1,0:T(8,128)(2,1)} %param.31) | copy-start | bytes 1769476
  1.9 86.5 %copy-start.5 = (bf16[3,1,128,768]{3,2,1,0:T(8,128)(2,1)S(1)}, bf16[3,1,128,768]{3,2,1,0:T(8,128)(2,1)}, u32[]{:S(2)}) copy-start(bf16[3,1,128,768]{3,2,1,0:T(8,128)(2,1)} %param.16) | copy-start | bytes 1769476
  88.4 2.9 %copy-start.10 = (bf16[4,192,3072]{2,1,0:T(8,128)(2,1)S(1)}, bf16[4,192,3072]{2,1,0:T(8,128)(2,1)}, u32[]{:S(2)}) copy-start(bf16[4,192,3072]{2,1,0:T(8,128)(2,1)} %get-tuple-element.33) | copy-start | bytes 14155780
  91.0 3.3 %slice-start = ((s8[4718592]{0:T(1024)(128)(4,1)}), s8[4194304]{0:T(1024)(128)(4,1)S(1)}, s32[]{:S(2)}) async-start(s8[4718592]{0:T(1024)(128)(4,1)} %bitcast.72), calls=%async_computation | async-start | bytes 8388608
  91.3 3.0 %copy-start.4 = (bf16[384,768]{1,0:T(8,128)(2,1)}, bf16[384,768]{1,0:T(8,128)(2,1)S(1)}, u32[]{:S(2)}) copy-start(bf16[384,768]{1,0:T(8,128)(2,1)S(1)} %fusion.15.refs_12_) | copy-start | bytes 1769476
  91.3 3.0 %slice-start.1 = ((s8[4718592]{0:T(1024)(128)(4,1)}), s8[524288]{0:T(1024)(128)(4,1)S(1)}, s32[]{:S(2)}) async-start(s8[4718592]{0:T(1024)(128)(4,1)} %bitcast.72), calls=%async_computation.1 | async-start | bytes 1048576
  94.3 2.2 copy-start.1
  98.7 3.6 %copy-start.3 = (bf16[384,768]{1,0:T(8,128)(2,1)}, bf16[384,768]{1,0:T(8,128)(2,1)S(1)}, u32[]{:S(2)}) copy-start(bf16[384,768]{1,0:T(8,128)(2,1)S(1)} %get-tuple-element.75.refs_9_) | copy-start | bytes 1769476
  102.3 2.4 %copy-start.2 = (bf16[384,3072]{1,0:T(8,128)(2,1)}, bf16[384,3072]{1,0:T(8,128)(2,1)S(1)}, u32[]{:S(2)}) copy-start(bf16[384,3072]{1,0:T(8,128)(2,1)S(1)} %get-tuple-element.101.refs_11_) | copy-start | bytes 7077892
  104.8 1.4 copy-start.11
  106.3 1.5 copy-start.6
  223.5 2.4 %copy-start.8 = (f32[192,288]{1,0:T(8,128)S(1)}, f32[192,288]{1,0:T(8,128)}, u32[]{:S(2)}) copy-start(f32[192,288]{1,0:T(8,128)} %get-tuple-element.121) | copy-start | bytes 663556
  223.5 3.1 %copy-start.9 = (f32[192,96]{1,0:T(8,128)S(1)}, f32[192,96]{1,0:T(8,128)}, u32[]{:S(2)}) copy-start(f32[192,96]{1,0:T(8,128)} %get-tuple-element.122) | copy-start | bytes 221188
  223.5 3.8 %copy-start.7 = (f32[192,384]{1,0:T(8,128)S(1)}, f32[192,384]{1,0:T(8,128)}, u32[]{:S(2)}) copy-start(f32[192,384]{1,0:T(8,128)} %get-tuple-element.123) | copy-start | bytes 884740

commit v6 on v5

--- a/solution.py
+++ b/solution.py
@@ -156,8 +156,8 @@
 
 def document(starts_ref, batch, position):
     docs = jnp.zeros(position.shape, jnp.int32) - 1
-    for j in range(starts_ref.shape[1]):
-        docs = docs + jnp.where(position >= starts_ref[batch, j], 1, 0)
+    for j in range(starts_ref.shape[2]):
+        docs = docs + jnp.where(position >= starts_ref[batch, 0, j], 1, 0)
     return docs
 
 
@@ -344,12 +344,14 @@
     wide_ref,
     lse_ref,
     joint_out,
-    vec_out,
+    vec_full,
+    inner_bias_full,
     mixer_out,
     inner_out,
     outer_out,
     joint_all,
     vec_put,
+    vec_out,
     bias_rows,
     put,
     back_put,
@@ -462,18 +464,41 @@
     vec_out[shard] = vec_put[...]
     pl.semaphore_wait(barrier, count + 1)
 
-    vec_y = remote(vec_put, vec_out.at[shard], weight_sems, (0, 0), other_y)
-    vec_core = remote(vec_put, vec_out.at[shard], weight_sems, (0, 1), other_core)
-    vec_pass = remote(vec_out.at[far], vec_out.at[far], weight_sems, (0, 2), other_core)
+    class Vectors:
+        def __init__(self, rows, columns, keys):
+            mine, theirs = vec_out.at[shard, rows, columns], vec_out.at[far, rows, columns]
+            source = vec_put.at[rows, columns]
+            self.over_y = remote(source, mine, weight_sems, keys[0], other_y)
+            self.core = remote(source, mine, weight_sems, keys[1], other_core)
+            self.all = remote(theirs, theirs, weight_sems, keys[2], other_core)
+
+        def begin(self):
+            self.over_y.start()
+            self.core.start()
+
+        def hand_on(self):
+            self.over_y.wait_recv()
+            self.all.start()
+
+        def arrive(self):
+            self.core.wait_recv()
+            self.all.wait_recv()
+
+        def end(self):
+            for copy in (self.over_y, self.core, self.all):
+                copy.wait_send()
+
+    narrow = Vectors(pl.ds(0, 8), pl.ds(0, -(-part // 128) * 128), ((0, 0), (0, 1), (0, 2)))
+    broad = Vectors(pl.ds(8, 8), pl.ds(0, D), ((0, 3), (1, 3), (2, 3)))
     mixer_y = remote(mixer_ref, mixer_out.at[shard], weight_sems, (1, 0), other_y)
     mixer_core = remote(mixer_ref, mixer_out.at[shard], weight_sems, (1, 1), other_core)
     mixer_pass = remote(mixer_out.at[far], mixer_out.at[far], weight_sems, (1, 2), other_core)
     class Relayed:
-        def __init__(self, ref, out, index):
+        def __init__(self, ref, out, index, pieces):
             size = ref.shape[0] // 2
             piece = size // RELAY_PIECES
-            self.over_y, self.over_x = [], []
-            for k in range(RELAY_PIECES):
+            self.over_y, self.over_x, self.rest = [], [], []
+            for k in range(pieces):
                 rows = pl.ds(pl.multiple_of(x * size + k * piece, piece), piece)
                 self.over_y.append(
                     remote(
@@ -486,6 +511,18 @@
                 )
                 passed = out.at[far, rows, :]
                 self.over_x.append(remote(passed, passed, relay_sems, (index, 1, k), other_x))
+            for k in range(2):
+                if pieces < RELAY_PIECES:
+                    rows = pl.ds(k * size + pieces * piece, size - pieces * piece)
+                    self.rest.append(
+                        remote(
+                            ref.at[rows, :],
+                            out.at[shard, rows, :],
+                            relay_sems,
+                            (index, 2, k),
+                            other_y,
+                        )
+                    )
             self.core = remote(ref, out.at[shard], weight_sems, (2 + index, 0), other_core)
             self.all = remote(out.at[far], out.at[far], weight_sems, (2 + index, 1), other_core)
 
@@ -494,25 +531,28 @@
                 copy.start()
             self.core.start()
 
+        def begin_rest(self):
+            for copy in self.rest:
+                copy.start()
+
         def relay(self, k):
             self.over_y[k].wait_recv()
             self.over_x[k].start()
 
         def hand_on(self):
-            for copy in self.over_x:
+            for copy in self.over_x + self.rest:
                 copy.wait_recv()
             self.all.start()
 
         def end(self):
-            for copy in self.over_y + self.over_x:
+            for copy in self.over_y + self.over_x + self.rest:
                 copy.wait_send()
             self.core.wait()
             self.all.wait()
 
-    outer_way = Relayed(outer_ref, outer_out, 0)
-    inner_way = Relayed(inner_ref, inner_out, 1)
-    vec_y.start()
-    vec_core.start()
+    outer_way = Relayed(outer_ref, outer_out, 0, RELAY_PIECES)
+    inner_way = Relayed(inner_ref, inner_out, 1, 1)
+    narrow.begin()
 
     def send_joint(pair, carry):
         each_third(pair, joint_y, "start")
@@ -524,14 +564,14 @@
     inner_way.begin()
     mixer_y.start()
     mixer_core.start()
+    inner_way.begin_rest()
+    broad.begin()
     for first, second in zip(own_in, own_out):
         first.wait()
         second.start()
 
-    vec_y.wait_recv()
-    vec_pass.start()
-    vec_core.wait_recv()
-    vec_pass.wait_recv()
+    narrow.hand_on()
+    narrow.arrive()
 
     def bias_of(slot):
         pieces = [
@@ -703,26 +743,44 @@
             @pl.when(slot == 1)
             def _():
                 outer_way.relay(2)
-                inner_way.relay(0)
 
             @pl.when(slot == 2)
             def _():
-                inner_way.relay(1)
-                inner_way.relay(2)
+                inner_way.relay(0)
 
         return carry
 
     lax.fori_loop(0, mine, unit_step, 0)
 
     if not early:
-        for k in range(RELAY_PIECES):
-            outer_way.relay(k)
-        for k in range(RELAY_PIECES):
-            inner_way.relay(k)
+        outer_way.relay(0)
+        outer_way.relay(1)
+        outer_way.relay(2)
+        inner_way.relay(0)
     mixer_y.wait_recv()
     mixer_pass.start()
     outer_way.hand_on()
+
+    def sent(unit, carry):
+        @pl.when(owner_of(count, unit) != me)
+        def _():
+            send_copy(unit).wait_send()
+
+        return carry
+
+    lax.fori_loop(0, total_units, sent, 0)
+
+    def returned(slot, carry):
+        def one(step, inner):
+            back_copy(lax.rem(me + step, count), slot).wait_send()
+            return inner
+
+        lax.fori_loop(1, count, one, 0)
+        return carry
+
+    lax.fori_loop(0, mine, returned, 0)
     inner_way.hand_on()
+    broad.hand_on()
 
     def home(unit, carry):
         owner, slot = owner_of(count, unit), unit // count
@@ -755,9 +813,14 @@
 
     outer_way.end()
     inner_way.end()
-    vec_y.wait_send()
-    vec_core.wait_send()
-    vec_pass.wait_send()
+    broad.arrive()
+    narrow.end()
+    broad.end()
+    for i in range(8):
+        vec_full[i : i + 1, :] = bias_of(i)
+    vec_full[8:16, :] = jnp.zeros((8, D), F32)
+    for k in range(4):
+        inner_bias_full[:, k * D : (k + 1) * D] = vec_out[k, 8:9, :]
     mixer_y.wait_send()
     mixer_core.wait()
     mixer_pass.wait()
@@ -767,24 +830,6 @@
     for copy in own_out:
         copy.wait()
 
-    def sent(unit, carry):
-        @pl.when(owner_of(count, unit) != me)
-        def _():
-            send_copy(unit).wait_send()
-
-        return carry
-
-    lax.fori_loop(0, total_units, sent, 0)
-
-    def returned(slot, carry):
-        def one(step, inner):
-            back_copy(lax.rem(me + step, count), slot).wait_send()
-            return inner
-
-        lax.fori_loop(1, count, one, 0)
-        return carry
-
-    lax.fori_loop(0, mine, returned, 0)
     for pair in range(pairs):
         joint_store(pair).wait()
 
@@ -807,16 +852,18 @@
             jax.ShapeDtypeStruct((units, HD, length), F32),
             jax.ShapeDtypeStruct((units, 1, length), F32),
             jax.ShapeDtypeStruct((pairs, 4, part, 384), BF16),
-            jax.ShapeDtypeStruct((4, BIAS_ROWS, D), F32),
+            jax.ShapeDtypeStruct((BIAS_ROWS, D), F32),
+            jax.ShapeDtypeStruct((1, FF), F32),
             jax.ShapeDtypeStruct((4, *mixer.shape), BF16),
             jax.ShapeDtypeStruct((4, *inner.shape), BF16),
             jax.ShapeDtypeStruct((4, *outer.shape), BF16),
         ),
         in_specs=[pl.BlockSpec(memory_space=pltpu.SMEM), vm] + [hbm] * 4 + [vm] * 9,
-        out_specs=(vm, vm, vm, vm, hbm, vm, hbm, hbm, hbm),
+        out_specs=(vm, vm, vm, vm, hbm, vm, vm, hbm, hbm, hbm),
         scratch_shapes=[
             pltpu.VMEM((pairs, 4, part, 384), BF16),
             pltpu.VMEM((BIAS_ROWS, D), F32),
+            pltpu.VMEM((4, BIAS_ROWS, D), F32),
             pltpu.VMEM((pairs, 8, 384), F32),
             pltpu.VMEM((count, units, 3 * HD, lanes), BF16),
             pltpu.VMEM((count, units, HD, lanes), BF16),
@@ -833,7 +880,7 @@
             dma((count, units)),
             dma((2, 3, pairs, 3)),
             dma((2, 4, 4)),
-            dma((2, 2, 2, RELAY_PIECES)),
+            dma((2, 2, 3, RELAY_PIECES)),
             dma((3, max(pairs, units, 4), 3)),
         ],
         compiler_params=pltpu.CompilerParams(
@@ -1427,7 +1474,9 @@
         out[...] = jnp.concatenate(pieces, axis=0).T
 
     one, two = parts_of(0), parts_of(1)
-    put_out(outer_out, [jnp.where(p.core == 0, a, b) for a, b in zip(one, two)])
+    outer_out[...] = jnp.concatenate(
+        [jnp.where(p.core == 0, a, b) for a, b in zip(one, two)], axis=0
+    )
     i_two.stage_five()
     m_one.stage_five()
     one, two = parts_of(2), parts_of(3)
@@ -1435,7 +1484,25 @@
     put_out(mixer_out, [own_lanes(r) for r in parts_of(4)])
     for copy in bias_z:
         copy.wait()
-    bias_out[...] = bias_sum[2] + bias_got[4] + bias_got[5] + bias_got[6]
+    bias_total = bias_sum[2] + bias_got[4] + bias_got[5] + bias_got[6]
+    index = me * 4 + p.shard
+    world = 4 * count
+    lane = lax.broadcasted_iota(jnp.int32, (D, 128), 0)
+    place = lax.broadcasted_iota(jnp.int32, (D, 128), 1)
+
+    def picked(rows, first):
+        ones_there = jnp.where(lane == place + first, 1.0, 0.0)
+        return jnp.dot(
+            rows, ones_there, precision=lax.Precision.HIGHEST, preferred_element_type=F32
+        )
+
+    own_hidden = FF // world
+    in_row = D // own_hidden
+    row = lax.broadcasted_iota(jnp.int32, (8, D), 0)
+    hidden = jnp.where(row == index // in_row, bias_total[8:16], 0.0)
+    hidden = jnp.broadcast_to(jnp.sum(hidden, axis=0, keepdims=True), (8, D))
+    bias_out[0:8, :] = picked(bias_total[0:8], index * (D // world))
+    bias_out[8:16, :] = picked(hidden, lax.rem(index, in_row) * own_hidden)
 
     def sent(unit, carry):
         owner, slot = owner_of(count, unit), unit // count
@@ -1489,7 +1556,7 @@
     for half, full, head, _ in plan:
         buffers += reduction_buffers(half, full // 2, head, BF16)
     outs = [
-        jax.ShapeDtypeStruct((FF // 4, 2 * small), F32),
+        jax.ShapeDtypeStruct((2 * small, FF // 4), F32),
         jax.ShapeDtypeStruct((D // 4, FF // count), F32),
         jax.ShapeDtypeStruct((D // 4, 2 * small), F32),
         jax.ShapeDtypeStruct((D // 4, 2 * half_joint), F32),
@@ -1499,7 +1566,7 @@
         out_shape=(
             jax.ShapeDtypeStruct(residual.shape, F32),
             *outs,
-            jax.ShapeDtypeStruct((BIAS_ROWS, D), F32),
+            jax.ShapeDtypeStruct((BIAS_ROWS, 128), F32),
         ),
         in_specs=[pl.BlockSpec(memory_space=pltpu.SMEM)] + [vm] * 7 + [hbm] + [vm] * 6,
         out_specs=(vm,) * 6,
@@ -1534,6 +1601,28 @@
     )(starts, flow, got, wide, lse, source, residual, biases, joint, *activations)
 
 
+def settle_kernel(count, *refs):
+    copies = [
+        pltpu.make_async_copy(refs[i], refs[count + i], refs[2 * count].at[i])
+        for i in range(count)
+    ]
+    start(copies)
+    for copy in copies:
+        copy.wait()
+
+
+def settle(*arrays):
+    count = len(arrays)
+    return pl.pallas_call(
+        functools.partial(settle_kernel, count),
+        out_shape=[jax.ShapeDtypeStruct(a.shape, a.dtype) for a in arrays],
+        in_specs=[pl.BlockSpec(memory_space=pltpu.VMEM)] * count,
+        out_specs=[pl.BlockSpec(memory_space=pl.ANY)] * count,
+        scratch_shapes=[pltpu.SemaphoreType.DMA((count,))],
+        name="settle",
+    )(*arrays)
+
+
 def on_device(
     count,
     shards,
@@ -1572,11 +1661,9 @@
         inner_bias,
     ]
     source = tokens.reshape(MB * rows, D)
-    batch_starts = doc_starts[:, 0]
-
-    attended, received, wide, lse, joint, vectors, mixer, inner, outer = forward(
+    attended, received, wide, lse, joint, vectors, ibias, mixer, inner, outer = forward(
         count,
-        batch_starts,
+        doc_starts,
         source,
         joint_weight,
         mixer_weight,
@@ -1587,12 +1674,9 @@
     )
     joint = joint.reshape(H // 2, D, 384)
     mixer, inner, outer = mixer.reshape(D, D), inner.reshape(D, FF), outer.reshape(FF, D)
-    heads_of = [
-        vectors[:, i, :part].reshape(D)
-        for i in range(8)
+    _, _, mbias, gain_one, shift_one, obias, gain_two, shift_two = [
+        vectors[i : i + 1] for i in range(8)
     ]
-    _, _, mbias, gain_one, shift_one, obias, gain_two, shift_two = heads_of
-    ibias = vectors[:, 8].reshape(FF)
 
     branch = mul_nn(attended, mixer) + mbias
     first, first_normed, first_recip = norm_forward(
@@ -1635,7 +1719,7 @@
         flow = mul_nt(d_branch, mixer).astype(BF16)
         biases = jnp.pad(jnp.stack(sums), ((2, BIAS_ROWS - 2 - len(sums)), (0, 0)))
         tokens_grad, *blocks, biases = backward(
-            batch_starts,
+            doc_starts,
             flow,
             received,
             wide,
@@ -1647,11 +1731,14 @@
             [d_outer, activated_low, d_inner, first_low, d_branch, attended],
             1,
         )
+        tokens_grad, *blocks = settle(tokens_grad, *blocks)
+        blocks[0] = blocks[0].T
+        own, own_hidden = biases[:8, : D // world], biases[8, : FF // world]
     else:
         natural = joint.reshape(H // 2, D, 3, 128).transpose(1, 2, 0, 3).reshape(D, 3 * D)
         flow = mul_nt(mixer, d_branch).astype(BF16)
         flow_units = exchange(to_units(flow, 1, count, units), 2)
-        d_units = attend_back(received, flow_units, batch_starts, wide, lse)
+        d_units = attend_back(received, flow_units, doc_starts, wide, lse)
         d_joint = from_units(exchange(d_units, 3), 3)
         bias_sums = jnp.sum(d_joint.astype(F32), axis=1)
         turned = [
@@ -1672,11 +1759,11 @@
         blocks = [reduced(g) for g in turned]
         biases = jnp.stack([bias_sums[:D], bias_sums[2 * D :], *sums])
         biases = lax.psum(biases, ("ctx", "fsdp"))
+        own = lax.dynamic_slice_in_dim(biases[:8], index * (D // world), D // world, 1)
+        hidden_rows = biases[8 : 8 + FF // D].reshape(FF)
+        own_hidden = lax.dynamic_slice_in_dim(hidden_rows, index * (FF // world), FF // world, 0)
     tokens_grad = tokens_grad.reshape(MB, 1, rows, D)
     outer_out_grad, inner_out, mixer_out, joint_out = blocks
-    own = lax.dynamic_slice_in_dim(biases[:8], index * (D // world), D // world, 1)
-    hidden_rows = biases[8 : 8 + FF // D].reshape(FF)
-    own_hidden = lax.dynamic_slice_in_dim(hidden_rows, index * (FF // world), FF // world, 0)
     sums = [*own[:5], own_hidden, *own[5:]]
     return (result, tokens_grad, joint_out, mixer_out, inner_out, outer_out_grad, *sums)
 

time: 228 us -> 217 us (0.952)
  local copies, waits for them, and re-layouts: 13.6 us -> 3.35 us
    unnamed x34 -> x26, local copies, waits for them, and re-layouts: 7.68 us -> 0.53 us
    pallas_call x1, Pallas kernels: 83.6 us -> 79 us  [forward(): pl.pallas_call(functools.partial(forward_kernel, width), out_shape=(jax.S...]
    pallas_call x0 -> x1, Pallas kernels: none -> 2.92 us  [settle(): pl.pallas_call(functools.partial(settle_kernel, count), out_shape=[jax.Sh...]
    slice x4 -> x1, local copies, waits for them, and re-layouts: 3.54 us -> 1.01 us  [on_device(): vectors[i:i + 1]]
where the time goes in v6:
time: 217 us
  Pallas kernels  193 us (89%)
  matrix products  15.1 us (7%)
  other arithmetic  4.46 us (2%)
  local copies, waits for them, and re-layouts  3.35 us (2%)
    pallas_call x1, Pallas kernels, backward(): pl.pallas_call(functools.partial(backward_kernel, width, plan), out_shape...  111 us
    pallas_call x1, Pallas kernels, forward(): pl.pallas_call(functools.partial(forward_kernel, width), out_shape=(jax.S...  79 us
    dot_general x3, matrix products, mul_nt(): lax.dot_general(a, b, (((1,), (1,)), ((), ())), preferred_element_type=F32)  7.64 us
    dot_general x3, matrix products, mul_nn(): return jnp.dot(a, b, preferred_element_type=F32)  7.48 us

profile of v6, /device:TPU:0, one launch (start us, length us, event | category | flops | bytes accessed | tf_op | source)
XLA Modules:
  0.0 216.6 jit_solution(5976628278046837912)
XLA Ops:
  0.7 0.0 copy-start
  0.7 0.0 copy-start.3
  0.7 79.0 %forward.1 = (bf16[384,768]{1,0:T(8,128)(2,1)}, bf16[8,5,192,128]{3,2,1,0:T(8,128)(2,1)}, f32[5,64,1024]{2,1,0:T(8,128)}, f32[5,1,1024]{2,1,0:T(1,128)}, bf16[6,...) custom-call(s32[3,1,8]{2,1,0:T(1,128)} %refs_0_.3, ...), custom_call_target="tpu_custom_call" | custom-call | tf_op jit(solution)/shard_map/forward/pallas_call | solution.py:847
  79.7 1.0 slice_reduce_fusion.1
  80.7 0.0 copy-done
  80.7 0.3 convert_reduce_fusion.1
  81.0 0.0 copy-done.3
  81.0 0.0 copy-start.8
  81.0 2.3 %fusion.18 = (f32[384]{0:T(512)S(1)}, f32[384,768]{1,0:T(8,128)S(1)}) fusion(f32[768]{0:T(1024)S(1)} %get-tuple-element.85, bf16[384,768]{1,0:T(8,128)(2,1)} %get-tuple-element.36.refs_14_, bf16[768,768]{1,0:T(8,128)(2,1)} %bitcast.72, bf16[384,768]{1,0:T(8,128)(2,1)S(1)} %bitcast.64), kind=kOutput, calls=%fused_computation.65 | convolution fusion | flops 454164096 | bytes 3543552 | tf_op jit(solution)/shard_map/dot_general | solution.py:315
  83.3 0.3 multiply_reduce_fusion.3
  83.6 0.0 copy-start.10
  83.6 0.0 slice-start
  83.6 0.3 fusion.15.refs_12_
  83.9 0.0 copy-done.8
  83.9 0.5 copy-done.10
  84.4 0.0 copy-start.2
  84.4 0.0 slice-start.1
  84.4 3.0 %multiply_convert_fusion = (bf16[384,3072]{1,0:T(8,128)(2,1)S(1)}, f32[384,3072]{1,0:T(8,128)S(1)}) fusion(f32[3072]{0:T(1024)S(1)} %bitcast.76, bf16[384,768]{1,0:T(8,128)(2,1)S(1)} %fusion.15.refs_12_, bf16[768,3072]{1,0:T(8,128)(2,1)S(1)} %bitcast.66), kind=kOutput, calls=%fused_computation.8 | convolution fusion | flops 1819017216 | bytes 12398592 | tf_op jit(solution)/shard_map/dot_general | solution.py:315
  87.4 0.0 copy-done.2
  87.4 0.0 copy-start.5
  87.4 0.0 slice-done
  87.4 0.0 slice-done.1
  87.4 2.2 %fusion.19 = (f32[384]{0:T(512)S(1)}, f32[384,768]{1,0:T(8,128)S(1)}) fusion(f32[768]{0:T(1024)S(1)} %get-tuple-element.82, bf16[384,3072]{1,0:T(8,128)(2,1)S(1)} %get-tuple-element.107.refs_10_, bf16[3072,768]{1,0:T(8,128)(2,1)S(1)} %bitcast.70, f32[768]{0:T(1024)S(1)} %get-tuple-element.83, f32[768]{0:T(1024)S(1)} %get-tuple-element.84, ...), kind=kOutput, calls=%fused_computation.66 | convolution fusion | flops 1814003328 | bytes 9451008 | tf_op jit(solution)/shard_map/dot_general | solution.py:315
  89.6 0.0 copy-done.5
  89.6 0.3 multiply_reduce_fusion.2
  89.9 0.6 fusion.14
  90.5 1.4 convert_reduce_fusion.2
  91.9 0.0 copy-start.1
  91.9 3.7 %convert_reduce_fusion = (f32[3072]{0:T(1024)S(1)}, bf16[384,3072]{1,0:T(8,128)(2,1)S(1)}) fusion(f32[384,3072]{1,0:T(8,128)S(1)} %get-tuple-element.108, bf16[384,768]{1,0:T(8,128)(2,1)S(1)} %get-tuple-element.87.refs_9_, bf16[3072,768]{1,0:T(8,128)(2,1)S(1)} %bitcast.71), kind=kOutput, calls=%fused_computation.7 | convolution fusion | flops 1826092032 | bytes 12398592 | tf_op jit(solution)/shard_map/dot_general | solution.py:323
  95.5 0.0 copy-done.1
  95.5 0.0 copy-start.6
  95.5 2.5 %multiply_reduce_fusion = (f32[768]{0:T(1024)S(1)}, f32[384]{0:T(512)S(1)}, f32[384]{0:T(512)S(1)}, f32[768]{0:T(1024)S(1)}, f32[384,768]{1,0:T(8,128)S(1)}) fusion(f32[384,768]{1,0:T(8,128)S(1)} %get-tuple-element.106, f32[384]{0:T(512)S(1)} %add_rsqrt_fusion.1, f32[384]{0:T(512)S(1)} %broadcast_multiply_fusion.4, f32[768]{0:T(1024)S(1)} %get-tuple-element.84, ...), kind=kOutput, calls=%fused_computation.29 | convolution fusion | flops 1814886144 | bytes 10632192 | tf_op jit(solution)/shard_map/dot_general | solution.py:323
  98.0 0.0 copy-done.6
  98.2 0.0 copy-start.9
  98.2 1.4 convert_reduce_fusion.3
  99.6 0.0 copy-start.4
  99.6 0.0 copy-done.9
  99.6 1.5 convolution_convert_fusion.refs_1_
  101.1 0.0 copy-done.4
  101.1 0.1 stack.27
  101.2 0.6 pad.4.refs_7_
  101.8 110.7 %backward.1 = (f32[384,768]{1,0:T(8,128)}, f32[96,768]{1,0:T(8,128)}, f32[192,384]{1,0:T(8,128)}, f32[192,96]{1,0:T(8,128)}, f32[192,288]{1,0:T(8,128)}, /*index=5*/f32[16,128]{1,0:T(8,128)}) custom-call(s32[3,1,8]{2,1,0:T(1,128)} %refs_0_.3, bf16[384,768]{1,0:T(8,128)(2,1)} %convolution_convert_fusion.refs_1_, ...), custom_call_target="tpu_custom_call" | custom-call | tf_op jit(solution)/shard_map/backward/pallas_call | solution.py:1564
  212.6 0.0 copy-start.7
  212.6 2.9 %settle.1 = (f32[384,768]{1,0:T(8,128)}, f32[96,768]{1,0:T(8,128)}, f32[192,384]{1,0:T(8,128)}, f32[192,96]{1,0:T(8,128)}, f32[192,288]{1,0:T(8,128)}) custom-call(f32[384,768]{1,0:T(8,128)} %get-tuple-element.46.refs_0_, f32[96,768]{1,0:T(8,128)} %get-tuple-element.47.refs_1_, f32[192,384]{1,0:T(8,128)} %get-tuple-element.48.refs_2_, ...), custom_call_target="tpu_custom_call" | custom-call | tf_op jit(solution)/shard_map/settle/pallas_call | solution.py:1616
  215.5 0.0 copy-done.7
  215.5 0.5 slice_bitcast_fusion.3
  216.0 0.5 slice_bitcast_fusion
  (19 shorter events, 0.1 us)
Async XLA Ops:
  0.7 80.0 %copy-start = (bf16[3,1,128,768]{3,2,1,0:T(8,128)(2,1)S(1)}, bf16[3,1,128,768]{3,2,1,0:T(8,128)(2,1)}, u32[]{:S(2)}) copy-start(bf16[3,1,128,768]{3,2,1,0:T(8,128)(2,1)} %param.31) | copy-start | bytes 1769476
  0.7 80.3 %copy-start.3 = (bf16[3,1,128,768]{3,2,1,0:T(8,128)(2,1)S(1)}, bf16[3,1,128,768]{3,2,1,0:T(8,128)(2,1)}, u32[]{:S(2)}) copy-start(bf16[3,1,128,768]{3,2,1,0:T(8,128)(2,1)} %param.16) | copy-start | bytes 1769476
  81.0 2.9 %copy-start.8 = (bf16[4,192,3072]{2,1,0:T(8,128)(2,1)S(1)}, bf16[4,192,3072]{2,1,0:T(8,128)(2,1)}, u32[]{:S(2)}) copy-start(bf16[4,192,3072]{2,1,0:T(8,128)(2,1)} %get-tuple-element.39) | copy-start | bytes 14155780
  83.6 0.8 copy-start.10
  83.6 3.8 %slice-start = ((s8[4718592]{0:T(1024)(128)(4,1)}), s8[4194304]{0:T(1024)(128)(4,1)S(1)}, s32[]{:S(2)}) async-start(s8[4718592]{0:T(1024)(128)(4,1)} %bitcast.68), calls=%async_computation | async-start | bytes 8388608
  84.4 3.0 %copy-start.2 = (bf16[384,768]{1,0:T(8,128)(2,1)}, bf16[384,768]{1,0:T(8,128)(2,1)S(1)}, u32[]{:S(2)}) copy-start(bf16[384,768]{1,0:T(8,128)(2,1)S(1)} %fusion.15.refs_12_) | copy-start | bytes 1769476
  84.4 3.0 %slice-start.1 = ((s8[4718592]{0:T(1024)(128)(4,1)}), s8[524288]{0:T(1024)(128)(4,1)S(1)}, s32[]{:S(2)}) async-start(s8[4718592]{0:T(1024)(128)(4,1)} %bitcast.68), calls=%async_computation.1 | async-start | bytes 1048576
  87.4 2.2 %copy-start.5 = (bf16[384,3072]{1,0:T(8,128)(2,1)}, bf16[384,3072]{1,0:T(8,128)(2,1)S(1)}, u32[]{:S(2)}) copy-start(bf16[384,3072]{1,0:T(8,128)(2,1)S(1)} %get-tuple-element.107.refs_10_) | copy-start | bytes 7077892
  91.9 3.7 %copy-start.1 = (bf16[384,768]{1,0:T(8,128)(2,1)}, bf16[384,768]{1,0:T(8,128)(2,1)S(1)}, u32[]{:S(2)}) copy-start(bf16[384,768]{1,0:T(8,128)(2,1)S(1)} %get-tuple-element.87.refs_9_) | copy-start | bytes 1769476
  95.5 2.5 %copy-start.6 = (bf16[384,3072]{1,0:T(8,128)(2,1)}, bf16[384,3072]{1,0:T(8,128)(2,1)S(1)}, u32[]{:S(2)}) copy-start(bf16[384,3072]{1,0:T(8,128)(2,1)S(1)} %get-tuple-element.113.refs_11_) | copy-start | bytes 7077892
  98.2 1.4 copy-start.9
  99.6 1.5 copy-start.4
  212.6 2.9 %copy-start.7 = (f32[16,128]{1,0:T(8,128)S(1)}, f32[16,128]{1,0:T(8,128)}, u32[]{:S(2)}) copy-start(f32[16,128]{1,0:T(8,128)} %get-tuple-element.56) | copy-start | bytes 24580

commit v7 on v6

--- a/solution.py
+++ b/solution.py
@@ -340,15 +340,18 @@
     vec_refs = refs[:9]
     (
     att_ref,
-    got_ref,
-    wide_ref,
-    lse_ref,
+    got_out,
+    wide_out,
+    lse_out,
     joint_out,
     vec_full,
     inner_bias_full,
     mixer_out,
     inner_out,
     outer_out,
+    got_ref,
+    wide_ref,
+    lse_ref,
     joint_all,
     vec_put,
     vec_out,
@@ -370,6 +373,7 @@
     weight_sems,
     relay_sems,
     own_sems,
+    out_sems,
     ) = refs[9:]
     count, units, _, lanes = got_ref.shape
     length = count * lanes
@@ -626,7 +630,7 @@
                         turned[j * HD : (j + 1) * HD]
                     )
         for i in range(2 * MB):
-            unit = 2 * pair * MB + lax.rem(i + me, 2 * MB)
+            unit = 2 * pair * MB + i
             owner, slot = owner_of(count, unit), unit // count
 
             @pl.when(owner != me)
@@ -666,6 +670,13 @@
 
     early = total_units // count > 2
 
+    def outputs(slot):
+        return (
+            pltpu.make_async_copy(got_ref.at[:, slot], got_out.at[:, slot], out_sems.at[slot, 0]),
+            pltpu.make_async_copy(wide_ref.at[slot], wide_out.at[slot], out_sems.at[slot, 1]),
+            pltpu.make_async_copy(lse_ref.at[slot], lse_out.at[slot], out_sems.at[slot, 2]),
+        )
+
     def unit_step(slot, carry):
         def wait_one(step, inner):
             arrival(lax.rem(me + step, count), slot).wait_recv()
@@ -673,6 +684,7 @@
 
         lax.fori_loop(1, count, wait_one, 0)
         keep_copy(slot).wait()
+        outputs(slot)[0].start()
         for i in range(count):
             rows = slice(i * lanes, (i + 1) * lanes)
             key_rows[rows, :] = got_ref[i, slot, HD : 2 * HD, :].T
@@ -719,7 +731,9 @@
             )
             mixed = mixed / total
             wide_ref[slot, :, pl.ds(begin, width)] = mixed
-            lse_ref[slot, :, pl.ds(begin, width)] = peak + jnp.log(total)
+            lse_ref[slot, :, pl.ds(begin, width)] = jnp.broadcast_to(
+                peak + jnp.log(total), (8, width)
+            )
             low = mixed.astype(BF16)
             for i in range(group):
                 back_put[number * group + i, slot] = low[:, i * lanes : (i + 1) * lanes]
@@ -733,6 +747,7 @@
 
         lax.fori_loop(1, count, send_one, 0)
         back_keep(slot).start()
+        start(outputs(slot)[1:])
         if early:
 
             @pl.when(slot == 0)
@@ -776,6 +791,8 @@
             return inner
 
         lax.fori_loop(1, count, one, 0)
+        for copy in outputs(slot):
+            copy.wait()
         return carry
 
     lax.fori_loop(0, mine, returned, 0)
@@ -850,7 +867,7 @@
             jax.ShapeDtypeStruct(tokens.shape, BF16),
             jax.ShapeDtypeStruct((count, units, 3 * HD, lanes), BF16),
             jax.ShapeDtypeStruct((units, HD, length), F32),
-            jax.ShapeDtypeStruct((units, 1, length), F32),
+            jax.ShapeDtypeStruct((units, 8, length), F32),
             jax.ShapeDtypeStruct((pairs, 4, part, 384), BF16),
             jax.ShapeDtypeStruct((BIAS_ROWS, D), F32),
             jax.ShapeDtypeStruct((1, FF), F32),
@@ -859,8 +876,11 @@
             jax.ShapeDtypeStruct((4, *outer.shape), BF16),
         ),
         in_specs=[pl.BlockSpec(memory_space=pltpu.SMEM), vm] + [hbm] * 4 + [vm] * 9,
-        out_specs=(vm, vm, vm, vm, hbm, vm, vm, hbm, hbm, hbm),
+        out_specs=(vm, hbm, hbm, hbm, hbm, vm, vm, hbm, hbm, hbm),
         scratch_shapes=[
+            pltpu.VMEM((count, units, 3 * HD, lanes), BF16),
+            pltpu.VMEM((units, HD, length), F32),
+            pltpu.VMEM((units, 8, length), F32),
             pltpu.VMEM((pairs, 4, part, 384), BF16),
             pltpu.VMEM((BIAS_ROWS, D), F32),
             pltpu.VMEM((4, BIAS_ROWS, D), F32),
@@ -882,6 +902,7 @@
             dma((2, 4, 4)),
             dma((2, 2, 3, RELAY_PIECES)),
             dma((3, max(pairs, units, 4), 3)),
+            dma((units, 3)),
         ],
         compiler_params=pltpu.CompilerParams(
             collective_id=number, has_side_effects=True, vmem_limit_bytes=56 * 1024 * 1024
@@ -1087,6 +1108,26 @@
 def backward_kernel(width, plan, *refs):
     (
         starts_ref,
+        flow_in,
+        got_in,
+        wide_in,
+        lse_in,
+        tok_in,
+        residual_in,
+        bias_in,
+        joint_in,
+        d_outer_in,
+        act_in,
+        d_inner_in,
+        first_in,
+        d_branch_in,
+        att_in,
+        tokens_out,
+        outer_out,
+        inner_out,
+        mixer_out,
+        joint_out,
+        bias_out,
         flow_ref,
         got_ref,
         wide_ref,
@@ -1094,19 +1135,12 @@
         tok_ref,
         residual_ref,
         bias_ref,
-        joint_ref,
         d_outer_ref,
         act_ref,
         d_inner_ref,
         first_ref,
         d_branch_ref,
         att_ref,
-        tokens_out,
-        outer_out,
-        inner_out,
-        mixer_out,
-        joint_out,
-        bias_out,
         flow_put,
         flow_got,
         put,
@@ -1134,6 +1168,7 @@
         sems,
         z_sems,
         bias_sems,
+        in_sems,
         *buffers,
     ) = refs
     count, units, _, lanes = got_ref.shape
@@ -1146,6 +1181,31 @@
     me = p.me
     mine = owned(count, me)
 
+    sources = (
+        (flow_in, flow_ref),
+        (d_outer_in, d_outer_ref),
+        (act_in, act_ref),
+        (d_inner_in, d_inner_ref),
+        (first_in, first_ref),
+        (d_branch_in, d_branch_ref),
+        (att_in, att_ref),
+        (bias_in, bias_ref),
+        (got_in, got_ref),
+        (wide_in, wide_ref),
+        (lse_in, lse_ref),
+        (tok_in, tok_ref),
+        (residual_in, residual_ref),
+    )
+    loads = [
+        pltpu.make_async_copy(source, held, in_sems.at[k])
+        for k, (source, held) in enumerate(sources)
+    ]
+    start(loads)
+
+    def loaded(first, last):
+        for copy in loads[first:last]:
+            copy.wait()
+
     barrier = pltpu.get_barrier_semaphore()
 
     def greet(step, carry):
@@ -1156,7 +1216,7 @@
     pl.semaphore_signal(barrier, inc=1, device_id=p.other_core)
     pl.semaphore_signal(barrier, inc=1, device_id=p.other_y)
     pl.semaphore_signal(barrier, inc=1, device_id={**p.other_y, **p.other_x})
-    joint_load = pltpu.make_async_copy(joint_ref, joint_all, own_sems.at[2, 0])
+    joint_load = pltpu.make_async_copy(joint_in, joint_all, own_sems.at[2, 0])
     joint_load.start()
 
     grads = (outer_one, outer_two, inner_one, inner_two, mixer_grad, joint_one, joint_two)
@@ -1196,6 +1256,7 @@
             ] = values[done : done + size]
             done += size
 
+    loaded(0, 3)
     d_outer_turned = d_outer_ref[...].T
 
     def outer_gradient(which):
@@ -1249,7 +1310,9 @@
                 unit = (2 * pair + j) * MB + batch
                 flow_put[owner_of(count, unit), unit // count] = block[j * HD : (j + 1) * HD]
 
+    outer_gradient(0)
     pl.semaphore_wait(barrier, count + 2)
+    o_one.stage_zero()
 
     def send_flow(turn, carry):
         slot, owner = turn // count, lax.rem(me + turn, count)
@@ -1265,9 +1328,8 @@
         return carry
 
     lax.fori_loop(0, units * count, send_flow, 0)
+    loaded(3, 8)
     bias_sum[0] = bias_ref[...]
-    outer_gradient(0)
-    o_one.stage_zero()
     outer_gradient(1)
     o_two.stage_zero()
     o_one.stage_one()
@@ -1276,6 +1338,8 @@
     i_two.stage_zero()
     mixer_gradient()
     m_one.stage_zero()
+
+    loaded(8, len(loads))
 
     def unit_step(slot, carry):
         def wait_one(step, inner):
@@ -1304,7 +1368,7 @@
             queries, flow = beside(got_ref), beside(flow_got)
             query_rows, flow_rows = queries.T, flow.T
             query_docs = query_documents(starts_ref, batch, begin, width)
-            log_total = lse_ref[slot, :, pl.ds(begin, width)]
+            log_total = lse_ref[slot, 0:1, pl.ds(begin, width)]
             spread = jnp.sum(
                 flow.astype(F32) * wide_ref[slot, :, pl.ds(begin, width)], axis=0, keepdims=True
             )
@@ -1346,10 +1410,13 @@
         def _():
             o_two.stage_one()
 
+        @pl.when(slot == 1)
+        def _():
+            i_one.stage_one()
+
         @pl.when(slot == 2)
         def _():
             o_one.stage_two()
-            i_one.stage_one()
 
         return carry
 
@@ -1546,8 +1613,8 @@
     plan = (
         (small, FF // 2, small, True),
         (small, FF // 2, small, True),
-        (2 * small, D, 4 * small // 3, True),
-        (2 * small, D, 4 * small // 3, True),
+        (2 * small, D, 2 * small - 16, True),
+        (2 * small, D, 2 * small - 16, True),
         (small, D, small, True),
         (early, D, first_rows(early, 16), False),
         (half_joint - early, D, first_rows(half_joint - early, 16), False),
@@ -1568,9 +1635,13 @@
             *outs,
             jax.ShapeDtypeStruct((BIAS_ROWS, 128), F32),
         ),
-        in_specs=[pl.BlockSpec(memory_space=pltpu.SMEM)] + [vm] * 7 + [hbm] + [vm] * 6,
+        in_specs=[pl.BlockSpec(memory_space=pltpu.SMEM)] + [hbm] * 14,
         out_specs=(vm,) * 6,
         scratch_shapes=[
+            *[
+                pltpu.VMEM(a.shape, a.dtype)
+                for a in (flow, got, wide, lse, source, residual, biases, *activations)
+            ],
             pltpu.VMEM((count, units, HD, lanes), BF16),
             pltpu.VMEM((count, units, HD, lanes), BF16),
             pltpu.VMEM((count, units, 3 * HD, lanes), BF16),
@@ -1592,6 +1663,7 @@
             dma((2, len(plan), 7)),
             dma((2, len(plan), 4)),
             dma((2, 7)),
+            dma((13,)),
             *buffers,
         ],
         compiler_params=pltpu.CompilerParams(
@@ -1738,7 +1810,7 @@
         natural = joint.reshape(H // 2, D, 3, 128).transpose(1, 2, 0, 3).reshape(D, 3 * D)
         flow = mul_nt(mixer, d_branch).astype(BF16)
         flow_units = exchange(to_units(flow, 1, count, units), 2)
-        d_units = attend_back(received, flow_units, doc_starts, wide, lse)
+        d_units = attend_back(received, flow_units, doc_starts, wide, lse[:, :1])
         d_joint = from_units(exchange(d_units, 3), 3)
         bias_sums = jnp.sum(d_joint.astype(F32), axis=1)
         turned = [

time: 217 us -> 203 us (0.935)
  Pallas kernels: 193 us -> 179 us
    pallas_call x1, Pallas kernels: 111 us -> 99.4 us  [backward(): pl.pallas_call(functools.partial(backward_kernel, width, plan), out_shape...]
    pallas_call x1, Pallas kernels: 79 us -> 76.5 us  [forward(): pl.pallas_call(functools.partial(forward_kernel, width), out_shape=(jax.S...]
where the time goes in v7:
time: 203 us
  Pallas kernels  179 us (88%)
  matrix products  15.1 us (7%)
  other arithmetic  4.46 us (2%)
  local copies, waits for them, and re-layouts  3.35 us (2%)
    pallas_call x1, Pallas kernels, backward(): pl.pallas_call(functools.partial(backward_kernel, width, plan), out_shape...  99.4 us
    pallas_call x1, Pallas kernels, forward(): pl.pallas_call(functools.partial(forward_kernel, width), out_shape=(jax.S...  76.5 us
    dot_general x3, matrix products, mul_nt(): lax.dot_general(a, b, (((1,), (1,)), ((), ())), preferred_element_type=F32)  7.64 us
    dot_general x3, matrix products, mul_nn(): return jnp.dot(a, b, preferred_element_type=F32)  7.46 us

profile of v7, /device:TPU:0, one launch (start us, length us, event | category | flops | bytes accessed | tf_op | source)
XLA Modules:
  0.0 202.7 jit_solution(16751011413343705150)
XLA Ops:
  0.7 0.0 copy-start
  0.7 0.0 copy-start.3
  0.7 76.5 %forward.1 = (bf16[384,768]{1,0:T(8,128)(2,1)}, bf16[8,5,192,128]{3,2,1,0:T(8,128)(2,1)}, f32[5,64,1024]{2,1,0:T(8,128)}, f32[5,8,1024]{2,1,0:T(8,128)}, bf16[6,...) custom-call(s32[3,1,8]{2,1,0:T(1,128)} %refs_0_.3, ...), custom_call_target="tpu_custom_call" | custom-call | tf_op jit(solution)/shard_map/forward/pallas_call | solution.py:864
  77.2 1.0 slice_reduce_fusion.1
  78.2 0.0 copy-done
  78.2 0.3 convert_reduce_fusion.1
  78.5 0.0 copy-done.3
  78.5 0.0 copy-start.8
  78.5 2.3 %fusion.18 = (f32[384]{0:T(512)S(1)}, f32[384,768]{1,0:T(8,128)S(1)}) fusion(f32[768]{0:T(1024)S(1)} %get-tuple-element.85, bf16[384,768]{1,0:T(8,128)(2,1)} %get-tuple-element.36.refs_14_, bf16[768,768]{1,0:T(8,128)(2,1)} %bitcast.72, bf16[384,768]{1,0:T(8,128)(2,1)S(1)} %bitcast.64), kind=kOutput, calls=%fused_computation.65 | convolution fusion | flops 454164096 | bytes 3543552 | tf_op jit(solution)/shard_map/dot_general | solution.py:315
  80.9 0.3 multiply_reduce_fusion.3
  81.1 0.0 copy-start.10
  81.2 0.0 slice-start
  81.2 0.3 fusion.15.refs_12_
  81.4 0.0 copy-done.8
  81.4 0.5 copy-done.10
  81.9 0.0 copy-start.2
  81.9 0.0 slice-start.1
  81.9 3.0 %multiply_convert_fusion = (bf16[384,3072]{1,0:T(8,128)(2,1)S(1)}, f32[384,3072]{1,0:T(8,128)S(1)}) fusion(f32[3072]{0:T(1024)S(1)} %bitcast.76, bf16[384,768]{1,0:T(8,128)(2,1)S(1)} %fusion.15.refs_12_, bf16[768,3072]{1,0:T(8,128)(2,1)S(1)} %bitcast.66), kind=kOutput, calls=%fused_computation.8 | convolution fusion | flops 1819017216 | bytes 12398592 | tf_op jit(solution)/shard_map/dot_general | solution.py:315
  84.9 0.0 copy-done.2
  84.9 0.0 copy-start.5
  84.9 0.0 slice-done
  84.9 0.0 slice-done.1
  84.9 2.2 %fusion.19 = (f32[384]{0:T(512)S(1)}, f32[384,768]{1,0:T(8,128)S(1)}) fusion(f32[768]{0:T(1024)S(1)} %get-tuple-element.82, bf16[384,3072]{1,0:T(8,128)(2,1)S(1)} %get-tuple-element.107.refs_10_, bf16[3072,768]{1,0:T(8,128)(2,1)S(1)} %bitcast.70, f32[768]{0:T(1024)S(1)} %get-tuple-element.83, f32[768]{0:T(1024)S(1)} %get-tuple-element.84, ...), kind=kOutput, calls=%fused_computation.66 | convolution fusion | flops 1814003328 | bytes 9451008 | tf_op jit(solution)/shard_map/dot_general | solution.py:315
  87.1 0.0 copy-done.5
  87.1 0.3 multiply_reduce_fusion.2
  87.4 0.6 fusion.14
  88.0 1.4 convert_reduce_fusion.2
  89.4 0.0 copy-start.1
  89.4 3.7 %convert_reduce_fusion = (f32[3072]{0:T(1024)S(1)}, bf16[384,3072]{1,0:T(8,128)(2,1)S(1)}) fusion(f32[384,3072]{1,0:T(8,128)S(1)} %get-tuple-element.108, bf16[384,768]{1,0:T(8,128)(2,1)S(1)} %get-tuple-element.87.refs_9_, bf16[3072,768]{1,0:T(8,128)(2,1)S(1)} %bitcast.71), kind=kOutput, calls=%fused_computation.7 | convolution fusion | flops 1826092032 | bytes 12398592 | tf_op jit(solution)/shard_map/dot_general | solution.py:323
  93.0 0.0 copy-done.1
  93.0 0.0 copy-start.6
  93.1 2.5 %multiply_reduce_fusion = (f32[768]{0:T(1024)S(1)}, f32[384]{0:T(512)S(1)}, f32[384]{0:T(512)S(1)}, f32[768]{0:T(1024)S(1)}, f32[384,768]{1,0:T(8,128)S(1)}) fusion(f32[384,768]{1,0:T(8,128)S(1)} %get-tuple-element.106, f32[384]{0:T(512)S(1)} %add_rsqrt_fusion.1, f32[384]{0:T(512)S(1)} %broadcast_multiply_fusion.4, f32[768]{0:T(1024)S(1)} %get-tuple-element.84, ...), kind=kOutput, calls=%fused_computation.29 | convolution fusion | flops 1814886144 | bytes 10632192 | tf_op jit(solution)/shard_map/dot_general | solution.py:323
  95.5 0.0 copy-done.6
  95.7 0.0 copy-start.9
  95.7 1.4 convert_reduce_fusion.3
  97.1 0.0 copy-start.4
  97.1 0.0 copy-done.9
  97.1 1.5 convolution_convert_fusion.refs_1_
  98.6 0.0 copy-done.4
  98.6 0.1 stack.27
  98.7 0.6 pad.4.refs_7_
  99.3 99.4 %backward.1 = (f32[384,768]{1,0:T(8,128)}, f32[96,768]{1,0:T(8,128)}, f32[192,384]{1,0:T(8,128)}, f32[192,96]{1,0:T(8,128)}, f32[192,288]{1,0:T(8,128)}, /*index=5*/f32[16,128]{1,0:T(8,128)}) custom-call(s32[3,1,8]{2,1,0:T(1,128)} %refs_0_.3, bf16[384,768]{1,0:T(8,128)(2,1)} %convolution_convert_fusion.refs_1_, ...), custom_call_target="tpu_custom_call" | custom-call | tf_op jit(solution)/shard_map/backward/pallas_call | solution.py:1631
  198.7 0.0 copy-start.7
  198.7 2.9 %settle.1 = (f32[384,768]{1,0:T(8,128)}, f32[96,768]{1,0:T(8,128)}, f32[192,384]{1,0:T(8,128)}, f32[192,96]{1,0:T(8,128)}, f32[192,288]{1,0:T(8,128)}) custom-call(f32[384,768]{1,0:T(8,128)} %get-tuple-element.46.refs_0_, f32[96,768]{1,0:T(8,128)} %get-tuple-element.47.refs_1_, f32[192,384]{1,0:T(8,128)} %get-tuple-element.48.refs_2_, ...), custom_call_target="tpu_custom_call" | custom-call | tf_op jit(solution)/shard_map/settle/pallas_call | solution.py:1688
  201.7 0.0 copy-done.7
  201.7 0.5 slice_bitcast_fusion.3
  202.2 0.5 slice_bitcast_fusion
  (19 shorter events, 0.1 us)
Async XLA Ops:
  0.7 77.6 %copy-start = (bf16[3,1,128,768]{3,2,1,0:T(8,128)(2,1)S(1)}, bf16[3,1,128,768]{3,2,1,0:T(8,128)(2,1)}, u32[]{:S(2)}) copy-start(bf16[3,1,128,768]{3,2,1,0:T(8,128)(2,1)} %param.31) | copy-start | bytes 1769476
  0.7 77.9 %copy-start.3 = (bf16[3,1,128,768]{3,2,1,0:T(8,128)(2,1)S(1)}, bf16[3,1,128,768]{3,2,1,0:T(8,128)(2,1)}, u32[]{:S(2)}) copy-start(bf16[3,1,128,768]{3,2,1,0:T(8,128)(2,1)} %param.16) | copy-start | bytes 1769476
  78.5 2.9 %copy-start.8 = (bf16[4,192,3072]{2,1,0:T(8,128)(2,1)S(1)}, bf16[4,192,3072]{2,1,0:T(8,128)(2,1)}, u32[]{:S(2)}) copy-start(bf16[4,192,3072]{2,1,0:T(8,128)(2,1)} %get-tuple-element.39) | copy-start | bytes 14155780
  81.1 0.8 copy-start.10
  81.2 3.8 %slice-start = ((s8[4718592]{0:T(1024)(128)(4,1)}), s8[4194304]{0:T(1024)(128)(4,1)S(1)}, s32[]{:S(2)}) async-start(s8[4718592]{0:T(1024)(128)(4,1)} %bitcast.68), calls=%async_computation | async-start | bytes 8388608
  81.9 3.0 %copy-start.2 = (bf16[384,768]{1,0:T(8,128)(2,1)}, bf16[384,768]{1,0:T(8,128)(2,1)S(1)}, u32[]{:S(2)}) copy-start(bf16[384,768]{1,0:T(8,128)(2,1)S(1)} %fusion.15.refs_12_) | copy-start | bytes 1769476
  81.9 3.0 %slice-start.1 = ((s8[4718592]{0:T(1024)(128)(4,1)}), s8[524288]{0:T(1024)(128)(4,1)S(1)}, s32[]{:S(2)}) async-start(s8[4718592]{0:T(1024)(128)(4,1)} %bitcast.68), calls=%async_computation.1 | async-start | bytes 1048576
  84.9 2.2 %copy-start.5 = (bf16[384,3072]{1,0:T(8,128)(2,1)}, bf16[384,3072]{1,0:T(8,128)(2,1)S(1)}, u32[]{:S(2)}) copy-start(bf16[384,3072]{1,0:T(8,128)(2,1)S(1)} %get-tuple-element.107.refs_10_) | copy-start | bytes 7077892
  89.4 3.7 %copy-start.1 = (bf16[384,768]{1,0:T(8,128)(2,1)}, bf16[384,768]{1,0:T(8,128)(2,1)S(1)}, u32[]{:S(2)}) copy-start(bf16[384,768]{1,0:T(8,128)(2,1)S(1)} %get-tuple-element.87.refs_9_) | copy-start | bytes 1769476
  93.0 2.5 %copy-start.6 = (bf16[384,3072]{1,0:T(8,128)(2,1)}, bf16[384,3072]{1,0:T(8,128)(2,1)S(1)}, u32[]{:S(2)}) copy-start(bf16[384,3072]{1,0:T(8,128)(2,1)S(1)} %get-tuple-element.113.refs_11_) | copy-start | bytes 7077892
  95.7 1.4 copy-start.9
  97.1 1.5 copy-start.4
  198.7 2.9 %copy-start.7 = (f32[16,128]{1,0:T(8,128)S(1)}, f32[16,128]{1,0:T(8,128)}, u32[]{:S(2)}) copy-start(f32[16,128]{1,0:T(8,128)} %get-tuple-element.56) | copy-start | bytes 24580

commit v8 on v7

--- a/solution.py
+++ b/solution.py
@@ -330,7 +330,7 @@
 def forward_kernel(
     width,
     starts_ref,
-    tok_ref,
+    tok_in,
     joint_ref,
     mixer_ref,
     inner_ref,
@@ -339,7 +339,7 @@
 ):
     vec_refs = refs[:9]
     (
-    att_ref,
+    att_out,
     got_out,
     wide_out,
     lse_out,
@@ -349,6 +349,8 @@
     mixer_out,
     inner_out,
     outer_out,
+    tok_ref,
+    att_ref,
     got_ref,
     wide_ref,
     lse_ref,
@@ -374,6 +376,7 @@
     relay_sems,
     own_sems,
     out_sems,
+    row_sems,
     ) = refs[9:]
     count, units, _, lanes = got_ref.shape
     length = count * lanes
@@ -451,6 +454,8 @@
 
         lax.fori_loop(0, pairs, body, 0)
 
+    tok_load = pltpu.make_async_copy(tok_in, tok_ref, row_sems.at[MB])
+    tok_load.start()
     every_pair(own_joint, "start")
     wholes = ((mixer_ref, mixer_own, mixer_out), (inner_ref, inner_own, inner_out), (outer_ref, outer_own, outer_out))
     own_in = [
@@ -576,6 +581,7 @@
 
     narrow.hand_on()
     narrow.arrive()
+    tok_load.wait()
 
     def bias_of(slot):
         pieces = [
@@ -819,14 +825,19 @@
         return carry
 
     lax.fori_loop(0, total_units, home, 0)
-    for pair in range(pairs):
-        for batch in range(MB):
+    att_stores = []
+    for batch in range(MB):
+        rows = slice(batch * lanes, (batch + 1) * lanes)
+        for pair in range(pairs):
             tops = []
             for j in range(2):
                 unit = (2 * pair + j) * MB + batch
                 tops.append(back_got[owner_of(count, unit), unit // count])
-            block = jnp.concatenate(tops, axis=0).T
-            att_ref[batch * lanes : (batch + 1) * lanes, pair * 128 : (pair + 1) * 128] = block
+            att_ref[rows, pair * 128 : (pair + 1) * 128] = jnp.concatenate(tops, axis=0).T
+        att_stores.append(
+            pltpu.make_async_copy(att_ref.at[rows, :], att_out.at[rows, :], row_sems.at[batch])
+        )
+        att_stores[-1].start()
 
     outer_way.end()
     inner_way.end()
@@ -847,6 +858,8 @@
     for copy in own_out:
         copy.wait()
 
+    for copy in att_stores:
+        copy.wait()
     for pair in range(pairs):
         joint_store(pair).wait()
 
@@ -875,9 +888,11 @@
             jax.ShapeDtypeStruct((4, *inner.shape), BF16),
             jax.ShapeDtypeStruct((4, *outer.shape), BF16),
         ),
-        in_specs=[pl.BlockSpec(memory_space=pltpu.SMEM), vm] + [hbm] * 4 + [vm] * 9,
-        out_specs=(vm, hbm, hbm, hbm, hbm, vm, vm, hbm, hbm, hbm),
+        in_specs=[pl.BlockSpec(memory_space=pltpu.SMEM)] + [hbm] * 5 + [vm] * 9,
+        out_specs=(hbm, hbm, hbm, hbm, hbm, vm, vm, hbm, hbm, hbm),
         scratch_shapes=[
+            pltpu.VMEM(tokens.shape, BF16),
+            pltpu.VMEM(tokens.shape, BF16),
             pltpu.VMEM((count, units, 3 * HD, lanes), BF16),
             pltpu.VMEM((units, HD, length), F32),
             pltpu.VMEM((units, 8, length), F32),
@@ -903,6 +918,7 @@
             dma((2, 2, 3, RELAY_PIECES)),
             dma((3, max(pairs, units, 4), 3)),
             dma((units, 3)),
+            dma((MB + 1,)),
         ],
         compiler_params=pltpu.CompilerParams(
             collective_id=number, has_side_effects=True, vmem_limit_bytes=56 * 1024 * 1024
@@ -1122,12 +1138,16 @@
         first_in,
         d_branch_in,
         att_in,
+        tokens_hbm,
+        outer_hbm,
+        inner_hbm,
+        mixer_hbm,
+        joint_out,
+        bias_out,
         tokens_out,
         outer_out,
         inner_out,
         mixer_out,
-        joint_out,
-        bias_out,
         flow_ref,
         got_ref,
         wide_ref,
@@ -1169,6 +1189,7 @@
         z_sems,
         bias_sems,
         in_sems,
+        result_sems,
         *buffers,
     ) = refs
     count, units, _, lanes = got_ref.shape
@@ -1513,6 +1534,18 @@
     i_two.stage_three()
     i_one.stage_four()
     token_terms(pairs // 2, pairs, tokens_out[...])
+    results = [
+        pltpu.make_async_copy(held, out, result_sems.at[k])
+        for k, (held, out) in enumerate(
+            (
+                (tokens_out, tokens_hbm),
+                (outer_out, outer_hbm),
+                (inner_out, inner_hbm),
+                (mixer_out, mixer_hbm),
+            )
+        )
+    ]
+    results[0].start()
     m_one.stage_three()
     for copy in bias_plane:
         copy.wait()
@@ -1544,11 +1577,14 @@
     outer_out[...] = jnp.concatenate(
         [jnp.where(p.core == 0, a, b) for a, b in zip(one, two)], axis=0
     )
+    results[1].start()
     i_two.stage_five()
     m_one.stage_five()
     one, two = parts_of(2), parts_of(3)
     put_out(inner_out, [own_lanes(r) for r in (one[0], two[0], one[1], two[1])])
+    results[2].start()
     put_out(mixer_out, [own_lanes(r) for r in parts_of(4)])
+    results[3].start()
     for copy in bias_z:
         copy.wait()
     bias_total = bias_sum[2] + bias_got[4] + bias_got[5] + bias_got[6]
@@ -1595,6 +1631,8 @@
     j_two.stage_five()
     one, two = parts_of(5), parts_of(6)
     put_out(joint_out, [own_lanes(r) for r in (one[0], two[0], one[1], two[1])])
+    for copy in results:
+        copy.wait()
 
 
 def backward(
@@ -1636,8 +1674,10 @@
             jax.ShapeDtypeStruct((BIAS_ROWS, 128), F32),
         ),
         in_specs=[pl.BlockSpec(memory_space=pltpu.SMEM)] + [hbm] * 14,
-        out_specs=(vm,) * 6,
+        out_specs=(hbm,) * 4 + (vm,) * 2,
         scratch_shapes=[
+            pltpu.VMEM(residual.shape, F32),
+            *[pltpu.VMEM(o.shape, F32) for o in outs[:3]],
             *[
                 pltpu.VMEM(a.shape, a.dtype)
                 for a in (flow, got, wide, lse, source, residual, biases, *activations)
@@ -1664,6 +1704,7 @@
             dma((2, len(plan), 4)),
             dma((2, 7)),
             dma((13,)),
+            dma((4,)),
             *buffers,
         ],
         compiler_params=pltpu.CompilerParams(
@@ -1674,12 +1715,17 @@
 
 
 def settle_kernel(count, *refs):
-    copies = [
-        pltpu.make_async_copy(refs[i], refs[count + i], refs[2 * count].at[i])
-        for i in range(count)
+    sources, outs, held = refs[:count], refs[count : 2 * count], refs[2 * count : 3 * count]
+    sems = refs[3 * count]
+    copies_in = [
+        pltpu.make_async_copy(sources[i], held[i], sems.at[0, i]) for i in range(count)
     ]
-    start(copies)
-    for copy in copies:
+    copies_out = [pltpu.make_async_copy(held[i], outs[i], sems.at[1, i]) for i in range(count)]
+    start(copies_in)
+    for first, second in zip(copies_in, copies_out):
+        first.wait()
+        second.start()
+    for copy in copies_out:
         copy.wait()
 
 
@@ -1688,9 +1734,12 @@
     return pl.pallas_call(
         functools.partial(settle_kernel, count),
         out_shape=[jax.ShapeDtypeStruct(a.shape, a.dtype) for a in arrays],
-        in_specs=[pl.BlockSpec(memory_space=pltpu.VMEM)] * count,
+        in_specs=[pl.BlockSpec(memory_space=pl.ANY)] * count,
         out_specs=[pl.BlockSpec(memory_space=pl.ANY)] * count,
-        scratch_shapes=[pltpu.SemaphoreType.DMA((count,))],
+        scratch_shapes=[
+            *[pltpu.VMEM(a.shape, a.dtype) for a in arrays],
+            pltpu.SemaphoreType.DMA((2, count)),
+        ],
         name="settle",
     )(*arrays)
 
@@ -1803,7 +1852,7 @@
             [d_outer, activated_low, d_inner, first_low, d_branch, attended],
             1,
         )
-        tokens_grad, *blocks = settle(tokens_grad, *blocks)
+        *blocks, tokens_grad = settle(*blocks, tokens_grad)
         blocks[0] = blocks[0].T
         own, own_hidden = biases[:8, : D // world], biases[8, : FF // world]
     else:

time: 203 us -> 202 us (level)
  no operation moved by 1% of the time
where the time goes in v8:
time: 202 us; the launch traced here: 201 us
  Pallas kernels  178 us (88%)
  matrix products  15.1 us (7%)
  other arithmetic  4.46 us (2%)
  local copies, waits for them, and re-layouts  3.35 us (2%)
    pallas_call x1, Pallas kernels, backward(): pl.pallas_call(functools.partial(backward_kernel, width, plan), out_shape...  99 us
    pallas_call x1, Pallas kernels, forward(): pl.pallas_call(functools.partial(forward_kernel, width), out_shape=(jax.S...  76 us
    dot_general x3, matrix products, mul_nt(): lax.dot_general(a, b, (((1,), (1,)), ((), ())), preferred_element_type=F32)  7.64 us
    dot_general x3, matrix products, mul_nn(): return jnp.dot(a, b, preferred_element_type=F32)  7.47 us

profile of v8, /device:TPU:0, one launch (start us, length us, event | category | flops | bytes accessed | tf_op | source)
XLA Modules:
  0.0 201.5 jit_solution(8800603901928691160)
XLA Ops:
  0.7 0.0 copy-start
  0.7 0.0 copy-start.3
  0.7 76.0 %forward.1 = (bf16[384,768]{1,0:T(8,128)(2,1)}, bf16[8,5,192,128]{3,2,1,0:T(8,128)(2,1)}, f32[5,64,1024]{2,1,0:T(8,128)}, f32[5,8,1024]{2,1,0:T(8,128)}, bf16[6,...) custom-call(s32[3,1,8]{2,1,0:T(1,128)} %refs_0_.3, ...), custom_call_target="tpu_custom_call" | custom-call | tf_op jit(solution)/shard_map/forward/pallas_call | solution.py:877
  76.6 1.0 slice_reduce_fusion.1
  77.7 0.0 copy-done
  77.7 0.3 convert_reduce_fusion.1
  78.0 0.0 copy-done.3
  78.0 0.0 copy-start.8
  78.0 2.3 %fusion.18 = (f32[384]{0:T(512)S(1)}, f32[384,768]{1,0:T(8,128)S(1)}) fusion(f32[768]{0:T(1024)S(1)} %get-tuple-element.85, bf16[384,768]{1,0:T(8,128)(2,1)} %get-tuple-element.36.refs_14_, bf16[768,768]{1,0:T(8,128)(2,1)} %bitcast.72, bf16[384,768]{1,0:T(8,128)(2,1)S(1)} %bitcast.64), kind=kOutput, calls=%fused_computation.65 | convolution fusion | flops 454164096 | bytes 3543552 | tf_op jit(solution)/shard_map/dot_general | solution.py:315
  80.3 0.3 multiply_reduce_fusion.3
  80.6 0.0 copy-start.10
  80.6 0.0 slice-start
  80.6 0.3 fusion.15.refs_12_
  80.9 0.0 copy-done.8
  80.9 0.5 copy-done.10
  81.4 0.0 copy-start.2
  81.4 0.0 slice-start.1
  81.4 3.0 %multiply_convert_fusion = (bf16[384,3072]{1,0:T(8,128)(2,1)S(1)}, f32[384,3072]{1,0:T(8,128)S(1)}) fusion(f32[3072]{0:T(1024)S(1)} %bitcast.76, bf16[384,768]{1,0:T(8,128)(2,1)S(1)} %fusion.15.refs_12_, bf16[768,3072]{1,0:T(8,128)(2,1)S(1)} %bitcast.66), kind=kOutput, calls=%fused_computation.8 | convolution fusion | flops 1819017216 | bytes 12398592 | tf_op jit(solution)/shard_map/dot_general | solution.py:315
  84.3 0.0 copy-done.2
  84.3 0.0 copy-start.5
  84.4 0.0 slice-done
  84.4 0.0 slice-done.1
  84.4 2.2 %fusion.19 = (f32[384]{0:T(512)S(1)}, f32[384,768]{1,0:T(8,128)S(1)}) fusion(f32[768]{0:T(1024)S(1)} %get-tuple-element.82, bf16[384,3072]{1,0:T(8,128)(2,1)S(1)} %get-tuple-element.107.refs_10_, bf16[3072,768]{1,0:T(8,128)(2,1)S(1)} %bitcast.70, f32[768]{0:T(1024)S(1)} %get-tuple-element.83, f32[768]{0:T(1024)S(1)} %get-tuple-element.84, ...), kind=kOutput, calls=%fused_computation.66 | convolution fusion | flops 1814003328 | bytes 9451008 | tf_op jit(solution)/shard_map/dot_general | solution.py:315
  86.6 0.0 copy-done.5
  86.6 0.3 multiply_reduce_fusion.2
  86.9 0.6 fusion.14
  87.5 1.4 convert_reduce_fusion.2
  88.8 0.0 copy-start.1
  88.8 3.7 %convert_reduce_fusion = (f32[3072]{0:T(1024)S(1)}, bf16[384,3072]{1,0:T(8,128)(2,1)S(1)}) fusion(f32[384,3072]{1,0:T(8,128)S(1)} %get-tuple-element.108, bf16[384,768]{1,0:T(8,128)(2,1)S(1)} %get-tuple-element.87.refs_9_, bf16[3072,768]{1,0:T(8,128)(2,1)S(1)} %bitcast.71), kind=kOutput, calls=%fused_computation.7 | convolution fusion | flops 1826092032 | bytes 12398592 | tf_op jit(solution)/shard_map/dot_general | solution.py:323
  92.5 0.0 copy-done.1
  92.5 0.0 copy-start.6
  92.5 2.5 %multiply_reduce_fusion = (f32[768]{0:T(1024)S(1)}, f32[384]{0:T(512)S(1)}, f32[384]{0:T(512)S(1)}, f32[768]{0:T(1024)S(1)}, f32[384,768]{1,0:T(8,128)S(1)}) fusion(f32[384,768]{1,0:T(8,128)S(1)} %get-tuple-element.106, f32[384]{0:T(512)S(1)} %add_rsqrt_fusion.1, f32[384]{0:T(512)S(1)} %broadcast_multiply_fusion.4, f32[768]{0:T(1024)S(1)} %get-tuple-element.84, ...), kind=kOutput, calls=%fused_computation.29 | convolution fusion | flops 1814886144 | bytes 10632192 | tf_op jit(solution)/shard_map/dot_general | solution.py:323
  95.0 0.0 copy-done.6
  95.1 0.0 copy-start.9
  95.1 1.4 convert_reduce_fusion.3
  96.5 0.0 copy-start.4
  96.5 0.0 copy-done.9
  96.5 1.5 convolution_convert_fusion.refs_1_
  98.0 0.0 copy-done.4
  98.0 0.1 stack.27
  98.1 0.6 pad.4.refs_7_
  98.8 99.0 %backward.1 = (f32[384,768]{1,0:T(8,128)}, f32[96,768]{1,0:T(8,128)}, f32[192,384]{1,0:T(8,128)}, f32[192,96]{1,0:T(8,128)}, f32[192,288]{1,0:T(8,128)}, /*index=5*/f32[16,128]{1,0:T(8,128)}) custom-call(s32[3,1,8]{2,1,0:T(1,128)} %refs_0_.3, bf16[384,768]{1,0:T(8,128)(2,1)} %convolution_convert_fusion.refs_1_, ...), custom_call_target="tpu_custom_call" | custom-call | tf_op jit(solution)/shard_map/backward/pallas_call | solution.py:1669
  197.7 0.0 copy-start.7
  197.7 2.7 %settle.1 = (f32[96,768]{1,0:T(8,128)}, f32[192,384]{1,0:T(8,128)}, f32[192,96]{1,0:T(8,128)}, f32[192,288]{1,0:T(8,128)}, f32[384,768]{1,0:T(8,128)}) custom-call(f32[96,768]{1,0:T(8,128)} %get-tuple-element.46.refs_0_, f32[192,384]{1,0:T(8,128)} %get-tuple-element.47.refs_1_, f32[192,96]{1,0:T(8,128)} %get-tuple-element.48.refs_2_, ...), custom_call_target="tpu_custom_call" | custom-call | tf_op jit(solution)/shard_map/settle/pallas_call | solution.py:1734
  200.4 0.0 copy-done.7
  200.4 0.5 slice_bitcast_fusion.3
  200.9 0.5 slice_bitcast_fusion
  (19 shorter events, 0.1 us)
Async XLA Ops:
  0.7 77.0 %copy-start = (bf16[3,1,128,768]{3,2,1,0:T(8,128)(2,1)S(1)}, bf16[3,1,128,768]{3,2,1,0:T(8,128)(2,1)}, u32[]{:S(2)}) copy-start(bf16[3,1,128,768]{3,2,1,0:T(8,128)(2,1)} %param.31) | copy-start | bytes 1769476
  0.7 77.3 %copy-start.3 = (bf16[3,1,128,768]{3,2,1,0:T(8,128)(2,1)S(1)}, bf16[3,1,128,768]{3,2,1,0:T(8,128)(2,1)}, u32[]{:S(2)}) copy-start(bf16[3,1,128,768]{3,2,1,0:T(8,128)(2,1)} %param.16) | copy-start | bytes 1769476
  78.0 2.9 %copy-start.8 = (bf16[4,192,3072]{2,1,0:T(8,128)(2,1)S(1)}, bf16[4,192,3072]{2,1,0:T(8,128)(2,1)}, u32[]{:S(2)}) copy-start(bf16[4,192,3072]{2,1,0:T(8,128)(2,1)} %get-tuple-element.39) | copy-start | bytes 14155780
  80.6 0.8 copy-start.10
  80.6 3.8 %slice-start = ((s8[4718592]{0:T(1024)(128)(4,1)}), s8[4194304]{0:T(1024)(128)(4,1)S(1)}, s32[]{:S(2)}) async-start(s8[4718592]{0:T(1024)(128)(4,1)} %bitcast.68), calls=%async_computation | async-start | bytes 8388608
  81.4 3.0 %copy-start.2 = (bf16[384,768]{1,0:T(8,128)(2,1)}, bf16[384,768]{1,0:T(8,128)(2,1)S(1)}, u32[]{:S(2)}) copy-start(bf16[384,768]{1,0:T(8,128)(2,1)S(1)} %fusion.15.refs_12_) | copy-start | bytes 1769476
  81.4 3.0 %slice-start.1 = ((s8[4718592]{0:T(1024)(128)(4,1)}), s8[524288]{0:T(1024)(128)(4,1)S(1)}, s32[]{:S(2)}) async-start(s8[4718592]{0:T(1024)(128)(4,1)} %bitcast.68), calls=%async_computation.1 | async-start | bytes 1048576
  84.3 2.2 %copy-start.5 = (bf16[384,3072]{1,0:T(8,128)(2,1)}, bf16[384,3072]{1,0:T(8,128)(2,1)S(1)}, u32[]{:S(2)}) copy-start(bf16[384,3072]{1,0:T(8,128)(2,1)S(1)} %get-tuple-element.107.refs_10_) | copy-start | bytes 7077892
  88.8 3.7 %copy-start.1 = (bf16[384,768]{1,0:T(8,128)(2,1)}, bf16[384,768]{1,0:T(8,128)(2,1)S(1)}, u32[]{:S(2)}) copy-start(bf16[384,768]{1,0:T(8,128)(2,1)S(1)} %get-tuple-element.87.refs_9_) | copy-start | bytes 1769476
  92.5 2.5 %copy-start.6 = (bf16[384,3072]{1,0:T(8,128)(2,1)}, bf16[384,3072]{1,0:T(8,128)(2,1)S(1)}, u32[]{:S(2)}) copy-start(bf16[384,3072]{1,0:T(8,128)(2,1)S(1)} %get-tuple-element.113.refs_11_) | copy-start | bytes 7077892
  95.1 1.4 copy-start.9
  96.5 1.5 copy-start.4
  197.7 2.7 %copy-start.7 = (f32[16,128]{1,0:T(8,128)S(1)}, f32[16,128]{1,0:T(8,128)}, u32[]{:S(2)}) copy-start(f32[16,128]{1,0:T(8,128)} %get-tuple-element.56) | copy-start | bytes 24580

commit v9 on v8

--- a/solution.py
+++ b/solution.py
@@ -571,9 +571,9 @@
     lax.fori_loop(0, pairs, send_joint, 0)
     outer_way.begin()
     inner_way.begin()
+    inner_way.begin_rest()
     mixer_y.start()
     mixer_core.start()
-    inner_way.begin_rest()
     broad.begin()
     for first, second in zip(own_in, own_out):
         first.wait()
@@ -778,8 +778,6 @@
         outer_way.relay(1)
         outer_way.relay(2)
         inner_way.relay(0)
-    mixer_y.wait_recv()
-    mixer_pass.start()
     outer_way.hand_on()
 
     def sent(unit, carry):
@@ -803,6 +801,8 @@
 
     lax.fori_loop(0, mine, returned, 0)
     inner_way.hand_on()
+    mixer_y.wait_recv()
+    mixer_pass.start()
     broad.hand_on()
 
     def home(unit, carry):

time: 202 us -> 202 us (level)
  no operation moved by 1% of the time
where the time goes in v9:
time: 202 us; the launch traced here: 201 us
  Pallas kernels  178 us (88%)
  matrix products  15.1 us (7%)
  other arithmetic  4.46 us (2%)
  local copies, waits for them, and re-layouts  3.35 us (2%)
    pallas_call x1, Pallas kernels, backward(): pl.pallas_call(functools.partial(backward_kernel, width, plan), out_shape...  99.4 us
    pallas_call x1, Pallas kernels, forward(): pl.pallas_call(functools.partial(forward_kernel, width), out_shape=(jax.S...  75.5 us
    dot_general x3, matrix products, mul_nt(): lax.dot_general(a, b, (((1,), (1,)), ((), ())), preferred_element_type=F32)  7.64 us
    dot_general x3, matrix products, mul_nn(): return jnp.dot(a, b, preferred_element_type=F32)  7.47 us

profile of v9, /device:TPU:0, one launch (start us, length us, event | category | flops | bytes accessed | tf_op | source)
XLA Modules:
  0.0 201.4 jit_solution(4773358950936926263)
XLA Ops:
  0.7 0.0 copy-start
  0.7 0.0 copy-start.3
  0.7 75.5 %forward.1 = (bf16[384,768]{1,0:T(8,128)(2,1)}, bf16[8,5,192,128]{3,2,1,0:T(8,128)(2,1)}, f32[5,64,1024]{2,1,0:T(8,128)}, f32[5,8,1024]{2,1,0:T(8,128)}, bf16[6,...) custom-call(s32[3,1,8]{2,1,0:T(1,128)} %refs_0_.3, ...), custom_call_target="tpu_custom_call" | custom-call | tf_op jit(solution)/shard_map/forward/pallas_call | solution.py:877
  76.1 1.0 slice_reduce_fusion.1
  77.2 0.0 copy-done
  77.2 0.3 convert_reduce_fusion.1
  77.5 0.0 copy-done.3
  77.5 0.0 copy-start.8
  77.5 2.3 %fusion.18 = (f32[384]{0:T(512)S(1)}, f32[384,768]{1,0:T(8,128)S(1)}) fusion(f32[768]{0:T(1024)S(1)} %get-tuple-element.85, bf16[384,768]{1,0:T(8,128)(2,1)} %get-tuple-element.36.refs_14_, bf16[768,768]{1,0:T(8,128)(2,1)} %bitcast.72, bf16[384,768]{1,0:T(8,128)(2,1)S(1)} %bitcast.64), kind=kOutput, calls=%fused_computation.65 | convolution fusion | flops 454164096 | bytes 3543552 | tf_op jit(solution)/shard_map/dot_general | solution.py:315
  79.8 0.3 multiply_reduce_fusion.3
  80.1 0.0 copy-start.10
  80.1 0.0 slice-start
  80.1 0.3 fusion.15.refs_12_
  80.4 0.0 copy-done.8
  80.4 0.5 copy-done.10
  80.9 0.0 copy-start.2
  80.9 0.0 slice-start.1
  80.9 3.0 %multiply_convert_fusion = (bf16[384,3072]{1,0:T(8,128)(2,1)S(1)}, f32[384,3072]{1,0:T(8,128)S(1)}) fusion(f32[3072]{0:T(1024)S(1)} %bitcast.76, bf16[384,768]{1,0:T(8,128)(2,1)S(1)} %fusion.15.refs_12_, bf16[768,3072]{1,0:T(8,128)(2,1)S(1)} %bitcast.66), kind=kOutput, calls=%fused_computation.8 | convolution fusion | flops 1819017216 | bytes 12398592 | tf_op jit(solution)/shard_map/dot_general | solution.py:315
  83.8 0.0 copy-done.2
  83.9 0.0 copy-start.5
  83.9 0.0 slice-done
  83.9 0.0 slice-done.1
  83.9 2.2 %fusion.19 = (f32[384]{0:T(512)S(1)}, f32[384,768]{1,0:T(8,128)S(1)}) fusion(f32[768]{0:T(1024)S(1)} %get-tuple-element.82, bf16[384,3072]{1,0:T(8,128)(2,1)S(1)} %get-tuple-element.107.refs_10_, bf16[3072,768]{1,0:T(8,128)(2,1)S(1)} %bitcast.70, f32[768]{0:T(1024)S(1)} %get-tuple-element.83, f32[768]{0:T(1024)S(1)} %get-tuple-element.84, ...), kind=kOutput, calls=%fused_computation.66 | convolution fusion | flops 1814003328 | bytes 9451008 | tf_op jit(solution)/shard_map/dot_general | solution.py:315
  86.1 0.0 copy-done.5
  86.1 0.3 multiply_reduce_fusion.2
  86.4 0.6 fusion.14
  87.0 1.4 convert_reduce_fusion.2
  88.3 0.0 copy-start.1
  88.3 3.7 %convert_reduce_fusion = (f32[3072]{0:T(1024)S(1)}, bf16[384,3072]{1,0:T(8,128)(2,1)S(1)}) fusion(f32[384,3072]{1,0:T(8,128)S(1)} %get-tuple-element.108, bf16[384,768]{1,0:T(8,128)(2,1)S(1)} %get-tuple-element.87.refs_9_, bf16[3072,768]{1,0:T(8,128)(2,1)S(1)} %bitcast.71), kind=kOutput, calls=%fused_computation.7 | convolution fusion | flops 1826092032 | bytes 12398592 | tf_op jit(solution)/shard_map/dot_general | solution.py:323
  92.0 0.0 copy-done.1
  92.0 0.0 copy-start.6
  92.0 2.5 %multiply_reduce_fusion = (f32[768]{0:T(1024)S(1)}, f32[384]{0:T(512)S(1)}, f32[384]{0:T(512)S(1)}, f32[768]{0:T(1024)S(1)}, f32[384,768]{1,0:T(8,128)S(1)}) fusion(f32[384,768]{1,0:T(8,128)S(1)} %get-tuple-element.106, f32[384]{0:T(512)S(1)} %add_rsqrt_fusion.1, f32[384]{0:T(512)S(1)} %broadcast_multiply_fusion.4, f32[768]{0:T(1024)S(1)} %get-tuple-element.84, ...), kind=kOutput, calls=%fused_computation.29 | convolution fusion | flops 1814886144 | bytes 10632192 | tf_op jit(solution)/shard_map/dot_general | solution.py:323
  94.5 0.0 copy-done.6
  94.6 0.0 copy-start.9
  94.6 1.4 convert_reduce_fusion.3
  96.0 0.0 copy-start.4
  96.0 0.0 copy-done.9
  96.0 1.5 convolution_convert_fusion.refs_1_
  97.5 0.0 copy-done.4
  97.6 0.1 stack.27
  97.6 0.6 pad.4.refs_7_
  98.3 99.4 %backward.1 = (f32[384,768]{1,0:T(8,128)}, f32[96,768]{1,0:T(8,128)}, f32[192,384]{1,0:T(8,128)}, f32[192,96]{1,0:T(8,128)}, f32[192,288]{1,0:T(8,128)}, /*index=5*/f32[16,128]{1,0:T(8,128)}) custom-call(s32[3,1,8]{2,1,0:T(1,128)} %refs_0_.3, bf16[384,768]{1,0:T(8,128)(2,1)} %convolution_convert_fusion.refs_1_, ...), custom_call_target="tpu_custom_call" | custom-call | tf_op jit(solution)/shard_map/backward/pallas_call | solution.py:1669
  197.7 0.0 copy-start.7
  197.7 2.7 %settle.1 = (f32[96,768]{1,0:T(8,128)}, f32[192,384]{1,0:T(8,128)}, f32[192,96]{1,0:T(8,128)}, f32[192,288]{1,0:T(8,128)}, f32[384,768]{1,0:T(8,128)}) custom-call(f32[96,768]{1,0:T(8,128)} %get-tuple-element.46.refs_0_, f32[192,384]{1,0:T(8,128)} %get-tuple-element.47.refs_1_, f32[192,96]{1,0:T(8,128)} %get-tuple-element.48.refs_2_, ...), custom_call_target="tpu_custom_call" | custom-call | tf_op jit(solution)/shard_map/settle/pallas_call | solution.py:1734
  200.4 0.0 copy-done.7
  200.4 0.5 slice_bitcast_fusion.3
  200.9 0.5 slice_bitcast_fusion
  (19 shorter events, 0.1 us)
Async XLA Ops:
  0.7 76.5 %copy-start = (bf16[3,1,128,768]{3,2,1,0:T(8,128)(2,1)S(1)}, bf16[3,1,128,768]{3,2,1,0:T(8,128)(2,1)}, u32[]{:S(2)}) copy-start(bf16[3,1,128,768]{3,2,1,0:T(8,128)(2,1)} %param.31) | copy-start | bytes 1769476
  0.7 76.8 %copy-start.3 = (bf16[3,1,128,768]{3,2,1,0:T(8,128)(2,1)S(1)}, bf16[3,1,128,768]{3,2,1,0:T(8,128)(2,1)}, u32[]{:S(2)}) copy-start(bf16[3,1,128,768]{3,2,1,0:T(8,128)(2,1)} %param.16) | copy-start | bytes 1769476
  77.5 2.9 %copy-start.8 = (bf16[4,192,3072]{2,1,0:T(8,128)(2,1)S(1)}, bf16[4,192,3072]{2,1,0:T(8,128)(2,1)}, u32[]{:S(2)}) copy-start(bf16[4,192,3072]{2,1,0:T(8,128)(2,1)} %get-tuple-element.39) | copy-start | bytes 14155780
  80.1 0.8 copy-start.10
  80.1 3.8 %slice-start = ((s8[4718592]{0:T(1024)(128)(4,1)}), s8[4194304]{0:T(1024)(128)(4,1)S(1)}, s32[]{:S(2)}) async-start(s8[4718592]{0:T(1024)(128)(4,1)} %bitcast.68), calls=%async_computation | async-start | bytes 8388608
  80.9 3.0 %copy-start.2 = (bf16[384,768]{1,0:T(8,128)(2,1)}, bf16[384,768]{1,0:T(8,128)(2,1)S(1)}, u32[]{:S(2)}) copy-start(bf16[384,768]{1,0:T(8,128)(2,1)S(1)} %fusion.15.refs_12_) | copy-start | bytes 1769476
  80.9 3.0 %slice-start.1 = ((s8[4718592]{0:T(1024)(128)(4,1)}), s8[524288]{0:T(1024)(128)(4,1)S(1)}, s32[]{:S(2)}) async-start(s8[4718592]{0:T(1024)(128)(4,1)} %bitcast.68), calls=%async_computation.1 | async-start | bytes 1048576
  83.9 2.2 %copy-start.5 = (bf16[384,3072]{1,0:T(8,128)(2,1)}, bf16[384,3072]{1,0:T(8,128)(2,1)S(1)}, u32[]{:S(2)}) copy-start(bf16[384,3072]{1,0:T(8,128)(2,1)S(1)} %get-tuple-element.107.refs_10_) | copy-start | bytes 7077892
  88.3 3.7 %copy-start.1 = (bf16[384,768]{1,0:T(8,128)(2,1)}, bf16[384,768]{1,0:T(8,128)(2,1)S(1)}, u32[]{:S(2)}) copy-start(bf16[384,768]{1,0:T(8,128)(2,1)S(1)} %get-tuple-element.87.refs_9_) | copy-start | bytes 1769476
  92.0 2.5 %copy-start.6 = (bf16[384,3072]{1,0:T(8,128)(2,1)}, bf16[384,3072]{1,0:T(8,128)(2,1)S(1)}, u32[]{:S(2)}) copy-start(bf16[384,3072]{1,0:T(8,128)(2,1)S(1)} %get-tuple-element.113.refs_11_) | copy-start | bytes 7077892
  94.6 1.4 copy-start.9
  96.0 1.5 copy-start.4
  197.7 2.7 %copy-start.7 = (f32[16,128]{1,0:T(8,128)S(1)}, f32[16,128]{1,0:T(8,128)}, u32[]{:S(2)}) copy-start(f32[16,128]{1,0:T(8,128)} %get-tuple-element.56) | copy-start | bytes 24580

commit v10 on v8

--- a/solution.py
+++ b/solution.py
@@ -579,6 +579,8 @@
         first.wait()
         second.start()
 
+    for batch in range(MB):
+        key_documents(starts_ref, batch, key_docs.at[batch])
     narrow.hand_on()
     narrow.arrive()
     tok_load.wait()
@@ -696,7 +698,6 @@
             key_rows[rows, :] = got_ref[i, slot, HD : 2 * HD, :].T
             value_t[:, rows] = got_ref[i, slot, 2 * HD : 3 * HD, :]
         batch = batch_of(count, me, slot)
-        key_documents(starts_ref, batch, key_docs)
 
         def block(number, inner):
             begin = pl.multiple_of(number * width, width)
@@ -710,7 +711,7 @@
                 scores = jnp.dot(
                     key_rows[pl.ds(first, depth), :], queries, preferred_element_type=F32
                 )
-                same = same_document(key_docs, first, depth, query_docs)
+                same = same_document(key_docs.at[batch], first, depth, query_docs)
                 scores = jnp.where(same, scores, MASKED)
                 new_peak = jnp.maximum(peak, jnp.max(scores, axis=0, keepdims=True))
                 scaling = jnp.exp(peak - new_peak)
@@ -905,7 +906,7 @@
             pltpu.VMEM((count, units, HD, lanes), BF16),
             pltpu.VMEM((length, HD), BF16),
             pltpu.VMEM((HD, length), BF16),
-            pltpu.VMEM((length, lanes), jnp.int32),
+            pltpu.VMEM((MB, length, lanes), jnp.int32),
             pltpu.VMEM(mixer.shape, BF16),
             pltpu.VMEM(inner.shape, BF16),
             pltpu.VMEM(outer.shape, BF16),

time: 202 us -> 202 us (level)
  no operation moved by 1% of the time
where the time goes in v10:
time: 202 us; the launch traced here: 201 us
  Pallas kernels  177 us (88%)
  matrix products  15.1 us (7%)
  other arithmetic  4.46 us (2%)
  local copies, waits for them, and re-layouts  3.35 us (2%)
    pallas_call x1, Pallas kernels, backward(): pl.pallas_call(functools.partial(backward_kernel, width, plan), out_shape...  98.9 us
    pallas_call x1, Pallas kernels, forward(): pl.pallas_call(functools.partial(forward_kernel, width), out_shape=(jax.S...  76 us
    dot_general x3, matrix products, mul_nt(): lax.dot_general(a, b, (((1,), (1,)), ((), ())), preferred_element_type=F32)  7.64 us
    dot_general x3, matrix products, mul_nn(): return jnp.dot(a, b, preferred_element_type=F32)  7.46 us

profile of v10, /device:TPU:0, one launch (start us, length us, event | category | flops | bytes accessed | tf_op | source)
XLA Modules:
  0.0 201.4 jit_solution(6271903204257967537)
XLA Ops:
  0.7 0.0 copy-start
  0.7 0.0 copy-start.3
  0.7 76.0 %forward.1 = (bf16[384,768]{1,0:T(8,128)(2,1)}, bf16[8,5,192,128]{3,2,1,0:T(8,128)(2,1)}, f32[5,64,1024]{2,1,0:T(8,128)}, f32[5,8,1024]{2,1,0:T(8,128)}, bf16[6,...) custom-call(s32[3,1,8]{2,1,0:T(1,128)} %refs_0_.3, ...), custom_call_target="tpu_custom_call" | custom-call | tf_op jit(solution)/shard_map/forward/pallas_call | solution.py:878
  76.6 1.0 slice_reduce_fusion.1
  77.7 0.0 copy-done
  77.7 0.3 convert_reduce_fusion.1
  78.0 0.0 copy-done.3
  78.0 0.0 copy-start.8
  78.0 2.3 %fusion.18 = (f32[384]{0:T(512)S(1)}, f32[384,768]{1,0:T(8,128)S(1)}) fusion(f32[768]{0:T(1024)S(1)} %get-tuple-element.85, bf16[384,768]{1,0:T(8,128)(2,1)} %get-tuple-element.36.refs_14_, bf16[768,768]{1,0:T(8,128)(2,1)} %bitcast.72, bf16[384,768]{1,0:T(8,128)(2,1)S(1)} %bitcast.64), kind=kOutput, calls=%fused_computation.65 | convolution fusion | flops 454164096 | bytes 3543552 | tf_op jit(solution)/shard_map/dot_general | solution.py:315
  80.3 0.3 multiply_reduce_fusion.3
  80.6 0.0 copy-start.10
  80.6 0.0 slice-start
  80.6 0.3 fusion.15.refs_12_
  80.9 0.0 copy-done.8
  80.9 0.5 copy-done.10
  81.4 0.0 copy-start.2
  81.4 0.0 slice-start.1
  81.4 3.0 %multiply_convert_fusion = (bf16[384,3072]{1,0:T(8,128)(2,1)S(1)}, f32[384,3072]{1,0:T(8,128)S(1)}) fusion(f32[3072]{0:T(1024)S(1)} %bitcast.76, bf16[384,768]{1,0:T(8,128)(2,1)S(1)} %fusion.15.refs_12_, bf16[768,3072]{1,0:T(8,128)(2,1)S(1)} %bitcast.66), kind=kOutput, calls=%fused_computation.8 | convolution fusion | flops 1819017216 | bytes 12398592 | tf_op jit(solution)/shard_map/dot_general | solution.py:315
  84.3 0.0 copy-done.2
  84.3 0.0 copy-start.5
  84.4 0.0 slice-done
  84.4 0.0 slice-done.1
  84.4 2.2 %fusion.19 = (f32[384]{0:T(512)S(1)}, f32[384,768]{1,0:T(8,128)S(1)}) fusion(f32[768]{0:T(1024)S(1)} %get-tuple-element.82, bf16[384,3072]{1,0:T(8,128)(2,1)S(1)} %get-tuple-element.107.refs_10_, bf16[3072,768]{1,0:T(8,128)(2,1)S(1)} %bitcast.70, f32[768]{0:T(1024)S(1)} %get-tuple-element.83, f32[768]{0:T(1024)S(1)} %get-tuple-element.84, ...), kind=kOutput, calls=%fused_computation.66 | convolution fusion | flops 1814003328 | bytes 9451008 | tf_op jit(solution)/shard_map/dot_general | solution.py:315
  86.6 0.0 copy-done.5
  86.6 0.3 multiply_reduce_fusion.2
  86.8 0.6 fusion.14
  87.5 1.4 convert_reduce_fusion.2
  88.8 0.0 copy-start.1
  88.8 3.7 %convert_reduce_fusion = (f32[3072]{0:T(1024)S(1)}, bf16[384,3072]{1,0:T(8,128)(2,1)S(1)}) fusion(f32[384,3072]{1,0:T(8,128)S(1)} %get-tuple-element.108, bf16[384,768]{1,0:T(8,128)(2,1)S(1)} %get-tuple-element.87.refs_9_, bf16[3072,768]{1,0:T(8,128)(2,1)S(1)} %bitcast.71), kind=kOutput, calls=%fused_computation.7 | convolution fusion | flops 1826092032 | bytes 12398592 | tf_op jit(solution)/shard_map/dot_general | solution.py:323
  92.5 0.0 copy-done.1
  92.5 0.0 copy-start.6
  92.5 2.5 %multiply_reduce_fusion = (f32[768]{0:T(1024)S(1)}, f32[384]{0:T(512)S(1)}, f32[384]{0:T(512)S(1)}, f32[768]{0:T(1024)S(1)}, f32[384,768]{1,0:T(8,128)S(1)}) fusion(f32[384,768]{1,0:T(8,128)S(1)} %get-tuple-element.106, f32[384]{0:T(512)S(1)} %add_rsqrt_fusion.1, f32[384]{0:T(512)S(1)} %broadcast_multiply_fusion.4, f32[768]{0:T(1024)S(1)} %get-tuple-element.84, ...), kind=kOutput, calls=%fused_computation.29 | convolution fusion | flops 1814886144 | bytes 10632192 | tf_op jit(solution)/shard_map/dot_general | solution.py:323
  95.0 0.0 copy-done.6
  95.1 0.0 copy-start.9
  95.1 1.4 convert_reduce_fusion.3
  96.5 0.0 copy-start.4
  96.5 0.0 copy-done.9
  96.5 1.5 convolution_convert_fusion.refs_1_
  98.0 0.0 copy-done.4
  98.0 0.1 stack.27
  98.1 0.6 pad.4.refs_7_
  98.7 98.9 %backward.1 = (f32[384,768]{1,0:T(8,128)}, f32[96,768]{1,0:T(8,128)}, f32[192,384]{1,0:T(8,128)}, f32[192,96]{1,0:T(8,128)}, f32[192,288]{1,0:T(8,128)}, /*index=5*/f32[16,128]{1,0:T(8,128)}) custom-call(s32[3,1,8]{2,1,0:T(1,128)} %refs_0_.3, bf16[384,768]{1,0:T(8,128)(2,1)} %convolution_convert_fusion.refs_1_, ...), custom_call_target="tpu_custom_call" | custom-call | tf_op jit(solution)/shard_map/backward/pallas_call | solution.py:1670
  197.6 0.0 copy-start.7
  197.6 2.7 %settle.1 = (f32[96,768]{1,0:T(8,128)}, f32[192,384]{1,0:T(8,128)}, f32[192,96]{1,0:T(8,128)}, f32[192,288]{1,0:T(8,128)}, f32[384,768]{1,0:T(8,128)}) custom-call(f32[96,768]{1,0:T(8,128)} %get-tuple-element.46.refs_0_, f32[192,384]{1,0:T(8,128)} %get-tuple-element.47.refs_1_, f32[192,96]{1,0:T(8,128)} %get-tuple-element.48.refs_2_, ...), custom_call_target="tpu_custom_call" | custom-call | tf_op jit(solution)/shard_map/settle/pallas_call | solution.py:1735
  200.3 0.0 copy-done.7
  200.3 0.5 slice_bitcast_fusion.3
  200.8 0.5 slice_bitcast_fusion
  (19 shorter events, 0.1 us)
Async XLA Ops:
  0.7 77.0 %copy-start = (bf16[3,1,128,768]{3,2,1,0:T(8,128)(2,1)S(1)}, bf16[3,1,128,768]{3,2,1,0:T(8,128)(2,1)}, u32[]{:S(2)}) copy-start(bf16[3,1,128,768]{3,2,1,0:T(8,128)(2,1)} %param.31) | copy-start | bytes 1769476
  0.7 77.3 %copy-start.3 = (bf16[3,1,128,768]{3,2,1,0:T(8,128)(2,1)S(1)}, bf16[3,1,128,768]{3,2,1,0:T(8,128)(2,1)}, u32[]{:S(2)}) copy-start(bf16[3,1,128,768]{3,2,1,0:T(8,128)(2,1)} %param.16) | copy-start | bytes 1769476
  78.0 2.9 %copy-start.8 = (bf16[4,192,3072]{2,1,0:T(8,128)(2,1)S(1)}, bf16[4,192,3072]{2,1,0:T(8,128)(2,1)}, u32[]{:S(2)}) copy-start(bf16[4,192,3072]{2,1,0:T(8,128)(2,1)} %get-tuple-element.39) | copy-start | bytes 14155780
  80.6 0.8 copy-start.10
  80.6 3.8 %slice-start = ((s8[4718592]{0:T(1024)(128)(4,1)}), s8[4194304]{0:T(1024)(128)(4,1)S(1)}, s32[]{:S(2)}) async-start(s8[4718592]{0:T(1024)(128)(4,1)} %bitcast.68), calls=%async_computation | async-start | bytes 8388608
  81.4 3.0 %copy-start.2 = (bf16[384,768]{1,0:T(8,128)(2,1)}, bf16[384,768]{1,0:T(8,128)(2,1)S(1)}, u32[]{:S(2)}) copy-start(bf16[384,768]{1,0:T(8,128)(2,1)S(1)} %fusion.15.refs_12_) | copy-start | bytes 1769476
  81.4 3.0 %slice-start.1 = ((s8[4718592]{0:T(1024)(128)(4,1)}), s8[524288]{0:T(1024)(128)(4,1)S(1)}, s32[]{:S(2)}) async-start(s8[4718592]{0:T(1024)(128)(4,1)} %bitcast.68), calls=%async_computation.1 | async-start | bytes 1048576
  84.3 2.2 %copy-start.5 = (bf16[384,3072]{1,0:T(8,128)(2,1)}, bf16[384,3072]{1,0:T(8,128)(2,1)S(1)}, u32[]{:S(2)}) copy-start(bf16[384,3072]{1,0:T(8,128)(2,1)S(1)} %get-tuple-element.107.refs_10_) | copy-start | bytes 7077892
  88.8 3.7 %copy-start.1 = (bf16[384,768]{1,0:T(8,128)(2,1)}, bf16[384,768]{1,0:T(8,128)(2,1)S(1)}, u32[]{:S(2)}) copy-start(bf16[384,768]{1,0:T(8,128)(2,1)S(1)} %get-tuple-element.87.refs_9_) | copy-start | bytes 1769476
  92.5 2.5 %copy-start.6 = (bf16[384,3072]{1,0:T(8,128)(2,1)}, bf16[384,3072]{1,0:T(8,128)(2,1)S(1)}, u32[]{:S(2)}) copy-start(bf16[384,3072]{1,0:T(8,128)(2,1)S(1)} %get-tuple-element.113.refs_11_) | copy-start | bytes 7077892
  95.1 1.4 copy-start.9
  96.5 1.5 copy-start.4
  197.6 2.7 %copy-start.7 = (f32[16,128]{1,0:T(8,128)S(1)}, f32[16,128]{1,0:T(8,128)}, u32[]{:S(2)}) copy-start(f32[16,128]{1,0:T(8,128)} %get-tuple-element.56) | copy-start | bytes 24580
